TPU v7x, 32 devices: a whole 2x2x4 slice. The times are simulated.
32 devices in a mesh: group: 2 (over x), engine: 4 (over y, core), chan: 4 (over z).
Axes of the slice: x: 2, y: 2, z: 4, core: 2. Of those that a mesh axis runs over, the one named last changes fastest.
Arguments:
- mr_qkv: bfloat16 [2, 3, 128, 8192], P(None, None, ('group', 'engine'), 'chan'), parts along dimension 2, may hold values from -6 to 6
- li_qkv: bfloat16 [2, 3, 128, 8192], P(None, None, ('group', 'engine'), 'chan'), parts along dimension 2, may hold values from -6 to 6
- conv_tails: bfloat16 [128, 127, 8192], P(('group', 'engine'), None, 'chan'), parts along dimension 0, may hold values from -6 to 6
- modal_states: float32 [128, 16, 8192], P(('group', 'engine'), None, 'chan'), parts along dimension 0, may hold values from -12 to 12
- source: int32 [128], P('group'), parts along dimension 0, may hold values from 0 to 63, as said below
- remaining: int32 [128], P(('group', 'engine')), parts along dimension 0, may hold values from 0 to 3
- mr_filter: bfloat16 [128, 8192], P(None, 'chan'), may hold values from -0.5 to 0.5
- li_decay: float32 [16, 8192], P(None, 'chan'), may hold values from 0.5 to 0.999
- li_residue: float32 [16, 8192], P(None, 'chan'), may hold values from -1.5 to 1.5
- mr_panels: bfloat16 [8, 8192, 512], P('engine', 'chan'), may hold values from -0.046875 to 0.046875
- li_panels: bfloat16 [8, 8192, 512], P('engine', 'chan'), may hold values from -0.046875 to 0.046875
- panel_slot: int32 [8], replicated, may hold values from 0 to 7, each once
Outputs:
- mixed: bfloat16 [2, 128, 4096], P(None, ('group', 'engine'), 'chan'), parts along dimension 1
- new_tails: bfloat16 [128, 127, 8192], P(('group', 'engine'), None, 'chan'), parts along dimension 0
- new_states: float32 [128, 16, 8192], P(('group', 'engine'), None, 'chan'), parts along dimension 0
There are 2 independent parts, one for each index of `group`. A program takes and returns all parts, laid end to end along the dimension named above; an argument that names none is the same for every part. Nothing has to cross between parts.
Inputs may be any that keep to these rules, and one draw needn't show every extreme that they name: `source`: A permutation of the old slots. Each engine's 16 new slots hold exactly 2 rollouts from each of 3 other engines and 10 rollouts from its own old slots; engine e takes from the engines e - d mod 4 for 3 distances d that are the same for every engine, so every engine also gives exactly 2 rollouts to each of 3 others.
All inputs are finite; a program needn't handle non-finite values.
Results may differ from a plain program's by a relative error of at most 0.008.
Values may be sent and summed in bfloat16 or wider, within the bound.
No kernel may reach another device: no remote copies, remote signals or barrier semaphores. Data moves between devices by JAX's collectives and lax.ppermute only.
A program may use at most 192 MiB of HBM per device.

v0:
```python
import jax
import jax.numpy as jnp
from jax import lax
from jax.sharding import PartitionSpec as P

CAP = 2


def body(
    mr_qkv,
    li_qkv,
    conv_tails,
    modal_states,
    source,
    remaining,
    mr_filter,
    li_decay,
    li_residue,
    mr_panels,
    li_panels,
    panel_slot,
):
    engines = lax.axis_size("engine")
    me = lax.axis_index("engine")
    rows = conv_tails.shape[0]
    tail_len = conv_tails.shape[1]
    width = conv_tails.shape[2]
    panel_cols = mr_panels.shape[2]
    panel_count = panel_slot.shape[0]
    owners = source.reshape(engines, rows)
    engine_ids = jnp.arange(engines, dtype=jnp.int32)
    from_me = (owners // rows == me) & (engine_ids[:, None] != me)
    order_rank = jnp.cumsum(from_me.astype(jnp.int32), axis=1) - 1
    place_ids = jnp.arange(CAP, dtype=jnp.int32)
    picks = from_me[:, :, None] & (order_rank[:, :, None] == place_ids[None, None, :])
    send_index = jnp.sum(picks.astype(jnp.int32) * (owners % rows)[:, :, None], axis=1)
    send_tails = conv_tails[send_index.reshape(-1)].reshape(engines, CAP, tail_len, width)
    send_states = modal_states[send_index.reshape(-1)].reshape(
        engines, CAP, modal_states.shape[1], width
    )
    got_tails = lax.all_to_all(send_tails, "engine", split_axis=0, concat_axis=0, tiled=True)
    got_states = lax.all_to_all(send_states, "engine", split_axis=0, concat_axis=0, tiled=True)
    mine = lax.dynamic_slice_in_dim(source, me * rows, rows)
    src_engine = mine // rows
    src_local = mine % rows
    row_ids = jnp.arange(rows, dtype=jnp.int32)
    earlier = (src_engine[:, None] == src_engine[None, :]) & (row_ids[None, :] < row_ids[:, None])
    arrive_rank = jnp.sum(earlier.astype(jnp.int32), axis=1)
    arrive_index = jnp.clip(src_engine * CAP + arrive_rank, 0, engines * CAP - 1)
    stays = src_engine == me
    tails = jnp.where(
        stays[:, None, None],
        conv_tails[src_local],
        got_tails.reshape(engines * CAP, tail_len, width)[arrive_index],
    )
    states = jnp.where(
        stays[:, None, None],
        modal_states[src_local],
        got_states.reshape(engines * CAP, got_states.shape[2], width)[arrive_index],
    )
    filt = mr_filter.astype(jnp.float32)
    part_first = jnp.einsum("rtc,tc->rc", tails, mr_filter[1:], preferred_element_type=jnp.float32)
    part_second = jnp.einsum(
        "rtc,tc->rc", tails[:, : tail_len - 1], mr_filter[2:], preferred_element_type=jnp.float32
    )
    zmr_first = (mr_qkv[0, 1].astype(jnp.float32) * mr_qkv[0, 2].astype(jnp.float32)).astype(
        jnp.bfloat16
    )
    zmr_second = (mr_qkv[1, 1].astype(jnp.float32) * mr_qkv[1, 2].astype(jnp.float32)).astype(
        jnp.bfloat16
    )
    new_tails = jnp.concatenate(
        [zmr_second[:, None, :], zmr_first[:, None, :], tails[:, : tail_len - 2]], axis=1
    )
    zmr0 = zmr_first.astype(jnp.float32)
    zmr1 = zmr_second.astype(jnp.float32)
    conv0 = filt[0] * zmr0 + part_first
    conv1 = filt[0] * zmr1 + filt[1] * zmr0 + part_second
    ymr0 = (mr_qkv[0, 0].astype(jnp.float32) * conv0).astype(jnp.bfloat16)
    ymr1 = (mr_qkv[1, 0].astype(jnp.float32) * conv1).astype(jnp.bfloat16)
    zli0 = (
        (li_qkv[0, 1].astype(jnp.float32) * li_qkv[0, 2].astype(jnp.float32))
        .astype(jnp.bfloat16)
        .astype(jnp.float32)
    )
    zli1 = (
        (li_qkv[1, 1].astype(jnp.float32) * li_qkv[1, 2].astype(jnp.float32))
        .astype(jnp.bfloat16)
        .astype(jnp.float32)
    )
    states1 = li_decay[None] * states + zli0[:, None, :]
    yli0 = (li_qkv[0, 0].astype(jnp.float32) * jnp.sum(li_residue[None] * states1, axis=1)).astype(
        jnp.bfloat16
    )
    states2 = li_decay[None] * states1 + zli1[:, None, :]
    yli1 = (li_qkv[1, 0].astype(jnp.float32) * jnp.sum(li_residue[None] * states2, axis=1)).astype(
        jnp.bfloat16
    )
    mr_rows = jnp.stack([ymr0, ymr1])
    li_rows = jnp.stack([yli0, yli1])
    mr_piece = lax.all_gather(mr_panels, "engine", axis=0, tiled=True)
    li_piece = lax.all_gather(li_panels, "engine", axis=0, tiled=True)
    upper = jnp.einsum("srd,gdc->srgc", mr_rows, mr_piece, preferred_element_type=jnp.float32)
    lower = jnp.einsum("srd,gdc->srgc", li_rows, li_piece, preferred_element_type=jnp.float32)
    sectioned = upper + lower
    partial_value = jnp.take(sectioned, panel_slot, axis=2).reshape(
        2, rows, panel_count * panel_cols
    )
    summed = lax.psum_scatter(partial_value, "chan", scatter_dimension=2, tiled=True)
    steps_ids = jnp.arange(2, dtype=jnp.int32)
    active = (remaining[None, :] > steps_ids[:, None]).astype(jnp.float32)
    mixed = (summed * active[:, :, None]).astype(jnp.bfloat16)
    return (mixed, new_tails, states2)


def solution(mesh):
    return jax.shard_map(
        body,
        mesh=mesh,
        in_specs=(
            P(None, None, ("group", "engine"), "chan"),
            P(None, None, ("group", "engine"), "chan"),
            P(("group", "engine"), None, "chan"),
            P(("group", "engine"), None, "chan"),
            P("group"),
            P(("group", "engine")),
            P(None, "chan"),
            P(None, "chan"),
            P(None, "chan"),
            P("engine", "chan", None),
            P("engine", "chan", None),
            P(),
        ),
        out_specs=(
            P(None, ("group", "engine"), "chan"),
            P(("group", "engine"), None, "chan"),
            P(("group", "engine"), None, "chan"),
        ),
        check_vma=False,
    )
```

profile of v0, /device:TPU:0, one launch (start us, length us, event | category | flops | bytes accessed | tf_op | source)
XLA Modules:
  0.0 315.2 jit_solution(9834262589492569166)
XLA Ops:
  7.2 0.0 copy-start
  7.2 0.0 copy-start.10
  7.2 0.0 all-gather.5.cloned.1.call-start
  7.2 0.7 all-gather.5.cloned.1.call-update
  7.9 0.0 all-gather.3.cloned.1.call-start
  8.0 0.7 all-gather.3.cloned.1.call-update
  8.7 0.0 copy-done.10
  8.7 0.1 reshape.363
  8.8 0.1 fusion.36
  8.9 0.2 reduce_window_sum.11
  9.1 0.1 select_reduce_fusion
  9.2 0.1 copy.22
  9.3 0.1 reshape.364
  9.4 0.0 copy-done
  9.4 1.6 gather_fusion.4
  11.0 4.2 %all-to-all-start.1 = ((f32[4,2,16,2048]{3,2,1,0:T(8,128)}), f32[4,2,16,2048]{3,2,1,0:T(8,128)S(1)}, u32[]{:S(2)}, u32[]{:S(2)}) async-start(f32[4,2,16,2048]{3,2,1,0:T(8,128)} %bitcast.94), calls=%async_computation.1 | async-start | bytes 2097152 | tf_op jit(solution)/shard_map/all_to_all | solution.py:42
  15.2 0.7 broadcast_compare_fusion.1
  15.9 0.2 convert_reduce_fusion
  16.1 13.2 %gather_fusion.1 = bf16[8,127,2048]{2,0,1:T(8,128)(2,1)} fusion(bf16[16,127,2048]{2,0,1:T(8,128)(2,1)} %param.14, s32[1024]{0:T(1024)S(1)} %pad_clamp_fusion.2), kind=kCustom, calls=%fused_computation.1 | custom fusion | bytes 8323104 | tf_op jit(solution)/shard_map/gather | solution.py:37
  29.3 9.3 %reshape.365 = bf16[4,2,127,2048]{3,1,0,2:T(2,128)(2,1)} reshape(bf16[8,127,2048]{2,0,1:T(8,128)(2,1)} %gather_fusion.1) | data formatting | bytes 8323072 | tf_op jit(solution)/shard_map/reshape | solution.py:37
  38.6 7.0 %copy.23 = bf16[4,2,127,2048]{3,1,2,0:T(2,128)(2,1)} copy(bf16[4,2,127,2048]{3,1,0,2:T(2,128)(2,1)} %reshape.365) | data formatting | bytes 8323072 | tf_op jit(solution)/shard_map/reshape | solution.py:37
  45.6 0.6 pad_clamp_fusion.1
  46.2 0.0 copy-done.11
  46.2 0.1 broadcast_bitcast_fusion
  46.3 0.0 all-to-all-done.1
  46.3 5.1 %all-to-all-start = ((bf16[4,2,127,2048]{3,1,2,0:T(2,128)(2,1)}), bf16[4,2,127,2048]{3,1,2,0:T(2,128)(2,1)}, u32[]{:S(2)}, u32[]{:S(2)}) async-start(bf16[4,2,127,2048]{3,1,2,0:T(2,128)(2,1)} %copy.23), calls=%async_computation | async-start | bytes 8323072 | tf_op jit(solution)/shard_map/all_to_all | solution.py:41
  51.3 0.0 reduce-scatter.2.cloned.1.call-start
  51.4 18.6 %gather_fusion = bf16[16,127,2048]{2,0,1:T(8,128)(2,1)} fusion(bf16[16,127,2048]{2,0,1:T(8,128)(2,1)} %param.14, s32[1024]{0:T(1024)S(1)} %pad_clamp_fusion.3), kind=kCustom, calls=%fused_computation | custom fusion | bytes 16646208 | tf_op jit(solution)/shard_map/gather | solution.py:53
  70.0 2.0 gather_fusion.3
  72.0 0.6 copy.46
  72.6 0.6 pad_clamp_fusion
  73.2 0.8 fusion.38
  74.1 1.0 fusion.23
  75.0 2.2 bitcast_convert_fusion.1
  77.2 2.2 bitcast_convert_fusion
  79.4 2.2 gather_fusion.5
  81.6 0.0 copy-done.7
  81.6 0.0 copy-done.3
  81.6 4.0 %multiply_reduce_fusion.3 = (f32[16,2048]{1,0:T(8,128)S(1)}, f32[16,2048]{1,0:T(8,128)S(1)}, f32[16,16,2048]{2,1,0:T(8,128)}) fusion(f32[16,2048]{1,0:T(8,128)S(1)} %copy-done.7, f32[16,2048]{1,0:T(8,128)S(1)} %get-tuple-element.22, f32[16,16,2048]{2,1,0:T(8,128)S(1)} %copy-done.3, f32[16,16,2048]{2,1,0:T(8,128)} %gather_fusion.5, ...), kind=kLoop, calls=%fused_computation.18 | loop fusion | flops 4653056 | bytes 7077904 | tf_op jit(solution)/shard_map/reduce_sum | solution.py:92
  85.6 0.9 fusion.19
  86.5 58.1 %all-to-all-done = bf16[4,2,127,2048]{3,1,2,0:T(2,128)(2,1)} async-done(((bf16[4,2,127,2048]{3,1,2,0:T(2,128)(2,1)}), bf16[4,2,127,2048]{3,1,2,0:T(2,128)(2,1)}, u32[]{:S(2)}, u32[]{:S(2)}) %all-to-all-start) | async-done | bytes 4161568 | tf_op jit(solution)/shard_map/all_to_all | solution.py:41
  144.6 6.0 %copy.24 = bf16[4,2,127,2048]{3,2,1,0:T(8,128)(2,1)} copy(bf16[4,2,127,2048]{3,1,2,0:T(2,128)(2,1)} %all-to-all-done) | data formatting | bytes 8323072 | tf_op jit(solution)/shard_map/all_to_all | solution.py:41
  150.6 7.1 %gather_fusion.2 = bf16[16,127,2048]{2,1,0:T(8,128)(2,1)} fusion(bf16[8,127,2048]{2,1,0:T(8,128)(2,1)} %bitcast.92, s32[1024]{0:T(1024)} %pad_clamp_fusion.1), kind=kCustom, calls=%fused_computation.2 | custom fusion | bytes 16646208 | tf_op jit(solution)/shard_map/gather | solution.py:54
  157.8 0.0 copy-done.9
  157.8 11.0 %multiply_reduce_fusion = (f32[2048,16]{0,1:T(8,128)S(1)}, bf16[16,127,2048]{2,0,1:T(8,128)(2,1)S(1)}) fusion(f32[2048,127]{0,1:T(8,128)S(1)} %copy-done.5, bf16[16,127,2048]{2,0,1:T(8,128)(2,1)} %gather_fusion, bf16[16,127,2048]{2,1,0:T(8,128)(2,1)} %gather_fusion.2, pred[16]{0:T(512)(128)(4,1)S(1)} %copy-done.9), kind=kLoop, calls=%fused_computation.11 | loop fusion | flops 16613376 | bytes 26140688 | tf_op jit(solution)/shard_map/rtc,tc->rc/dot_general | solution.py:62
  168.8 0.0 copy-start.2
  168.8 0.0 copy-start.6
  168.8 3.3 %copy-done.2 = bf16[16,127,2048]{2,0,1:T(8,128)(2,1)} copy-done((bf16[16,127,2048]{2,0,1:T(8,128)(2,1)}, bf16[16,127,2048]{2,0,1:T(8,128)(2,1)S(1)}, u32[]{:S(2)}) %copy-start.2) | copy-done | bytes 8323096
  172.1 2.4 multiply_reduce_fusion.1
  174.5 0.1 fusion.25
  174.6 0.0 all-gather.5.cloned.1.call-done
  174.7 11.4 %fusion = f32[2,16,8,512]{3,1,2,0:T(8,128)S(1)} fusion(bf16[8,2048,512]{2,1,0:T(8,128)(2,1)} %all-gather.5.cloned.1.call-done, bf16[1,16,2048]{2,1,0:T(8,128)(2,1)S(1)} %get-tuple-element.20, bf16[1,16,2048]{2,1,0:T(8,128)(2,1)S(1)} %get-tuple-element.19), kind=kOutput, calls=%fused_computation.7 | convolution fusion | flops 537133056 | bytes 17432576 | tf_op jit(solution)/shard_map/srd,gdc->srgc/dot_general | solution.py:104
  186.1 88.8 %all-gather.3.cloned.1.call-done = bf16[8,2048,512]{2,1,0:T(8,128)(2,1)} async-done(((bf16[2,2048,512]{2,1,0:T(8,128)(2,1)}), bf16[8,2048,512]{2,1,0:T(8,128)(2,1)}) %all-gather.3.cloned.1.call-update) | async-done | bytes 16777232 | tf_op jit(solution)/shard_map/all_gather | solution.py:101
  274.9 8.7 %fusion.4 = f32[2,16,8,512]{3,1,2,0:T(8,128)S(1)} fusion(f32[2,16,8,512]{3,1,2,0:T(8,128)S(1)} %fusion, bf16[8,2048,512]{2,1,0:T(8,128)(2,1)} %all-gather.3.cloned.1.call-done, bf16[1,16,2048]{2,1,0:T(8,128)(2,1)S(1)} %get-tuple-element.16, bf16[1,16,2048]{2,1,0:T(8,128)(2,1)S(1)} %get-tuple-element.15), kind=kOutput, calls=%fused_computation.20 | convolution fusion | flops 537264128 | bytes 17956864 | tf_op jit(solution)/shard_map/srd,gdc->srgc/dot_general | solution.py:103
  283.6 0.7 gather_fusion.6
  284.3 0.0 copy-done.8
  284.3 0.9 broadcast_select_fusion
  285.2 0.0 reduce-scatter.2.cloned.1.call-update
  285.2 0.0 copy-done.12
  285.3 8.1 %slice.90 = bf16[16,125,2048]{2,0,1:T(8,128)(2,1)} slice(bf16[16,127,2048]{2,0,1:T(8,128)(2,1)} %copy-done.2), slice={[0:16], [0:125], [0:2048]} | slice | bytes 16384000 | tf_op jit(solution)/shard_map/slice | solution.py:73
  293.4 7.2 %pad_maximum_fusion = bf16[16,127,2048]{2,0,1:T(8,128)(2,1)} fusion(bf16[16,125,2048]{2,0,1:T(8,128)(2,1)} %slice.90, bf16[16,1,2048]{2,0,1:T(8,128)(2,1)S(1)} %get-tuple-element.18, bf16[16,1,2048]{2,0,1:T(8,128)(2,1)S(1)} %get-tuple-element.17), kind=kLoop, calls=%fused_computation.13 | loop fusion | flops 8323072 | bytes 16646144 | tf_op jit(solution)/shard_map/concatenate | solution.py:72
  300.6 6.4 %reduce-scatter.2.cloned.1.call-done = f32[2,16,1024]{2,1,0:T(8,128)} async-done(((f32[2,16,4096]{2,1,0:T(8,128)}), f32[2,16,1024]{2,1,0:T(8,128)}) %reduce-scatter.2.cloned.1.call-update) | async-done | bytes 131088 | tf_op jit(solution)/shard_map/reduce_scatter | solution.py:109
  307.1 1.6 multiply_convert_fusion
  308.7 0.0 copy-done.1
  (24 shorter events, 0.2 us)
Async XLA Ops:
  7.2 2.2 copy-start
  7.2 1.5 copy-start.10
  7.2 167.5 %all-gather.5.cloned.1.call-start = ((), (), s32[]{:S(2)}) async-start(), calls=%async_computation.4 | async-start | bytes 20971520 | tf_op jit(solution)/shard_map/all_gather | solution.py:102
  7.9 266.9 %all-gather.3.cloned.1.call-start = ((), (), s32[]{:S(2)}) async-start(), calls=%async_computation.3 | async-start | bytes 20971520 | tf_op jit(solution)/shard_map/all_gather | solution.py:101
  11.0 35.3 %all-to-all-start.1 = ((f32[4,2,16,2048]{3,2,1,0:T(8,128)}), f32[4,2,16,2048]{3,2,1,0:T(8,128)S(1)}, u32[]{:S(2)}, u32[]{:S(2)}) async-start(f32[4,2,16,2048]{3,2,1,0:T(8,128)} %bitcast.94), calls=%async_computation.1 | async-start | bytes 2097152 | tf_op jit(solution)/shard_map/all_to_all | solution.py:42
  29.3 16.9 %copy-start.11 = (s32[8]{0:T(128)S(1)}, s32[8]{0:T(128)}, u32[]{:S(2)}) copy-start(s32[8]{0:T(128)} %param.23) | copy-start | bytes 100
  46.3 98.3 %all-to-all-start = ((bf16[4,2,127,2048]{3,1,2,0:T(2,128)(2,1)}), bf16[4,2,127,2048]{3,1,2,0:T(2,128)(2,1)}, u32[]{:S(2)}, u32[]{:S(2)}) async-start(bf16[4,2,127,2048]{3,1,2,0:T(2,128)(2,1)} %copy.23), calls=%async_computation | async-start | bytes 8323072 | tf_op jit(solution)/shard_map/all_to_all | solution.py:41
  51.3 255.7 %reduce-scatter.2.cloned.1.call-start = ((), (), s32[]{:S(2)}) async-start(), calls=%async_computation.5 | async-start | bytes 655360 | tf_op jit(solution)/shard_map/reduce_scatter | solution.py:109
  70.0 11.6 %copy-start.7 = (f32[16,2048]{1,0:T(8,128)S(1)}, f32[16,2048]{1,0:T(8,128)}, u32[]{:S(2)}) copy-start(f32[16,2048]{1,0:T(8,128)} %param.20) | copy-start | bytes 393220
  72.0 9.6 %copy-start.3 = (f32[16,16,2048]{2,1,0:T(8,128)S(1)}, f32[16,16,2048]{2,1,0:T(8,128)}, u32[]{:S(2)}) copy-start(f32[16,16,2048]{2,1,0:T(8,128)} %gather_fusion.3) | copy-start | bytes 6291460
  150.6 7.2 %copy-start.5 = (f32[2048,127]{0,1:T(8,128)S(1)}, f32[2048,127]{0,1:T(8,128)}, u32[]{:S(2)}) copy-start(f32[2048,127]{0,1:T(8,128)} %bitcast_convert_fusion.1) | copy-start | bytes 3121156
  150.6 7.2 %copy-start.9 = (pred[16]{0:T(512)(128)(4,1)S(1)}, pred[16]{0:T(512)(128)(4,1)}, u32[]{:S(2)}) copy-start(pred[16]{0:T(512)(128)(4,1)} %get-tuple-element.8) | copy-start | bytes 52
  157.8 14.4 %copy-start.4 = (f32[2048,126]{0,1:T(8,128)S(1)}, f32[2048,126]{0,1:T(8,128)}, u32[]{:S(2)}) copy-start(f32[2048,126]{0,1:T(8,128)} %bitcast_convert_fusion) | copy-start | bytes 3096580
  168.8 3.4 %copy-start.2 = (bf16[16,127,2048]{2,0,1:T(8,128)(2,1)}, bf16[16,127,2048]{2,0,1:T(8,128)(2,1)S(1)}, u32[]{:S(2)}) copy-start(bf16[16,127,2048]{2,0,1:T(8,128)(2,1)S(1)} %get-tuple-element.6) | copy-start | bytes 24969220
  168.8 5.8 %copy-start.6 = (bf16[2,3,16,2048]{3,2,1,0:T(8,128)(2,1)S(1)}, bf16[2,3,16,2048]{3,2,1,0:T(8,128)(2,1)}, u32[]{:S(2)}) copy-start(bf16[2,3,16,2048]{3,2,1,0:T(8,128)(2,1)} %param.12) | copy-start | bytes 1179652
  274.9 9.5 %copy-start.8 = (pred[1,4,8,128]{3,1,2,0:T(4,128)(4,1)S(1)}, pred[1,4,8,128]{3,1,2,0:T(4,128)(4,1)}, u32[]{:S(2)}) copy-start(pred[1,4,8,128]{3,1,2,0:T(4,128)(4,1)} %copy.46) | copy-start | bytes 12292
  274.9 10.4 %copy-start.12 = (s32[16]{0:T(128)S(1)}, s32[16]{0:T(128)}, u32[]{:S(2)}) copy-start(s32[16]{0:T(128)} %param.17) | copy-start | bytes 196
  293.4 15.3 %copy-start.1 = (f32[16,16,2048]{2,1,0:T(8,128)S(1)}, f32[16,16,2048]{2,1,0:T(8,128)}, u32[]{:S(2)}) copy-start(f32[16,16,2048]{2,1,0:T(8,128)} %param.15) | copy-start | bytes 6291460
Sparse Core Ops, SparseCore 0:
  9.6 156.7 all-gather.4
  167.9 106.8 all-gather.2
  285.4 21.6 reduce-scatter.1
where the time goes:
time: 316 us; the launch traced here: 315 us
  waiting for transfers between devices  155 us (49%)
  local copies, waits for them, and re-layouts  81 us (26%)
  other arithmetic  36 us (11%)
  matrix products  20.1 us (6%)
  between operations  13.9 us (4%)
  starting transfers between devices  9.4 us (3%)
    all_gather x1, waiting for transfers between devices, body(): mr_piece = lax.all_gather(mr_panels, 'engine', axis=0, tiled=True)  88.8 us
    all_to_all x1, waiting for transfers between devices, body(): lax.all_to_all(send_tails, 'engine', split_axis=0, concat_axis=0, tiled=T...  58.1 us
    gather x1, local copies, waits for them, and re-layouts, body(): conv_tails[src_local]  18.6 us
    reshape x2, local copies, waits for them, and re-layouts, body(): conv_tails[send_index.reshape(-1)].reshape(engines, CAP, tail_len, width)  16.3 us
    gather x1, local copies, waits for them, and re-layouts, body(): conv_tails[send_index.reshape(-1)].reshape(engines, CAP, tail_len, width)  13.2 us
    dot_general x1, matrix products, body(): jnp.einsum('srd,gdc->srgc', li_rows, li_piece, preferred_element_type=jnp...  11.4 us
    dot_general x1, other arithmetic, body(): jnp.einsum('rtc,tc->rc', tails, mr_filter[1:], preferred_element_type=jnp...  11 us
    dot_general x1, matrix products, body(): jnp.einsum('srd,gdc->srgc', mr_rows, mr_piece, preferred_element_type=jnp...  8.7 us
  transfers between devices with their start and end apart: 5, of which 3 were waited for; matrix products, arithmetic and copies ran while one was open for 39% of the time, Pallas kernels for 0%

commit v1 on v0

v1 whole, which is shorter than its diff:
```python
import functools

import jax
import jax.numpy as jnp
from jax import lax
from jax.experimental import pallas as pl
from jax.experimental.pallas import tpu as pltpu
from jax.sharding import PartitionSpec as P

CAP = 2
BF = jnp.bfloat16
F32 = jnp.float32
ANY = pl.BlockSpec(memory_space=pl.ANY)
SM = pl.BlockSpec(memory_space=pltpu.SMEM)
VM = pl.BlockSpec(memory_space=pltpu.VMEM)
VLIM = 56 << 20


def lane_chunk(width):
    for size in (256, 128):
        if width % size == 0:
            return size
    return width


def links(engines):
    chips = engines // 2
    return [(k, f) for k in range(chips) for f in (0, 1)]


def send(x, engines, k, f):
    chips = engines // 2
    pairs = [(e, ((e // 2 + k) % chips) * 2 + ((e % 2) ^ f)) for e in range(engines)]
    return lax.ppermute(x, "engine", pairs)


def to_engine(me, k, f, engines):
    chips = engines // 2
    return ((me // 2 + k) % chips) * 2 + ((me % 2 + f) % 2)


def relation_of(me, owner, engines):
    chips = engines // 2
    k = (me // 2 + chips - owner // 2) % chips
    return 2 * k + (owner + me) % 2


def shifted_filters(filt_ref, f1, f2, width, chunk):
    taps = filt_ref.shape[0]
    for c in range(0, width, chunk):
        cols = pl.ds(c, chunk)
        f = filt_ref[:, cols].astype(F32)
        f1[0 : taps - 1, cols] = f[1:taps]
        f2[0 : taps - 2, cols] = f[2:taps]
        f2[taps - 2 : taps - 1, cols] = jnp.zeros((1, chunk), F32)


def pack_body(engines, rows, source, tails, states, filt, decay, resid, *refs):
    others = engines - 1
    count = others * CAP
    msgs = refs[: 1 + (others - 1) * CAP]
    parts = refs[len(msgs) : len(msgs) + others]
    f1, f2, tbuf, sbuf, mbuf, index, tsem, ssem, osem = refs[len(msgs) + others :]
    width = tails.shape[2]
    tail_len = tails.shape[1]
    modes = states.shape[1]
    chunk = lane_chunk(width)
    me = lax.axis_index("engine")
    rels = links(engines)
    order = [(rel, j) for rel in range(2, engines) for j in range(CAP)] + [(1, j) for j in range(CAP)]

    def fetch(rel, j):
        slot = (rel - 1) * CAP + j
        row = index[rel * (CAP + 1) + j]
        return (
            pltpu.make_async_copy(tails.at[row], tbuf.at[slot], tsem.at[slot]),
            pltpu.make_async_copy(states.at[row], sbuf.at[slot], ssem.at[slot]),
        )

    for rel in range(1, engines):
        k, f = rels[rel]
        there = to_engine(me, k, f, engines)
        for j in range(CAP):
            index[rel * (CAP + 1) + j] = 0

        def scan(i, found):
            old = source[there * rows + i]
            index[rel * (CAP + 1) + jnp.minimum(found, CAP)] = old % rows
            return found + jnp.where(old // rows == me, 1, 0)

        lax.fori_loop(0, rows, scan, 0)
    for rel, j in order:
        for copy in fetch(rel, j):
            copy.start()
    shifted_filters(filt, f1, f2, width, chunk)

    def target(rel, j):
        slot = (rel - 1) * CAP + j
        out = msgs[0].at[j] if rel == 1 else msgs[1 + (rel - 2) * CAP + j]
        return pltpu.make_async_copy(mbuf.at[slot], out, osem.at[slot])

    for rel, j in order:
        slot = (rel - 1) * CAP + j
        for copy in fetch(rel, j):
            copy.wait()

        def columns(c, carry):
            cols = pl.ds(pl.multiple_of(c * chunk, chunk), chunk)
            t = tbuf[slot, :, cols].astype(F32)
            parts[rel - 1][4 * j : 4 * j + 1, cols] = jnp.sum(t * f1[:, cols], axis=0, keepdims=True)
            parts[rel - 1][4 * j + 1 : 4 * j + 2, cols] = jnp.sum(t * f2[:, cols], axis=0, keepdims=True)
            mbuf[slot, 0:tail_len, cols] = jnp.concatenate(
                [jnp.zeros((2, chunk), F32), t[: tail_len - 2]], axis=0
            ).astype(BF)
            s = sbuf[slot, :, cols]
            d = decay[:, cols]
            a = resid[:, cols] * d * s
            parts[rel - 1][4 * j + 2 : 4 * j + 3, cols] = jnp.sum(a, axis=0, keepdims=True)
            parts[rel - 1][4 * j + 3 : 4 * j + 4, cols] = jnp.sum(a * d, axis=0, keepdims=True)
            mbuf[slot, tail_len + 1 : tail_len + 1 + modes, cols] = s.astype(BF)
            return carry

        lax.fori_loop(0, width // chunk, columns, 0)
        target(rel, j).start()
    for rel, j in order:
        target(rel, j).wait()


def keep_body(engines, rows, source, tails, states, filt, decay, resid, mr, li, new_tails, new_states, parts, gates,
              f1, f2, tbuf, sbuf, obuf, tsem, ssem, otsem, ossem):
    width = tails.shape[2]
    tail_len = tails.shape[1]
    chunk = lane_chunk(width)
    me = lax.axis_index("engine")

    def fetch(r):
        row = source[me * rows + r] % rows
        return (
            pltpu.make_async_copy(tails.at[row], tbuf.at[r], tsem.at[r]),
            pltpu.make_async_copy(states.at[row], sbuf.at[r], ssem.at[r]),
        )

    def store(r):
        return (
            pltpu.make_async_copy(obuf.at[r], new_tails.at[r], otsem.at[r]),
            pltpu.make_async_copy(sbuf.at[r], new_states.at[r], ossem.at[r]),
        )

    def stays(r):
        return source[me * rows + r] // rows == me

    def begin(r, carry):
        @pl.when(stays(r))
        def _():
            for copy in fetch(r):
                copy.start()

        return carry

    lax.fori_loop(0, rows, begin, 0)
    shifted_filters(filt, f1, f2, width, chunk)
    for c in range(0, width, chunk):
        cols = pl.ds(c, chunk)
        for step in range(2):
            gates[step, :, cols] = (
                (mr[step, 1, :, cols].astype(F32) * mr[step, 2, :, cols].astype(F32)).astype(BF).astype(F32)
            )
            gates[2 + step, :, cols] = (
                (li[step, 1, :, cols].astype(F32) * li[step, 2, :, cols].astype(F32)).astype(BF).astype(F32)
            )

    def work(r, carry):
        @pl.when(stays(r))
        def _():
            for copy in fetch(r):
                copy.wait()

            def columns(c, inner):
                cols = pl.ds(pl.multiple_of(c * chunk, chunk), chunk)
                one = pl.ds(r, 1)
                t = tbuf[r, :, cols].astype(F32)
                parts[0, one, cols] = jnp.sum(t * f1[:, cols], axis=0, keepdims=True)
                parts[1, one, cols] = jnp.sum(t * f2[:, cols], axis=0, keepdims=True)
                obuf[r, :, cols] = jnp.concatenate(
                    [gates[1, one, cols], gates[0, one, cols], t[: tail_len - 2]], axis=0
                ).astype(BF)
                s = sbuf[r, :, cols]
                d = decay[:, cols]
                w = resid[:, cols]
                ds = d * s
                parts[2, one, cols] = jnp.sum(w * ds, axis=0, keepdims=True)
                parts[3, one, cols] = jnp.sum(w * d * ds, axis=0, keepdims=True)
                sbuf[r, :, cols] = d * (ds + gates[2, one, cols]) + gates[3, one, cols]
                return inner

            lax.fori_loop(0, width // chunk, columns, 0)
            for copy in store(r):
                copy.start()

        return carry

    lax.fori_loop(0, rows, work, 0)

    def finish(r, carry):
        @pl.when(stays(r))
        def _():
            for copy in store(r):
                copy.wait()

        return carry

    lax.fori_loop(0, rows, finish, 0)


def arrivals(engines, rows, source, slots, found, me):
    for rel in range(engines):
        found[rel] = 0

    def scan(r, carry):
        rel = relation_of(me, source[me * rows + r] // rows, engines)
        at = found[rel]
        slots[rel * (CAP + 1) + jnp.minimum(at, CAP)] = r
        found[rel] = at + 1
        return carry

    lax.fori_loop(0, rows, scan, 0)


def mix_body(engines, rows, source, parts_in, gates, mr, li, filt, decay, resid, *refs):
    got = refs[: engines - 1]
    y, parts, slots, found = refs[engines - 1 :]
    width = y.shape[1]
    chunk = lane_chunk(width)
    me = lax.axis_index("engine")
    arrivals(engines, rows, source, slots, found, me)
    parts[...] = parts_in[...]
    for rel in range(1, engines):
        for j in range(CAP):

            @pl.when(found[rel] > j)
            def _():
                one = pl.ds(slots[rel * (CAP + 1) + j], 1)
                for i in range(4):
                    parts[i, one, :] = got[rel - 1][4 * j + i : 4 * j + i + 1, :].astype(F32)

    for c in range(0, width, chunk):
        cols = pl.ds(c, chunk)
        f = filt[0:16, cols].astype(F32)
        d = decay[:, cols]
        w = resid[:, cols]
        r0 = jnp.sum(w, axis=0, keepdims=True)
        r1 = jnp.sum(w * d, axis=0, keepdims=True)
        conv0 = f[0:1] * gates[0, :, cols] + parts[0, :, cols]
        conv1 = f[0:1] * gates[1, :, cols] + f[1:2] * gates[0, :, cols] + parts[1, :, cols]
        y[0:rows, cols] = (mr[0, 0, :, cols].astype(F32) * conv0).astype(BF)
        y[rows : 2 * rows, cols] = (mr[1, 0, :, cols].astype(F32) * conv1).astype(BF)
        modal0 = parts[2, :, cols] + gates[2, :, cols] * r0
        modal1 = parts[3, :, cols] + gates[2, :, cols] * r1 + gates[3, :, cols] * r0
        y[2 * rows : 3 * rows, cols] = (li[0, 0, :, cols].astype(F32) * modal0).astype(BF)
        y[3 * rows : 4 * rows, cols] = (li[1, 0, :, cols].astype(F32) * modal1).astype(BF)


def project_body(engines, rows, slots_here, depth, *refs):
    ys = refs[:engines]
    mr_w, li_w = refs[engines : engines + 2]
    outs = refs[engines + 2 : 2 * engines + 2]
    x, acc = refs[2 * engines + 2 :]
    two = 2 * rows
    width = ys[0].shape[1]
    pw = mr_w.shape[2]
    step = pl.program_id(0)

    @pl.when(step == 0)
    def _():
        for rel in range(engines):
            for b in range(width // depth):
                x[b, 0, rel * two : (rel + 1) * two, :] = ys[rel][0:two, b * depth : (b + 1) * depth]
                x[b, 1, rel * two : (rel + 1) * two, :] = ys[rel][two : 2 * two, b * depth : (b + 1) * depth]
        acc[...] = jnp.zeros_like(acc)

    for g in range(slots_here):
        cols = slice(g * pw, (g + 1) * pw)
        acc[:, cols] += jnp.dot(x[step, 0], mr_w[g], preferred_element_type=F32) + jnp.dot(
            x[step, 1], li_w[g], preferred_element_type=F32
        )

    @pl.when(step == pl.num_programs(0) - 1)
    def _():
        for rel in range(engines):
            outs[rel][...] = acc[rel * two : (rel + 1) * two, :].astype(BF)


def sort_body(engines, chans, slots_here, slot_of, *refs):
    got = refs[:engines]
    outs = refs[engines : engines + chans]
    tiles = refs[engines + chans]
    pw = tiles.shape[2]
    me = lax.axis_index("engine")
    here = lax.axis_index("chan")
    per_chan = slot_of.shape[0] // chans
    for rel in range(engines):
        for g in range(slots_here):
            tiles[rel * slots_here + g] = got[rel][:, g * pw : (g + 1) * pw]
    for d in range(chans):
        there = (here + d) % chans
        for h in range(per_chan):
            slot = slot_of[there * per_chan + h]
            rel = relation_of(me, slot // slots_here, engines)
            outs[d][:, h * pw : (h + 1) * pw] = tiles[rel * slots_here + slot % slots_here]


def place_body(engines, rows, items, source, gates, decay, *refs):
    msgs = refs[: len(items)]
    old_tails, old_states = refs[len(items) : len(items) + 2]
    new_tails, new_states = refs[len(items) + 2 : len(items) + 4]
    mbuf, obuf, sbuf, slots, found, isem, osem, ssem = refs[len(items) + 4 :]
    tail_len = new_tails.shape[1]
    width = new_tails.shape[2]
    modes = new_states.shape[1]
    chunk = lane_chunk(width)
    me = lax.axis_index("engine")

    def inbound(n):
        return pltpu.make_async_copy(msgs[n], mbuf.at[n], isem.at[n])

    def outbound(n, row):
        return (
            pltpu.make_async_copy(obuf.at[n], new_tails.at[row], osem.at[n]),
            pltpu.make_async_copy(sbuf.at[n], new_states.at[row], ssem.at[n]),
        )

    for n in range(len(items)):
        inbound(n).start()
    arrivals(engines, rows, source, slots, found, me)
    for n, (rel, j) in enumerate(items):
        inbound(n).wait()

        @pl.when(found[rel] > j)
        def _():
            row = slots[rel * (CAP + 1) + j]
            one = pl.ds(row, 1)

            def columns(c, carry):
                cols = pl.ds(pl.multiple_of(c * chunk, chunk), chunk)
                obuf[n, :, cols] = mbuf[n, 0:tail_len, cols]
                obuf[n, 0:2, cols] = jnp.concatenate([gates[1, one, cols], gates[0, one, cols]], axis=0).astype(BF)
                s = mbuf[n, tail_len + 1 : tail_len + 1 + modes, cols].astype(F32)
                d = decay[:, cols]
                sbuf[n, :, cols] = d * (d * s + gates[2, one, cols]) + gates[3, one, cols]
                return carry

            lax.fori_loop(0, width // chunk, columns, 0)
            for copy in outbound(n, row):
                copy.start()

    for n, (rel, j) in enumerate(items):

        @pl.when(found[rel] > j)
        def _():
            for copy in outbound(n, slots[rel * (CAP + 1) + j]):
                copy.wait()


def body(mr_qkv, li_qkv, conv_tails, modal_states, source, remaining, mr_filter, li_decay, li_residue, mr_panels,
         li_panels, panel_slot):
    engines = lax.axis_size("engine")
    chans = lax.axis_size("chan")
    rows, tail_len, width = conv_tails.shape
    modes = modal_states.shape[1]
    taps = mr_filter.shape[0]
    slots_here, _, pw = mr_panels.shape
    others = engines - 1
    count = others * CAP
    chips = engines // 2
    rels = links(engines)
    msg_rows = tail_len + 1 + modes
    sds = jax.ShapeDtypeStruct
    dma = pltpu.SemaphoreType.DMA
    params = pltpu.CompilerParams(vmem_limit_bytes=VLIM)

    cross = [(rel, j) for rel in range(2, engines) for j in range(CAP)]
    packed = pl.pallas_call(
        functools.partial(pack_body, engines, rows),
        in_specs=[SM, ANY, ANY, VM, VM, VM],
        out_specs=[ANY] * (1 + len(cross)) + [VM] * others,
        out_shape=[sds((CAP, msg_rows, width), BF)]
        + [sds((msg_rows, width), BF)] * len(cross)
        + [sds((4 * CAP, width), F32)] * others,
        scratch_shapes=[
            pltpu.VMEM((taps - 1, width), F32),
            pltpu.VMEM((taps - 1, width), F32),
            pltpu.VMEM((count, tail_len, width), BF),
            pltpu.VMEM((count, modes, width), F32),
            pltpu.VMEM((count, msg_rows, width), BF),
            pltpu.SMEM((engines * (CAP + 1),), jnp.int32),
            dma((count,)),
            dma((count,)),
            dma((count,)),
        ],
        compiler_params=params,
        name="pack",
    )(source, conv_tails, modal_states, mr_filter, li_decay, li_residue)
    near_msg = packed[0]
    far_msgs = packed[1 : 1 + len(cross)]
    parts_out = packed[1 + len(cross) :]

    quarter = (len(cross) + 3) // 4
    batch = [list(range(i * quarter, min((i + 1) * quarter, len(cross)))) for i in range(4)]
    far_got = {}

    def launch(group, token=None):
        for n in group:
            msg = far_msgs[n]
            if token is not None:
                msg, _ = lax.optimization_barrier((msg, token))
            k, f = rels[cross[n][0]]
            far_got[n] = send(msg, engines, k, f)

    parts_got = [send(parts_out[rel - 1], engines, *rels[rel]) for rel in range(1, engines)]
    launch(batch[0])
    near_got = send(near_msg, engines, 0, 1)

    new_tails, new_states, parts, gates = pl.pallas_call(
        functools.partial(keep_body, engines, rows),
        in_specs=[SM, ANY, ANY, VM, VM, VM, VM, VM],
        out_specs=[ANY, ANY, VM, VM],
        out_shape=[
            sds((rows, tail_len, width), BF),
            sds((rows, modes, width), F32),
            sds((4, rows, width), F32),
            sds((4, rows, width), F32),
        ],
        scratch_shapes=[
            pltpu.VMEM((taps - 1, width), F32),
            pltpu.VMEM((taps - 1, width), F32),
            pltpu.VMEM((rows, tail_len, width), BF),
            pltpu.VMEM((rows, modes, width), F32),
            pltpu.VMEM((rows, tail_len, width), BF),
            dma((rows,)),
            dma((rows,)),
            dma((rows,)),
            dma((rows,)),
        ],
        compiler_params=params,
        name="keep",
    )(source, conv_tails, modal_states, mr_filter, li_decay, li_residue, mr_qkv, li_qkv)
    launch(batch[1], gates[0, 0, 0])

    y = pl.pallas_call(
        functools.partial(mix_body, engines, rows),
        in_specs=[SM] + [VM] * 7 + [VM] * others,
        out_specs=VM,
        out_shape=sds((4 * rows, width), BF),
        scratch_shapes=[
            pltpu.VMEM((4, rows, width), F32),
            pltpu.SMEM((engines * (CAP + 1),), jnp.int32),
            pltpu.SMEM((engines,), jnp.int32),
        ],
        compiler_params=params,
        name="mix",
    )(source, parts, gates, mr_qkv, li_qkv, mr_filter, li_decay, li_residue, *parts_got)

    same_core = [y] + [send(y, engines, k, 0) for k in range(1, chips)]
    launch(batch[2], y[0, 0])
    ys = []
    for k in range(chips):
        ys += [same_core[k], send(same_core[k], engines, 0, 1)]

    depth = 512
    outs = pl.pallas_call(
        functools.partial(project_body, engines, rows, slots_here, depth),
        grid=(width // depth,),
        in_specs=[pl.BlockSpec((4 * rows, width), lambda i: (0, 0))] * engines
        + [pl.BlockSpec((slots_here, depth, pw), lambda i: (0, i, 0))] * 2,
        out_specs=[pl.BlockSpec((2 * rows, slots_here * pw), lambda i: (0, 0))] * engines,
        out_shape=[sds((2 * rows, slots_here * pw), BF)] * engines,
        scratch_shapes=[
            pltpu.VMEM((width // depth, 2, engines * 2 * rows, depth), BF),
            pltpu.VMEM((engines * 2 * rows, slots_here * pw), F32),
        ],
        compiler_params=params,
        name="project",
    )(*ys, mr_panels, li_panels)

    back = [outs[0]]
    for k, f in rels[1:]:
        back.append(send(outs[2 * ((chips - k) % chips) + f], engines, k, f))
    launch(batch[3], outs[0][0, 0])

    per_chan = panel_slot.shape[0] // chans
    blocks = pl.pallas_call(
        functools.partial(sort_body, engines, chans, slots_here),
        in_specs=[SM] + [VM] * engines,
        out_specs=[VM] * chans,
        out_shape=[sds((2 * rows, per_chan * pw), BF)] * chans,
        scratch_shapes=[pltpu.VMEM((engines * slots_here, 2 * rows, pw), BF)],
        compiler_params=params,
        name="sort",
    )(panel_slot, *back)
    total = blocks[0].astype(F32)
    for d in range(1, chans):
        total = total + lax.ppermute(blocks[d], "chan", [(c, (c + d) % chans) for c in range(chans)]).astype(F32)
    steps_ids = jnp.arange(2, dtype=jnp.int32)
    active = (remaining[None, :] > steps_ids[:, None]).astype(F32)
    mixed = (total.reshape(2, rows, per_chan * pw) * active[:, :, None]).astype(BF)

    def place(items, arrays, tails, states):
        return pl.pallas_call(
            functools.partial(place_body, engines, rows, items),
            in_specs=[SM, VM, VM] + [ANY] * (len(items) + 2),
            out_specs=[ANY, ANY],
            out_shape=[sds(tails.shape, BF), sds(states.shape, F32)],
            input_output_aliases={3 + len(items): 0, 4 + len(items): 1},
            scratch_shapes=[
                pltpu.VMEM((len(items), msg_rows, width), BF),
                pltpu.VMEM((len(items), tail_len, width), BF),
                pltpu.VMEM((len(items), modes, width), F32),
                pltpu.SMEM((engines * (CAP + 1),), jnp.int32),
                pltpu.SMEM((engines,), jnp.int32),
                dma((len(items),)),
                dma((len(items),)),
                dma((len(items),)),
            ],
            compiler_params=params,
            name="place",
        )(source, gates, li_decay, *arrays, tails, states)

    new_tails, new_states = place(
        [(1, j) for j in range(CAP)], [near_got[j] for j in range(CAP)], new_tails, new_states
    )
    for group in batch:
        if group:
            new_tails, new_states = place([cross[n] for n in group], [far_got[n] for n in group], new_tails, new_states)
    return (mixed, new_tails, new_states)


def solution(mesh):
    return jax.shard_map(
        body,
        mesh=mesh,
        in_specs=(
            P(None, None, ("group", "engine"), "chan"),
            P(None, None, ("group", "engine"), "chan"),
            P(("group", "engine"), None, "chan"),
            P(("group", "engine"), None, "chan"),
            P("group"),
            P(("group", "engine")),
            P(None, "chan"),
            P(None, "chan"),
            P(None, "chan"),
            P("engine", "chan", None),
            P("engine", "chan", None),
            P(),
        ),
        out_specs=(
            P(None, ("group", "engine"), "chan"),
            P(("group", "engine"), None, "chan"),
            P(("group", "engine"), None, "chan"),
        ),
        check_vma=False,
    )
```

time: 316 us -> 139 us (0.44)
  waiting for transfers between devices: 155 us -> 44.6 us
  local copies, waits for them, and re-layouts: 81 us -> 29 us
  Pallas kernels: 0 us -> 45.2 us
  other arithmetic: 36 us -> 1.59 us
  matrix products: 20.1 us -> 0 us
  between operations: 13.9 us -> 0.84 us
  starting transfers between devices: 9.4 us -> 17.3 us
    all_gather x2 -> x0, waiting for transfers between devices: 88.8 us -> none  [the longest x1 88.8 us: body(): mr_piece = lax.all_gather(mr_panels, 'engine', axis=0, tiled=True)]
    all_to_all x2 -> x0, waiting for transfers between devices: 58.1 us -> none  [the longest x1 58.1 us: body(): lax.all_to_all(send_tails, 'engine', split_axis=0, concat_axis=0, tiled=T...]
    gather x8 -> x0, local copies, waits for them, and re-layouts: 45.5 us -> none  [the longest x1 18.6 us: body(): conv_tails[src_local]]
    pallas_call x0 -> x10, Pallas kernels: none -> 45.2 us  [the longest x5 16.1 us: place(): pl.pallas_call(functools.partial(place_body, engines, rows, items), in_sp...]
    ppermute x0 -> x17, waiting for transfers between devices: none -> 44.6 us  [the longest x14 41.2 us: send(): return lax.ppermute(x, 'engine', pairs)]
    unnamed x28 -> x40, local copies, waits for them, and re-layouts: 4.08 us -> 27.8 us
    dot_general x2 -> x0, matrix products: 20.1 us -> none  [the longest x1 11.4 us: body(): jnp.einsum('srd,gdc->srgc', li_rows, li_piece, preferred_element_type=jnp...]
    ppermute x0 -> x17, starting transfers between devices: none -> 17.3 us  [the longest x14 11.8 us: send(): return lax.ppermute(x, 'engine', pairs)]
  transfers between devices with their start and end apart: 5 -> 17, of which waited for: 3 -> 7; matrix products, arithmetic and copies ran while one was open for 39% -> 2% of each run, Pallas kernels for 0% -> 23%
where the time goes in v1:
time: 139 us
  Pallas kernels  45.2 us (33%)
  waiting for transfers between devices  44.6 us (32%)
  local copies, waits for them, and re-layouts  29 us (21%)
  starting transfers between devices  17.3 us (12%)
  other arithmetic  1.59 us (1%)
    ppermute x14, waiting for transfers between devices, send(): return lax.ppermute(x, 'engine', pairs)  41.2 us
    unnamed x40, local copies, waits for them, and re-layouts  27.8 us
    pallas_call x5, Pallas kernels, place(): pl.pallas_call(functools.partial(place_body, engines, rows, items), in_sp...  16.1 us
    ppermute x14, starting transfers between devices, send(): return lax.ppermute(x, 'engine', pairs)  11.8 us
    pallas_call x1, Pallas kernels, body(): pl.pallas_call(functools.partial(keep_body, engines, rows), in_specs=[SM,...  10.6 us
    pallas_call x1, Pallas kernels, body(): pl.pallas_call(functools.partial(pack_body, engines, rows), in_specs=[SM,...  7.62 us
    pallas_call x1, Pallas kernels, body(): pl.pallas_call(functools.partial(project_body, engines, rows, slots_here,...  5.85 us
    ppermute x3, starting transfers between devices, body(): lax.ppermute(blocks[d], 'chan', [(c, (c + d) % chans) for c in range(chan...  5.43 us
  transfers between devices with their start and end apart: 17, of which 7 were waited for; matrix products, arithmetic and copies ran while one was open for 2% of the time, Pallas kernels for 23%

profile of v1, /device:TPU:0, one launch (start us, length us, event | category | flops | bytes accessed | tf_op | source)
XLA Modules:
  0.0 138.5 jit_solution(16284298644305832214)
XLA Ops:
  0.6 11.2 %copy.25.tails = bf16[16,127,2048]{2,1,0:T(8,128)(2,1)} copy(bf16[16,127,2048]{2,0,1:T(8,128)(2,1)} %param.14) | data formatting | bytes 16646144 | tf_op args[2]
  11.8 7.6 %pack.1 = (bf16[2,144,2048]{2,1,0:T(8,128)(2,1)}, bf16[144,2048]{1,0:T(8,128)(2,1)}, bf16[144,2048]{1,0:T(8,128)(2,1)}, bf16[144,2048]{1,0:T(8,128)(2,1)}, bf16[...) custom-call(s32[64]{0:T(128)} %source.15, ...), custom_call_target="tpu_custom_call" | custom-call | tf_op jit(solution)/shard_map/pack/pallas_call | solution.py:382
  19.5 0.5 collective-permute-start
  20.0 2.6 %collective-permute-start.1 = (f32[8,2048]{1,0:T(8,128)}, f32[8,2048]{1,0:T(8,128)S(1)}, u32[]{:S(2)}, u32[]{:S(2)}) collective-permute-start(f32[8,2048]{1,0:T(8,128)} %get-tuple-element.36), channel_id=1, source_target_pairs={{0,8},{4,12},{8,0},{12,4},{1,9},{5,13},{9,1},{13,5},{2,10},{6,14},... | collective-permute-start | bytes 196616 | tf_op jit(solution)/shard_map/ppermute | solution.py:34
  22.6 0.1 collective-permute-start.2
  22.7 10.6 %keep.1 = (bf16[16,127,2048]{2,1,0:T(8,128)(2,1)}, f32[16,16,2048]{2,1,0:T(8,128)}, f32[4,16,2048]{2,1,0:T(8,128)}, f32[4,16,2048]{2,1,0:T(8,128)}) custom-call(s32[64]{0:T(128)} %source.15, bf16[16,127,2048]{2,1,0:T(8,128)(2,1)} %copy.25.tails, f32[16,16,2048]{2,1,0:T(8,128)} %states.3, bf16[128,2048]{1,0:T(8,128)(2,1)} %filt.5, f32[16,2048]{1,0:T(8,128)} %decay.15, ...), custom_call_target="tpu_custom_call" | custom-call | tf_op jit(solution)/shard_map/keep/pallas_call | solution.py:423
  33.3 0.0 collective-permute-done.refs_0_
  33.3 0.0 copy-start.7
  33.3 0.0 collective-permute-done.1.refs_1_
  33.3 0.0 collective-permute-done.2.refs_2_
  33.3 0.0 copy-start.9
  33.4 0.6 copy-done.7
  33.9 0.0 copy-done.8
  33.9 0.0 copy-done.9
  34.0 3.2 %mix.1.refs_0_ = bf16[64,2048]{1,0:T(8,128)(2,1)} custom-call(s32[64]{0:T(128)} %source.15, f32[4,16,2048]{2,1,0:T(8,128)} %get-tuple-element.33.parts_in, f32[4,16,2048]{2,1,0:T(8,128)} %get-tuple-element.34.gates, bf16[2,3,16,2048]{3,2,1,0:T(8,128)(2,1)} %mr.3, bf16[2,3,16,2048]{3,2,1,0:T(8,128)(2,1)} %li.3, bf16[128,2048]{1,0:T(8,128)(2,1)} %filt.5, ...), custom_call_target="tpu_custom_call" | custom-call | tf_op jit(solution)/shard_map/mix/pallas_call | solution.py:449
  37.2 1.7 %collective-permute-start.4 = (bf16[64,2048]{1,0:T(8,128)(2,1)}, bf16[64,2048]{1,0:T(8,128)(2,1)S(1)}, u32[]{:S(2)}, u32[]{:S(2)}) collective-permute-start(bf16[64,2048]{1,0:T(8,128)(2,1)} %mix.1.refs_0_), channel_id=1, source_target_pairs={{0,8},{4,12},{8,0},{12,4},{1,9},{5,13},{9,1},{13,5},{2,10},{6,14},... | collective-permute-start | bytes 786440 | tf_op jit(solution)/shard_map/ppermute | solution.py:34
  38.9 0.1 collective-permute-start.16
  39.0 0.4 collective-permute-start.3
  39.5 6.4 %collective-permute-done.4.refs_2_ = bf16[64,2048]{1,0:T(8,128)(2,1)S(1)} collective-permute-done((bf16[64,2048]{1,0:T(8,128)(2,1)}, bf16[64,2048]{1,0:T(8,128)(2,1)S(1)}, u32[]{:S(2)}, u32[]{:S(2)}) %collective-permute-start.4) | collective-permute-done | bytes 262176 | tf_op jit(solution)/shard_map/ppermute | solution.py:34
  45.9 0.0 collective-permute-start.5
  45.9 0.0 collective-permute-done.3.refs_1_
  45.9 0.0 copy-start.5
  45.9 1.5 %collective-permute-done.5.refs_3_ = bf16[64,2048]{1,0:T(8,128)(2,1)S(1)} collective-permute-done((bf16[64,2048]{1,0:T(8,128)(2,1)S(1)}, bf16[64,2048]{1,0:T(8,128)(2,1)S(1)}, u32[]{:S(2)}, u32[]{:S(2)}) %collective-permute-start.5) | collective-permute-done | bytes 262176 | tf_op jit(solution)/shard_map/ppermute | solution.py:34
  47.4 0.7 copy-done.6
  48.1 5.9 %project.1 = (bf16[32,1024]{1,0:T(8,128)(2,1)}, bf16[32,1024]{1,0:T(8,128)(2,1)}, bf16[32,1024]{1,0:T(8,128)(2,1)}, bf16[32,1024]{1,0:T(8,128)(2,1)}) custom-call(bf16[64,2048]{1,0:T(8,128)(2,1)} %mix.1.refs_0_, bf16[64,2048]{1,0:T(8,128)(2,1)} %copy-done.5, bf16[64,2048]{1,0:T(8,128)(2,1)} %copy-done.4, bf16[64,2048]{1,0:T(8,128)(2,1)} %copy-done.6, ...), custom_call_target="tpu_custom_call" | custom-call | tf_op jit(solution)/shard_map/project/pallas_call | solution.py:470
  54.0 0.2 collective-permute-start.6
  54.2 1.8 %collective-permute-start.7 = (bf16[32,1024]{1,0:T(8,128)(2,1)}, bf16[32,1024]{1,0:T(8,128)(2,1)S(1)}, u32[]{:S(2)}, u32[]{:S(2)}) collective-permute-start(bf16[32,1024]{1,0:T(8,128)(2,1)} %get-tuple-element.40), channel_id=1, source_target_pairs={{0,8},{4,12},{8,0},{12,4},{1,9},{5,13},{9,1},{13,5},{2,10},{6,14},... | collective-permute-start | bytes 196616 | tf_op jit(solution)/shard_map/ppermute | solution.py:34
  55.9 0.0 collective-permute-start.8
  55.9 1.8 %collective-permute-start.12 = (bf16[144,2048]{1,0:T(8,128)(2,1)S(1)}, bf16[144,2048]{1,0:T(8,128)(2,1)S(1)}, u32[]{:S(2)}, u32[]{:S(2)}) collective-permute-start(bf16[144,2048]{1,0:T(8,128)(2,1)S(1)} %copy-done.14), channel_id=1, source_target_pairs={{0,12},{4,8},{8,4},{12,0},{1,13},{5,9},{9,5},{13,1},{2,14},{6,10},... | collective-permute-start | bytes 1769480 | tf_op jit(solution)/shard_map/ppermute | solution.py:34
  57.7 0.0 collective-permute-done.6.refs_1_
  57.7 1.0 collective-permute-done.7.refs_2_
  58.8 1.6 %collective-permute-done.8.refs_3_ = bf16[32,1024]{1,0:T(8,128)(2,1)S(1)} collective-permute-done((bf16[32,1024]{1,0:T(8,128)(2,1)}, bf16[32,1024]{1,0:T(8,128)(2,1)S(1)}, u32[]{:S(2)}, u32[]{:S(2)}) %collective-permute-start.8) | collective-permute-done | bytes 65568 | tf_op jit(solution)/shard_map/ppermute | solution.py:34
  60.4 0.6 copy-done.12
  61.0 1.8 %sort.1 = (bf16[32,1024]{1,0:T(8,128)(2,1)}, bf16[32,1024]{1,0:T(8,128)(2,1)}, bf16[32,1024]{1,0:T(8,128)(2,1)}, bf16[32,1024]{1,0:T(8,128)(2,1)}) custom-call(s32[8]{0:T(128)} %slot_of.1, bf16[32,1024]{1,0:T(8,128)(2,1)} %get-tuple-element.38.refs_0_, bf16[32,1024]{1,0:T(8,128)(2,1)} %copy-done.10, bf16[32,1024]{1,0:T(8,128)(2,1)} %copy-done.11, ...), custom_call_target="tpu_custom_call" | custom-call | tf_op jit(solution)/shard_map/sort/pallas_call | solution.py:491
  62.8 1.5 %collective-permute-start.9 = (bf16[32,1024]{1,0:T(8,128)(2,1)}, bf16[32,1024]{1,0:T(8,128)(2,1)S(1)}, u32[]{:S(2)}, u32[]{:S(2)}) collective-permute-start(bf16[32,1024]{1,0:T(8,128)(2,1)} %get-tuple-element.43), channel_id=1, source_target_pairs={{0,1},{1,2},{2,3},{3,0},{4,5},{5,6},{6,7},{7,4},{8,9},{9,10},{10,1... | collective-permute-start | bytes 196616 | tf_op jit(solution)/shard_map/ppermute | solution.py:502
  64.3 2.6 %collective-permute-start.10 = (bf16[32,1024]{1,0:T(8,128)(2,1)}, bf16[32,1024]{1,0:T(8,128)(2,1)S(1)}, u32[]{:S(2)}, u32[]{:S(2)}) collective-permute-start(bf16[32,1024]{1,0:T(8,128)(2,1)} %get-tuple-element.44), channel_id=1, source_target_pairs={{0,2},{1,3},{2,0},{3,1},{4,6},{5,7},{6,4},{7,5},{8,10},{9,11},{10,... | collective-permute-start | bytes 196616 | tf_op jit(solution)/shard_map/ppermute | solution.py:502
  66.8 1.3 collective-permute-start.11
  68.2 1.3 collective-permute-done.9
  69.5 0.7 collective-permute-start.13
  70.2 2.1 %collective-permute-done.10 = bf16[32,1024]{1,0:T(8,128)(2,1)S(1)} collective-permute-done((bf16[32,1024]{1,0:T(8,128)(2,1)}, bf16[32,1024]{1,0:T(8,128)(2,1)S(1)}, u32[]{:S(2)}, u32[]{:S(2)}) %collective-permute-start.10) | collective-permute-done | bytes 65568 | tf_op jit(solution)/shard_map/ppermute | solution.py:502
  72.3 1.3 collective-permute-start.14
  73.6 0.0 collective-permute-done.11
  73.6 0.7 collective-permute-start.15
  74.3 0.9 convert_add_fusion
  75.2 0.7 multiply_convert_fusion
  75.9 0.0 collective-permute-done.16
  75.9 1.2 slice_bitcast_fusion
  77.1 3.4 %place.5 = (bf16[16,127,2048]{2,1,0:T(8,128)(2,1)}, f32[16,16,2048]{2,1,0:T(8,128)}) custom-call(s32[64]{0:T(128)} %source.15, f32[4,16,2048]{2,1,0:T(8,128)} %get-tuple-element.34.gates, f32[16,2048]{1,0:T(8,128)} %decay.15, bf16[144,2048]{1,0:T(8,128)(2,1)} %get-tuple-element.67.refs_0_, ...), custom_call_target="tpu_custom_call", output_to_operand_aliasing={{0}: (5, {}), {1}: (6, {})} | custom-call | tf_op jit(solution)/shard_map/place/pallas_call | solution.py:508
  80.5 30.6 %collective-permute-done.15.refs_0_ = bf16[144,2048]{1,0:T(8,128)(2,1)S(1)} collective-permute-done((bf16[144,2048]{1,0:T(8,128)(2,1)S(1)}, bf16[144,2048]{1,0:T(8,128)(2,1)S(1)}, u32[]{:S(2)}, u32[]{:S(2)}) %collective-permute-start.15) | collective-permute-done | bytes 589856 | tf_op jit(solution)/shard_map/ppermute | solution.py:34
  111.1 0.8 copy-done.3
  111.9 3.2 %place.6 = (bf16[16,127,2048]{2,1,0:T(8,128)(2,1)}, f32[16,16,2048]{2,1,0:T(8,128)}) custom-call(s32[64]{0:T(128)} %source.15, f32[4,16,2048]{2,1,0:T(8,128)} %get-tuple-element.34.gates, f32[16,2048]{1,0:T(8,128)} %decay.15, bf16[144,2048]{1,0:T(8,128)(2,1)} %copy-done.3, ...), custom_call_target="tpu_custom_call", output_to_operand_aliasing={{0}: (4, {}), {1}: (5, {})} | custom-call | tf_op jit(solution)/shard_map/place/pallas_call | solution.py:508
  115.1 0.0 collective-permute-done.14.refs_0_
  115.1 0.0 copy-start.2
  115.1 0.8 copy-done.2
  116.0 3.2 %place.7 = (bf16[16,127,2048]{2,1,0:T(8,128)(2,1)}, f32[16,16,2048]{2,1,0:T(8,128)}) custom-call(s32[64]{0:T(128)} %source.15, f32[4,16,2048]{2,1,0:T(8,128)} %get-tuple-element.34.gates, f32[16,2048]{1,0:T(8,128)} %decay.15, bf16[144,2048]{1,0:T(8,128)(2,1)} %copy-done.2, ...), custom_call_target="tpu_custom_call", output_to_operand_aliasing={{0}: (4, {}), {1}: (5, {})} | custom-call | tf_op jit(solution)/shard_map/place/pallas_call | solution.py:508
  119.1 0.0 collective-permute-done.13.refs_0_
  119.1 0.0 copy-start.1
  119.2 0.8 copy-done.1
  120.0 3.2 %place.8 = (bf16[16,127,2048]{2,1,0:T(8,128)(2,1)}, f32[16,16,2048]{2,1,0:T(8,128)}) custom-call(s32[64]{0:T(128)} %source.15, f32[4,16,2048]{2,1,0:T(8,128)} %get-tuple-element.34.gates, f32[16,2048]{1,0:T(8,128)} %decay.15, bf16[144,2048]{1,0:T(8,128)(2,1)} %copy-done.1, ...), custom_call_target="tpu_custom_call", output_to_operand_aliasing={{0}: (4, {}), {1}: (5, {})} | custom-call | tf_op jit(solution)/shard_map/place/pallas_call | solution.py:508
  123.1 0.0 collective-permute-done.12.refs_0_
  123.2 0.0 copy-start
  123.2 0.8 copy-done
  124.0 3.2 %place.9 = (bf16[16,127,2048]{2,1,0:T(8,128)(2,1)}, f32[16,16,2048]{2,1,0:T(8,128)}) custom-call(s32[64]{0:T(128)} %source.15, f32[4,16,2048]{2,1,0:T(8,128)} %get-tuple-element.34.gates, f32[16,2048]{1,0:T(8,128)} %decay.15, bf16[144,2048]{1,0:T(8,128)(2,1)} %copy-done, ...), custom_call_target="tpu_custom_call", output_to_operand_aliasing={{0}: (4, {}), {1}: (5, {})} | custom-call | tf_op jit(solution)/shard_map/place/pallas_call | solution.py:508
  127.2 11.4 %copy.27 = bf16[16,127,2048]{2,0,1:T(8,128)(2,1)} copy(bf16[16,127,2048]{2,1,0:T(8,128)(2,1)} %get-tuple-element.64) | data formatting | bytes 16646144
  (24 shorter events, 0.0 us)
Async XLA Ops:
  19.5 13.8 %collective-permute-start = (f32[8,2048]{1,0:T(8,128)}, f32[8,2048]{1,0:T(8,128)S(1)}, u32[]{:S(2)}, u32[]{:S(2)}) collective-permute-start(f32[8,2048]{1,0:T(8,128)} %get-tuple-element.35), channel_id=1, source_target_pairs={{0,4},{4,0},{8,12},{12,8},{1,5},{5,1},{9,13},{13,9},{2,6},{6,2},{1... | collective-permute-start | bytes 196616 | tf_op jit(solution)/shard_map/ppermute | solution.py:34
  20.0 13.3 %collective-permute-start.1 = (f32[8,2048]{1,0:T(8,128)}, f32[8,2048]{1,0:T(8,128)S(1)}, u32[]{:S(2)}, u32[]{:S(2)}) collective-permute-start(f32[8,2048]{1,0:T(8,128)} %get-tuple-element.36), channel_id=1, source_target_pairs={{0,8},{4,12},{8,0},{12,4},{1,9},{5,13},{9,1},{13,5},{2,10},{6,14},... | collective-permute-start | bytes 196616 | tf_op jit(solution)/shard_map/ppermute | solution.py:34
  22.6 16.3 %copy-start.13 = (bf16[2,144,2048]{2,1,0:T(8,128)(2,1)S(1)}, bf16[2,144,2048]{2,1,0:T(8,128)(2,1)}, u32[]{:S(2)}) copy-start(bf16[2,144,2048]{2,1,0:T(8,128)(2,1)} %get-tuple-element.50) | copy-start | bytes 3538948
  22.6 10.8 %collective-permute-start.2 = (f32[8,2048]{1,0:T(8,128)}, f32[8,2048]{1,0:T(8,128)S(1)}, u32[]{:S(2)}, u32[]{:S(2)}) collective-permute-start(f32[8,2048]{1,0:T(8,128)} %get-tuple-element.37), channel_id=1, source_target_pairs={{0,12},{4,8},{8,4},{12,0},{1,13},{5,9},{9,5},{13,1},{2,14},{6,10},... | collective-permute-start | bytes 196616 | tf_op jit(solution)/shard_map/ppermute | solution.py:34
  33.3 0.6 copy-start.7
  33.3 0.6 copy-start.8
  33.3 0.6 copy-start.9
  37.2 8.7 %collective-permute-start.4 = (bf16[64,2048]{1,0:T(8,128)(2,1)}, bf16[64,2048]{1,0:T(8,128)(2,1)S(1)}, u32[]{:S(2)}, u32[]{:S(2)}) collective-permute-start(bf16[64,2048]{1,0:T(8,128)(2,1)} %mix.1.refs_0_), channel_id=1, source_target_pairs={{0,8},{4,12},{8,0},{12,4},{1,9},{5,13},{9,1},{13,5},{2,10},{6,14},... | collective-permute-start | bytes 786440 | tf_op jit(solution)/shard_map/ppermute | solution.py:34
  38.9 17.1 %copy-start.14 = (bf16[144,2048]{1,0:T(8,128)(2,1)S(1)}, bf16[144,2048]{1,0:T(8,128)(2,1)}, u32[]{:S(2)}) copy-start(bf16[144,2048]{1,0:T(8,128)(2,1)} %get-tuple-element.46) | copy-start | bytes 1769476
  38.9 29.3 %copy-start.18 = (s32[16]{0:T(128)S(1)}, s32[16]{0:T(128)}, u32[]{:S(2)}) copy-start(s32[16]{0:T(128)} %param.17) | copy-start | bytes 196
  38.9 30.7 %copy-start.15 = (bf16[144,2048]{1,0:T(8,128)(2,1)S(1)}, bf16[144,2048]{1,0:T(8,128)(2,1)}, u32[]{:S(2)}) copy-start(bf16[144,2048]{1,0:T(8,128)(2,1)} %get-tuple-element.47) | copy-start | bytes 1769476
  38.9 33.4 %copy-start.16 = (bf16[144,2048]{1,0:T(8,128)(2,1)S(1)}, bf16[144,2048]{1,0:T(8,128)(2,1)}, u32[]{:S(2)}) copy-start(bf16[144,2048]{1,0:T(8,128)(2,1)} %get-tuple-element.48) | copy-start | bytes 1769476
  38.9 34.7 %copy-start.17 = (bf16[144,2048]{1,0:T(8,128)(2,1)S(1)}, bf16[144,2048]{1,0:T(8,128)(2,1)}, u32[]{:S(2)}) copy-start(bf16[144,2048]{1,0:T(8,128)(2,1)} %get-tuple-element.49) | copy-start | bytes 1769476
  38.9 37.0 %collective-permute-start.16 = (bf16[2,144,2048]{2,1,0:T(8,128)(2,1)S(1)}, bf16[2,144,2048]{2,1,0:T(8,128)(2,1)S(1)}, u32[]{:S(2)}, u32[]{:S(2)}) collective-permute-start(bf16[2,144,2048]{2,1,0:T(8,128)(2,1)S(1)} %copy-done.13), channel_id=1, source_target_pairs={{0,4},{4,0},{8,12},{12,8},{1,5},{5,1},{9,13},{13,9},{2,6},{6,2},{1... | collective-permute-start | bytes 3538952 | tf_op jit(solution)/shard_map/ppermute | solution.py:34
  39.0 6.9 %collective-permute-start.3 = (bf16[64,2048]{1,0:T(8,128)(2,1)}, bf16[64,2048]{1,0:T(8,128)(2,1)S(1)}, u32[]{:S(2)}, u32[]{:S(2)}) collective-permute-start(bf16[64,2048]{1,0:T(8,128)(2,1)} %mix.1.refs_0_), channel_id=1, source_target_pairs={{0,4},{4,0},{8,12},{12,8},{1,5},{5,1},{9,13},{13,9},{2,6},{6,2},{1... | collective-permute-start | bytes 786440 | tf_op jit(solution)/shard_map/ppermute | solution.py:34
  45.9 1.5 %copy-start.4 = (bf16[64,2048]{1,0:T(8,128)(2,1)}, bf16[64,2048]{1,0:T(8,128)(2,1)S(1)}, u32[]{:S(2)}) copy-start(bf16[64,2048]{1,0:T(8,128)(2,1)S(1)} %collective-permute-done.4.refs_2_) | copy-start | bytes 786436
  45.9 1.5 %collective-permute-start.5 = (bf16[64,2048]{1,0:T(8,128)(2,1)S(1)}, bf16[64,2048]{1,0:T(8,128)(2,1)S(1)}, u32[]{:S(2)}, u32[]{:S(2)}) collective-permute-start(bf16[64,2048]{1,0:T(8,128)(2,1)S(1)} %collective-permute-done.4.refs_2_), channel_id=1, source_target_pairs={{0,4},{4,0},{8,12},{12,8},{1,5},{5,1},{9,13},{13,9},{2,6},{6,2},{1... | collective-permute-start | bytes 786440 | tf_op jit(solution)/shard_map/ppermute | solution.py:34
  45.9 1.5 %copy-start.5 = (bf16[64,2048]{1,0:T(8,128)(2,1)}, bf16[64,2048]{1,0:T(8,128)(2,1)S(1)}, u32[]{:S(2)}) copy-start(bf16[64,2048]{1,0:T(8,128)(2,1)S(1)} %collective-permute-done.3.refs_1_) | copy-start | bytes 786436
  47.4 0.7 copy-start.6
  54.0 3.7 %collective-permute-start.6 = (bf16[32,1024]{1,0:T(8,128)(2,1)}, bf16[32,1024]{1,0:T(8,128)(2,1)S(1)}, u32[]{:S(2)}, u32[]{:S(2)}) collective-permute-start(bf16[32,1024]{1,0:T(8,128)(2,1)} %get-tuple-element.39), channel_id=1, source_target_pairs={{0,4},{4,0},{8,12},{12,8},{1,5},{5,1},{9,13},{13,9},{2,6},{6,2},{1... | collective-permute-start | bytes 196616 | tf_op jit(solution)/shard_map/ppermute | solution.py:34
  54.2 4.6 %collective-permute-start.7 = (bf16[32,1024]{1,0:T(8,128)(2,1)}, bf16[32,1024]{1,0:T(8,128)(2,1)S(1)}, u32[]{:S(2)}, u32[]{:S(2)}) collective-permute-start(bf16[32,1024]{1,0:T(8,128)(2,1)} %get-tuple-element.40), channel_id=1, source_target_pairs={{0,8},{4,12},{8,0},{12,4},{1,9},{5,13},{9,1},{13,5},{2,10},{6,14},... | collective-permute-start | bytes 196616 | tf_op jit(solution)/shard_map/ppermute | solution.py:34
  55.9 4.4 %collective-permute-start.8 = (bf16[32,1024]{1,0:T(8,128)(2,1)}, bf16[32,1024]{1,0:T(8,128)(2,1)S(1)}, u32[]{:S(2)}, u32[]{:S(2)}) collective-permute-start(bf16[32,1024]{1,0:T(8,128)(2,1)} %get-tuple-element.41), channel_id=1, source_target_pairs={{0,12},{4,8},{8,4},{12,0},{1,13},{5,9},{9,5},{13,1},{2,14},{6,10},... | collective-permute-start | bytes 196616 | tf_op jit(solution)/shard_map/ppermute | solution.py:34
  55.9 67.2 %collective-permute-start.12 = (bf16[144,2048]{1,0:T(8,128)(2,1)S(1)}, bf16[144,2048]{1,0:T(8,128)(2,1)S(1)}, u32[]{:S(2)}, u32[]{:S(2)}) collective-permute-start(bf16[144,2048]{1,0:T(8,128)(2,1)S(1)} %copy-done.14), channel_id=1, source_target_pairs={{0,12},{4,8},{8,4},{12,0},{1,13},{5,9},{9,5},{13,1},{2,14},{6,10},... | collective-permute-start | bytes 1769480 | tf_op jit(solution)/shard_map/ppermute | solution.py:34
  57.7 2.6 %copy-start.10 = (bf16[32,1024]{1,0:T(8,128)(2,1)}, bf16[32,1024]{1,0:T(8,128)(2,1)S(1)}, u32[]{:S(2)}) copy-start(bf16[32,1024]{1,0:T(8,128)(2,1)S(1)} %collective-permute-done.6.refs_1_) | copy-start | bytes 196612
  58.8 1.6 %copy-start.11 = (bf16[32,1024]{1,0:T(8,128)(2,1)}, bf16[32,1024]{1,0:T(8,128)(2,1)S(1)}, u32[]{:S(2)}) copy-start(bf16[32,1024]{1,0:T(8,128)(2,1)S(1)} %collective-permute-done.7.refs_2_) | copy-start | bytes 196612
  60.4 0.6 copy-start.12
  62.8 6.8 %collective-permute-start.9 = (bf16[32,1024]{1,0:T(8,128)(2,1)}, bf16[32,1024]{1,0:T(8,128)(2,1)S(1)}, u32[]{:S(2)}, u32[]{:S(2)}) collective-permute-start(bf16[32,1024]{1,0:T(8,128)(2,1)} %get-tuple-element.43), channel_id=1, source_target_pairs={{0,1},{1,2},{2,3},{3,0},{4,5},{5,6},{6,7},{7,4},{8,9},{9,10},{10,1... | collective-permute-start | bytes 196616 | tf_op jit(solution)/shard_map/ppermute | solution.py:502
  64.3 8.0 %collective-permute-start.10 = (bf16[32,1024]{1,0:T(8,128)(2,1)}, bf16[32,1024]{1,0:T(8,128)(2,1)S(1)}, u32[]{:S(2)}, u32[]{:S(2)}) collective-permute-start(bf16[32,1024]{1,0:T(8,128)(2,1)} %get-tuple-element.44), channel_id=1, source_target_pairs={{0,2},{1,3},{2,0},{3,1},{4,6},{5,7},{6,4},{7,5},{8,10},{9,11},{10,... | collective-permute-start | bytes 196616 | tf_op jit(solution)/shard_map/ppermute | solution.py:502
  66.8 6.8 %collective-permute-start.11 = (bf16[32,1024]{1,0:T(8,128)(2,1)}, bf16[32,1024]{1,0:T(8,128)(2,1)S(1)}, u32[]{:S(2)}, u32[]{:S(2)}) collective-permute-start(bf16[32,1024]{1,0:T(8,128)(2,1)} %get-tuple-element.45), channel_id=1, source_target_pairs={{0,3},{1,0},{2,1},{3,2},{4,7},{5,4},{6,5},{7,6},{8,11},{9,8},{10,9... | collective-permute-start | bytes 196616 | tf_op jit(solution)/shard_map/ppermute | solution.py:502
  69.5 49.6 %collective-permute-start.13 = (bf16[144,2048]{1,0:T(8,128)(2,1)S(1)}, bf16[144,2048]{1,0:T(8,128)(2,1)S(1)}, u32[]{:S(2)}, u32[]{:S(2)}) collective-permute-start(bf16[144,2048]{1,0:T(8,128)(2,1)S(1)} %copy-done.15), channel_id=1, source_target_pairs={{0,12},{4,8},{8,4},{12,0},{1,13},{5,9},{9,5},{13,1},{2,14},{6,10},... | collective-permute-start | bytes 1769480 | tf_op jit(solution)/shard_map/ppermute | solution.py:34
  72.3 42.8 %collective-permute-start.14 = (bf16[144,2048]{1,0:T(8,128)(2,1)S(1)}, bf16[144,2048]{1,0:T(8,128)(2,1)S(1)}, u32[]{:S(2)}, u32[]{:S(2)}) collective-permute-start(bf16[144,2048]{1,0:T(8,128)(2,1)S(1)} %copy-done.16), channel_id=1, source_target_pairs={{0,8},{4,12},{8,0},{12,4},{1,9},{5,13},{9,1},{13,5},{2,10},{6,14},... | collective-permute-start | bytes 1769480 | tf_op jit(solution)/shard_map/ppermute | solution.py:34
  73.6 37.5 %collective-permute-start.15 = (bf16[144,2048]{1,0:T(8,128)(2,1)S(1)}, bf16[144,2048]{1,0:T(8,128)(2,1)S(1)}, u32[]{:S(2)}, u32[]{:S(2)}) collective-permute-start(bf16[144,2048]{1,0:T(8,128)(2,1)S(1)} %copy-done.17), channel_id=1, source_target_pairs={{0,8},{4,12},{8,0},{12,4},{1,9},{5,13},{9,1},{13,5},{2,10},{6,14},... | collective-permute-start | bytes 1769480 | tf_op jit(solution)/shard_map/ppermute | solution.py:34
  111.1 0.8 copy-start.3
  115.1 0.8 copy-start.2
  119.1 0.8 copy-start.1
  123.2 0.8 copy-start

commit v2 on v0

v2 whole, which is shorter than its diff:
```python
import functools

import jax
import jax.numpy as jnp
from jax import lax
from jax.experimental import pallas as pl
from jax.experimental.pallas import tpu as pltpu
from jax.sharding import PartitionSpec as P

CAP = 2
BF = jnp.bfloat16
F32 = jnp.float32
ANY = pl.BlockSpec(memory_space=pl.ANY)
SM = pl.BlockSpec(memory_space=pltpu.SMEM)
VM = pl.BlockSpec(memory_space=pltpu.VMEM)
VLIM = 48 << 20
TB = 16
TINY = pl.CostEstimate(flops=1, transcendentals=0, bytes_accessed=1)


def lane_chunk(width):
    for size in (256, 128):
        if width % size == 0:
            return size
    return width


def wide_chunk(width):
    return 1024 if width % 1024 == 0 else lane_chunk(width)


def links(engines):
    chips = engines // 2
    return [(k, f) for k in range(chips) for f in (0, 1)]


def send(x, engines, k, f):
    chips = engines // 2
    pairs = [(e, ((e // 2 + k) % chips) * 2 + ((e % 2) ^ f)) for e in range(engines)]
    return lax.ppermute(x, "engine", pairs)


def to_engine(me, k, f, engines):
    chips = engines // 2
    return lax.rem(lax.div(me, 2) + k, chips) * 2 + lax.rem(me + f, 2)


def relation_of(me, owner, engines):
    chips = engines // 2
    k = lax.rem(lax.div(me, 2) + chips - lax.div(owner, 2), chips)
    return 2 * k + lax.rem(owner + me, 2)


def departures(engines, rows, source, leave, me):
    for rel, (k, f) in enumerate(links(engines)):
        if rel == 0:
            continue
        there = to_engine(me, k, f, engines)
        for j in range(CAP):
            leave[rel * (CAP + 1) + j] = 0

        found = 0
        for i in range(rows):
            old = source[there * rows + i]
            leave[rel * (CAP + 1) + jnp.minimum(found, CAP)] = lax.rem(old, rows)
            found = found + jnp.where(lax.div(old, rows) == me, 1, 0)


def send_selector(rels, rows, leave, pick):
    height, depth = pick.shape
    at = lax.broadcasted_iota(jnp.int32, (height, 1), 0)
    group = at // (TB * CAP)
    tap = (at % (TB * CAP)) // CAP
    place = at % CAP
    row = jnp.zeros((height, 1), jnp.int32)
    for i, rel in enumerate(rels):
        for j in range(CAP):
            row = jnp.where((group == i) & (place == j), leave[rel * (CAP + 1) + j], row)
    want = tap * rows + row
    pick[...] = (lax.broadcasted_iota(jnp.int32, (height, depth), 1) == want).astype(F32).astype(BF)


def sent_taps(b, tail_len):
    return min(TB, tail_len - 2 - b * TB)


def early_body(engines, rows, blocks, source, tails, *refs):
    far = list(range(2, engines))
    msgs = refs[: len(far)]
    tbuf, pick, leave, tsem = refs[len(far) :]
    tail_len, _, width = tails.shape
    chunk = wide_chunk(width)
    me = lax.axis_index("engine")

    def fetch(n):
        return pltpu.make_async_copy(tails.at[pl.ds(blocks[n] * TB, TB)], tbuf.at[pl.ds(n * TB, TB)], tsem.at[n])

    for n in range(len(blocks)):
        fetch(n).start()
    departures(engines, rows, source, leave, me)
    send_selector(far, rows, leave, pick)
    for n in range(len(blocks)):
        fetch(n).wait()

        for c in range(0, width, chunk):
            cols = pl.ds(c, chunk)
            old = tbuf[n * TB : (n + 1) * TB, :, cols].reshape(TB * rows, chunk)
            rowsel = jnp.dot(pick[...], old, preferred_element_type=F32).astype(BF)
            for i in range(len(far)):
                msgs[i][n * TB * CAP : (n + 1) * TB * CAP, cols] = rowsel[i * TB * CAP : (i + 1) * TB * CAP]


def lead_body(engines, rows, source, tails, states, filt, decay, resid, _, *refs):
    others = engines - 1
    parts = refs[0]
    small = refs[1 : 1 + others]
    fbuf, tbuf, sbuf, leave, tsem, ssem = refs[1 + others :]
    tail_len, _, width = tails.shape
    modes = states.shape[1]
    taps = filt.shape[0]
    chunk = wide_chunk(width)
    me = lax.axis_index("engine")
    total = pl.cdiv(tail_len, TB)

    def fetch(b):
        size = min(TB, tail_len - b * TB)
        return pltpu.make_async_copy(
            tails.at[pl.ds(b * TB, size)], tbuf.at[pl.ds(b * TB, size)], tsem.at[b]
        )

    for b in range(total):
        fetch(b).start()
    load_states = pltpu.make_async_copy(states, sbuf, ssem)
    load_states.start()
    departures(engines, rows, source, leave, me)
    for c in range(0, width, chunk):
        fbuf[0:taps, pl.ds(c, chunk)] = filt[:, pl.ds(c, chunk)].astype(F32)
        fbuf[taps : taps + 8, pl.ds(c, chunk)] = jnp.zeros((8, chunk), F32)
    for b in range(total):
        fetch(b).wait()
        size = min(TB, tail_len - b * TB)

        for c in range(0, width, chunk):
            cols = pl.ds(c, chunk)
            if b == 0:
                first = jnp.zeros((rows, chunk), F32)
                second = jnp.zeros((rows, chunk), F32)
            else:
                first = parts[0, :, cols]
                second = parts[1, :, cols]
            for i in range(size):
                t = tbuf[b * TB + i, :, cols].astype(F32)
                first += t * fbuf[b * TB + i + 1 : b * TB + i + 2, cols]
                second += t * fbuf[b * TB + i + 2 : b * TB + i + 3, cols]
            parts[0, :, cols] = first
            parts[1, :, cols] = second
    load_states.wait()

    def modal(r, carry):
        s = sbuf[r]
        a = resid[...] * (decay[...] * s)
        parts[2, pl.ds(r, 1), :] = jnp.sum(a, axis=0, keepdims=True)
        parts[3, pl.ds(r, 1), :] = jnp.sum(a * decay[...], axis=0, keepdims=True)
        return carry

    lax.fori_loop(0, rows, modal, 0)
    for rel in range(1, engines):
        for j in range(CAP):
            one = pl.ds(leave[rel * (CAP + 1) + j], 1)
            for i in range(4):
                small[rel - 1][4 * j + i : 4 * j + i + 1, :] = parts[i, one, :].astype(small[rel - 1].dtype)


def pack_body(engines, rows, chunks, state_chunk, source, tails, states, _, *refs):
    far = list(range(2, engines))
    near = refs[0]
    msgs = refs[1 : 1 + len(far) * len(chunks)]
    spread, tbuf, sbuf, pick, leave, slots, found, tsem, ssem = refs[1 + len(msgs) :]
    tail_len, _, width = tails.shape
    modes = states.shape[1]
    chunk = wide_chunk(width)
    me = lax.axis_index("engine")
    total = pl.cdiv(tail_len - 2, TB)
    others = engines - 1

    def fetch(b):
        n = sent_taps(b, tail_len)
        return pltpu.make_async_copy(tails.at[pl.ds(b * TB, n)], tbuf.at[pl.ds(b * TB, n)], tsem.at[b])

    def fetch_state(rel, j):
        slot = (rel - 1) * CAP + j
        return pltpu.make_async_copy(states.at[leave[rel * (CAP + 1) + j]], sbuf.at[slot], ssem.at[slot])

    for b in range(total):
        fetch(b).start()
    departures(engines, rows, source, leave, me)
    for rel in range(1, engines):
        for j in range(CAP):
            fetch_state(rel, j).start()
    send_selector([1] + far, rows, leave, pick)
    arrivals(engines, rows, source, slots, found, me)
    height, depth = spread.shape
    at = lax.broadcasted_iota(jnp.int32, (height, 1), 0)
    tap = at // rows
    new_row = at % rows
    want = jnp.zeros((height, 1), jnp.int32)
    for r in range(rows):
        old = source[me * rows + r]
        want = jnp.where(new_row == r, tap * rows + old % rows, want)
    for rel in range(1, engines):
        for j in range(CAP):
            row = jnp.where(found[rel] > j, slots[rel * (CAP + 1) + j], -1)
            want = jnp.where(new_row == row, TB * rows + (rel - 1) * TB * CAP + CAP * tap + j, want)
    spread[...] = (lax.broadcasted_iota(jnp.int32, (height, depth), 1) == want).astype(F32).astype(BF)
    for b in range(total):
        fetch(b).wait()
        n = sent_taps(b, tail_len)
        home = [i for i, blocks in enumerate(chunks) if b in blocks]
        tall = pick.shape[0] if home else TB * CAP

        for c in range(0, width, chunk):
            cols = pl.ds(c, chunk)
            old = tbuf[b * TB : b * TB + n, :, cols].reshape(n * rows, chunk)
            rowsel = jnp.dot(pick[0:tall, 0 : n * rows], old, preferred_element_type=F32).astype(BF)
            near[b * TB * CAP : (b + 1) * TB * CAP, cols] = rowsel[0 : TB * CAP]
            if home:
                base = (b - chunks[home[0]][0]) * TB * CAP
                for i in range(len(far)):
                    msgs[home[0] * len(far) + i][base : base + TB * CAP, cols] = rowsel[
                        (i + 1) * TB * CAP : (i + 2) * TB * CAP
                    ]
    for rel in range(1, engines):
        for j in range(CAP):
            fetch_state(rel, j).wait()
            slot = (rel - 1) * CAP + j
            if rel == 1:
                base = total * TB * CAP
                near[base + j * modes : base + (j + 1) * modes, :] = sbuf[slot].astype(BF)
            else:
                base = len(chunks[state_chunk]) * TB * CAP
                msgs[state_chunk * len(far) + rel - 2][base + j * modes : base + (j + 1) * modes, :] = sbuf[
                    slot
                ].astype(BF)


def arrivals(engines, rows, source, slots, found, me):
    for rel in range(engines):
        found[rel] = 0
    for r in range(rows):
        rel = relation_of(me, lax.div(source[me * rows + r], rows), engines)
        at = found[rel]
        slots[rel * (CAP + 1) + jnp.minimum(at, CAP)] = r
        found[rel] = at + 1


def mix_body(engines, rows, source, parts_in, mr, li, filt, decay, resid, *refs):
    got = refs[: engines - 1]
    y, gates, parts, slots, found = refs[-5:]
    width = y.shape[1]
    chunk = lane_chunk(width)
    me = lax.axis_index("engine")
    arrivals(engines, rows, source, slots, found, me)

    def stay(r, carry):
        old = source[me * rows + r] % rows
        for i in range(4):
            parts[i, pl.ds(r, 1), :] = parts_in[i, pl.ds(old, 1), :]
        return carry

    lax.fori_loop(0, rows, stay, 0)
    for rel in range(1, engines):
        for j in range(CAP):

            @pl.when(found[rel] > j)
            def _():
                one = pl.ds(slots[rel * (CAP + 1) + j], 1)
                for i in range(4):
                    parts[i, one, :] = got[rel - 1][4 * j + i : 4 * j + i + 1, :].astype(F32)

    for c in range(0, width, chunk):
        cols = pl.ds(c, chunk)
        f = filt[0:16, cols].astype(F32)
        d = decay[:, cols]
        w = resid[:, cols]
        r0 = jnp.sum(w, axis=0, keepdims=True)
        r1 = jnp.sum(w * d, axis=0, keepdims=True)
        z = []
        for n, qkv in enumerate((mr, mr, li, li)):
            gate = (qkv[n % 2, 1, :, cols].astype(F32) * qkv[n % 2, 2, :, cols].astype(F32)).astype(BF)
            gates[n, :, cols] = gate
            z.append(gate.astype(F32))
        conv0 = f[0:1] * z[0] + parts[0, :, cols]
        conv1 = f[0:1] * z[1] + f[1:2] * z[0] + parts[1, :, cols]
        y[0:rows, cols] = (mr[0, 0, :, cols].astype(F32) * conv0).astype(BF)
        y[rows : 2 * rows, cols] = (mr[1, 0, :, cols].astype(F32) * conv1).astype(BF)
        modal0 = parts[2, :, cols] + z[2] * r0
        modal1 = parts[3, :, cols] + z[2] * r1 + z[3] * r0
        y[2 * rows : 3 * rows, cols] = (li[0, 0, :, cols].astype(F32) * modal0).astype(BF)
        y[3 * rows : 4 * rows, cols] = (li[1, 0, :, cols].astype(F32) * modal1).astype(BF)


def project_body(engines, rows, slots_here, depth, *refs):
    ys = refs[:engines]
    mr_w, li_w = refs[engines : engines + 2]
    outs = refs[-2 - engines : -2]
    x, acc = refs[-2:]
    two = 2 * rows
    width = ys[0].shape[1]
    pw = mr_w.shape[2]
    step = pl.program_id(0)

    @pl.when(step == 0)
    def _():
        for rel in range(engines):
            for b in range(width // depth):
                x[b, 0, rel * two : (rel + 1) * two, :] = ys[rel][0:two, b * depth : (b + 1) * depth]
                x[b, 1, rel * two : (rel + 1) * two, :] = ys[rel][two : 2 * two, b * depth : (b + 1) * depth]
        acc[...] = jnp.zeros_like(acc)

    for g in range(slots_here):
        cols = slice(g * pw, (g + 1) * pw)
        acc[:, cols] += jnp.dot(x[step, 0], mr_w[g], preferred_element_type=F32) + jnp.dot(
            x[step, 1], li_w[g], preferred_element_type=F32
        )

    @pl.when(step == pl.num_programs(0) - 1)
    def _():
        for rel in range(engines):
            outs[rel][...] = acc[rel * two : (rel + 1) * two, :].astype(BF)


def sort_body(engines, chans, slots_here, slot_of, *refs):
    got = refs[:engines]
    outs = refs[-1 - chans : -1]
    tiles = refs[-1]
    pw = tiles.shape[2]
    me = lax.axis_index("engine")
    here = lax.axis_index("chan")
    per_chan = slot_of.shape[0] // chans
    for rel in range(engines):
        for g in range(slots_here):
            tiles[rel * slots_here + g] = got[rel][:, g * pw : (g + 1) * pw]
    for d in range(chans):
        there = (here + d) % chans
        for h in range(per_chan):
            slot = slot_of[there * per_chan + h]
            rel = relation_of(me, slot // slots_here, engines)
            outs[d][:, h * pw : (h + 1) * pw] = tiles[rel * slots_here + slot % slots_here]


def place_body(engines, rows, blocks, spread, gates, tails, near, *refs):
    others = engines - 1
    msgs = refs[: others - 1]
    new_tails = refs[others]
    tbuf, mbuf, obuf, isem, osem = refs[others + 1 :]
    tail_len, _, width = tails.shape
    chunk = lane_chunk(width)
    first = blocks[0] == 0
    lead = 2 if first else 0

    def fetch(n):
        b = blocks[n]
        taps = sent_taps(b, tail_len)
        copies = [pltpu.make_async_copy(tails.at[pl.ds(b * TB, taps)], tbuf.at[n, pl.ds(0, taps)], isem.at[n, 0])]
        for rel in range(1, engines):
            ref = near if rel == 1 else msgs[rel - 2]
            base = (b if rel == 1 else n) * TB * CAP
            copies.append(
                pltpu.make_async_copy(ref.at[pl.ds(base, TB * CAP)], mbuf.at[n, rel - 1], isem.at[n, rel])
            )
        return copies

    def store(n):
        b = blocks[n]
        taps = sent_taps(b, tail_len)
        extra = lead if n == 0 else 0
        return pltpu.make_async_copy(
            obuf.at[n, pl.ds(2 - extra, taps + extra)], new_tails.at[pl.ds(b * TB + 2 - extra, taps + extra)], osem.at[n]
        )

    for n in range(len(blocks)):
        for copy in fetch(n):
            copy.start()
    for n, b in enumerate(blocks):
        for copy in fetch(n):
            copy.wait()
        taps = sent_taps(b, tail_len)
        if first and n == 0:
            obuf[0, 0] = gates[1]
            obuf[0, 1] = gates[0]

        for c in range(0, width, chunk):
            cols = pl.ds(c, chunk)
            old = tbuf[n, 0:taps, :, cols].reshape(taps * rows, chunk)
            got = jnp.concatenate([mbuf[n, i, :, cols] for i in range(others)], axis=0)
            top = taps * rows
            new = jnp.dot(spread[0:top, 0:top], old, preferred_element_type=F32) + jnp.dot(
                spread[0:top, TB * rows :], got, preferred_element_type=F32
            )
            obuf[n, 2 : 2 + taps, :, cols] = new.astype(BF).reshape(taps, rows, chunk)
        store(n).start()
    for n in range(len(blocks)):
        store(n).wait()


def modal_body(engines, rows, bases, source, states, gates, decay, near, *refs):
    others = engines - 1
    msgs = refs[: others - 1]
    new_states = refs[others - 1]
    sbuf, mbuf, slots, found, isem, msem, osem = refs[others:]
    modes = states.shape[1]
    width = states.shape[2]
    chunk = lane_chunk(width)
    me = lax.axis_index("engine")

    def fetch(r):
        return pltpu.make_async_copy(states.at[source[me * rows + r] % rows], sbuf.at[r], isem.at[r])

    def arrive(rel):
        ref = near if rel == 1 else msgs[rel - 2]
        return pltpu.make_async_copy(ref.at[pl.ds(bases[min(rel, 2) - 1], CAP * modes)], mbuf.at[rel - 1], msem.at[rel - 1])

    def store(r):
        return pltpu.make_async_copy(sbuf.at[r], new_states.at[r], osem.at[r])

    for r in range(rows):
        fetch(r).start()
    for rel in range(1, engines):
        arrive(rel).start()
    arrivals(engines, rows, source, slots, found, me)
    for r in range(rows):
        fetch(r).wait()
    for rel in range(1, engines):
        arrive(rel).wait()
        for j in range(CAP):

            @pl.when(found[rel] > j)
            def _():
                sbuf[slots[rel * (CAP + 1) + j]] = mbuf[rel - 1, j * modes : (j + 1) * modes].astype(F32)

    for r in range(rows):
        for c in range(0, width, chunk):
            cols = pl.ds(c, chunk)
            d = decay[:, cols]
            z0 = gates[2, r : r + 1, cols].astype(F32)
            z1 = gates[3, r : r + 1, cols].astype(F32)
            sbuf[r, :, cols] = d * (d * sbuf[r, :, cols] + z0) + z1
        store(r).start()
    for r in range(rows):
        store(r).wait()


def split(total):
    cuts = [0, 3 * total // 8, 5 * total // 8, total]
    return [list(range(a, b)) for a, b in zip(cuts, cuts[1:]) if a < b]


def body(mr_qkv, li_qkv, conv_tails, modal_states, source, remaining, mr_filter, li_decay, li_residue, mr_panels,
         li_panels, panel_slot):
    engines = lax.axis_size("engine")
    chans = lax.axis_size("chan")
    rows, tail_len, width = conv_tails.shape
    modes = modal_states.shape[1]
    taps = mr_filter.shape[0]
    slots_here, _, pw = mr_panels.shape
    others = engines - 1
    chips = engines // 2
    rels = links(engines)
    far = list(range(2, engines))
    sds = jax.ShapeDtypeStruct
    dma = pltpu.SemaphoreType.DMA
    params = pltpu.CompilerParams(vmem_limit_bytes=VLIM)
    tails = jnp.transpose(conv_tails, (1, 0, 2))
    blocks = pl.cdiv(tail_len - 2, TB)
    chunks = split(blocks)
    state_chunk = len(chunks) - 2
    table = pltpu.SMEM((engines * (CAP + 1),), jnp.int32)
    tally = pltpu.SMEM((engines,), jnp.int32)

    def msg_rows(i):
        return len(chunks[i]) * TB * CAP + (CAP * modes if i == state_chunk else 0)

    msgs = {}
    msgs[0] = pl.pallas_call(
        functools.partial(early_body, engines, rows, chunks[0]),
        in_specs=[SM, ANY],
        out_specs=[VM] * len(far),
        out_shape=[sds((msg_rows(0), width), BF)] * len(far),
        scratch_shapes=[
            pltpu.VMEM((len(chunks[0]) * TB, rows, width), BF),
            pltpu.VMEM((len(far) * TB * CAP, TB * rows), BF),
            table,
            dma((len(chunks[0]),)),
        ],
        compiler_params=params,
        name="early",
    )(source, tails)
    got = {}

    def launch(i, token=None):
        arrays = list(msgs[i])
        if token is not None:
            arrays, token = lax.optimization_barrier((arrays, token))
        got[i] = [send(a, engines, *rels[rel]) for a, rel in zip(arrays, far)]
        return token

    launch(0)
    lead = pl.pallas_call(
        functools.partial(lead_body, engines, rows),
        in_specs=[SM, ANY, ANY, VM, VM, VM, ANY],
        out_specs=[VM] * (1 + others),
        out_shape=[sds((4, rows, width), F32)] + [sds((4 * CAP, width), BF)] * others,
        scratch_shapes=[
            pltpu.VMEM((taps + 8, width), F32),
            pltpu.VMEM((tail_len, rows, width), BF),
            pltpu.VMEM((rows, modes, width), F32),
            table,
            dma((pl.cdiv(tail_len, TB),)),
            dma(()),
        ],
        compiler_params=params,
        name="lead",
    )(source, tails, modal_states, mr_filter, li_decay, li_residue, msgs[0][0])
    parts = lead[0]
    small = lead[1 : 1 + others]
    parts_got = [send(small[rel - 1], engines, *rels[rel]) for rel in range(1, engines)]

    later = chunks[1:]
    packed = pl.pallas_call(
        functools.partial(pack_body, engines, rows, later, state_chunk - 1),
        in_specs=[SM, ANY, ANY, ANY],
        out_specs=[VM] * (2 + len(far) * len(later)),
        out_shape=[sds((blocks * TB * CAP + CAP * modes, width), BF)]
        + [sds((msg_rows(i), width), BF) for i in range(1, len(chunks)) for _ in far]
        + [sds((TB * rows, TB * rows + others * TB * CAP), BF)],
        scratch_shapes=[
            pltpu.VMEM((tail_len, rows, width), BF),
            pltpu.VMEM((others * CAP, modes, width), F32),
            pltpu.VMEM((others * TB * CAP, TB * rows), BF),
            table,
            table,
            tally,
            dma((blocks,)),
            dma((others * CAP,)),
        ],
        compiler_params=params,
        name="pack",
    )(source, tails, modal_states, small[0])
    near_msg = packed[0]
    spread = packed[-1]
    for i in range(1, len(chunks)):
        msgs[i] = packed[1 + (i - 1) * len(far) : 1 + i * len(far)]

    y, gates = pl.pallas_call(
        functools.partial(mix_body, engines, rows),
        in_specs=[SM] + [VM] * (6 + others) + [ANY] * (1 + len(far)),
        out_specs=[VM, VM],
        out_shape=[sds((4 * rows, width), BF), sds((4, rows, width), BF)],
        scratch_shapes=[pltpu.VMEM((4, rows, width), F32), table, tally],
        compiler_params=params,
        name="mix",
    )(source, parts, mr_qkv, li_qkv, mr_filter, li_decay, li_residue, *parts_got, spread, *got[0])

    near_msg, y = lax.optimization_barrier((near_msg, y))
    near_got = send(near_msg, engines, 0, 1)
    same_core = [y] + [send(y, engines, k, 0) for k in range(1, chips)]
    ys = []
    for k in range(chips):
        ys += [same_core[k], send(same_core[k], engines, 0, 1)]
    ys[1] = launch(1, ys[1])

    def place(i, new_tails):
        return pl.pallas_call(
            functools.partial(place_body, engines, rows, chunks[i]),
            in_specs=[VM, VM] + [ANY] * (2 + len(far) + 1),
            out_specs=ANY,
            out_shape=sds((tail_len, rows, width), BF),
            input_output_aliases={} if i == 0 else {4 + len(far): 0},
            scratch_shapes=[
                pltpu.VMEM((len(chunks[i]), TB, rows, width), BF),
                pltpu.VMEM((len(chunks[i]), others, TB * CAP, width), BF),
                pltpu.VMEM((len(chunks[i]), TB + 2, rows, width), BF),
                dma((len(chunks[i]), engines)),
                dma((len(chunks[i]),)),
            ],
            compiler_params=params,
            name="place",
 cost_estimate=TINY,
        )(spread, gates, tails, near_got, *got[i], spread if i == 0 else new_tails)

    new_tails = place(0, None)
    depth = 512
    outs = pl.pallas_call(
        functools.partial(project_body, engines, rows, slots_here, depth),
        grid=(width // depth,),
        in_specs=[pl.BlockSpec((4 * rows, width), lambda i: (0, 0))] * engines
        + [pl.BlockSpec((slots_here, depth, pw), lambda i: (0, i, 0))] * 2
        + [ANY],
        out_specs=[pl.BlockSpec((2 * rows, slots_here * pw), lambda i: (0, 0))] * engines,
        out_shape=[sds((2 * rows, slots_here * pw), BF)] * engines,
        scratch_shapes=[
            pltpu.VMEM((width // depth, 2, engines * 2 * rows, depth), BF),
            pltpu.VMEM((engines * 2 * rows, slots_here * pw), F32),
        ],
        compiler_params=params,
        name="project",
    )(*ys, mr_panels, li_panels, new_tails)

    back = [outs[0]]
    for k, f in rels[1:]:
        back.append(send(outs[2 * ((chips - k) % chips) + f], engines, k, f))
    back[1] = launch(2, back[1])

    per_chan = panel_slot.shape[0] // chans
    blocks_out = pl.pallas_call(
        functools.partial(sort_body, engines, chans, slots_here),
        in_specs=[SM] + [VM] * engines + [ANY] * len(far),
        out_specs=[VM] * chans,
        out_shape=[sds((2 * rows, per_chan * pw), BF)] * chans,
        scratch_shapes=[pltpu.VMEM((engines * slots_here, 2 * rows, pw), BF)],
        compiler_params=params,
        name="sort",
 cost_estimate=TINY,
    )(panel_slot, *back, *got[1])
    total = blocks_out[0].astype(F32)
    for d in range(1, chans):
        total = total + lax.ppermute(blocks_out[d], "chan", [(c, (c + d) % chans) for c in range(chans)]).astype(F32)
    steps_ids = jnp.arange(2, dtype=jnp.int32)
    active = (remaining[None, :] > steps_ids[:, None]).astype(F32)
    total, got[2] = lax.optimization_barrier((total, got[2]))
    mixed = (total.reshape(2, rows, per_chan * pw) * active[:, :, None]).astype(BF)

    new_tails = place(1, new_tails)
    new_tails = place(2, new_tails)
    new_states = pl.pallas_call(
        functools.partial(
            modal_body, engines, rows, [blocks * TB * CAP, len(chunks[state_chunk]) * TB * CAP]
        ),
        in_specs=[SM, ANY, VM, VM] + [ANY] * others,
        out_specs=ANY,
        out_shape=sds((rows, modes, width), F32),
        scratch_shapes=[
            pltpu.VMEM((rows, modes, width), F32),
            pltpu.VMEM((others, CAP * modes, width), BF),
            table,
            tally,
            dma((rows,)),
            dma((others,)),
            dma((rows,)),
        ],
        compiler_params=params,
        name="modal",
 cost_estimate=TINY,
    )(source, modal_states, gates, li_decay, near_got, *got[state_chunk])
    return (mixed, jnp.transpose(new_tails, (1, 0, 2)), new_states)


def solution(mesh):
    return jax.shard_map(
        body,
        mesh=mesh,
        in_specs=(
            P(None, None, ("group", "engine"), "chan"),
            P(None, None, ("group", "engine"), "chan"),
            P(("group", "engine"), None, "chan"),
            P(("group", "engine"), None, "chan"),
            P("group"),
            P(("group", "engine")),
            P(None, "chan"),
            P(None, "chan"),
            P(None, "chan"),
            P("engine", "chan", None),
            P("engine", "chan", None),
            P(),
        ),
        out_specs=(
            P(None, ("group", "engine"), "chan"),
            P(("group", "engine"), None, "chan"),
            P(("group", "engine"), None, "chan"),
        ),
        check_vma=False,
    )
```

time: 316 us -> 85 us (0.27)
  waiting for transfers between devices: 155 us -> 24 us
  local copies, waits for them, and re-layouts: 81 us -> 0.84 us
  Pallas kernels: 0 us -> 39.7 us
  other arithmetic: 36 us -> 0.75 us
  matrix products: 20.1 us -> 0 us
  between operations: 13.9 us -> 1.04 us
  starting transfers between devices: 9.4 us -> 18 us
    all_gather x2 -> x0, waiting for transfers between devices: 88.8 us -> none  [the longest x1 88.8 us: body(): mr_piece = lax.all_gather(mr_panels, 'engine', axis=0, tiled=True)]
    all_to_all x2 -> x0, waiting for transfers between devices: 58.1 us -> none  [the longest x1 58.1 us: body(): lax.all_to_all(send_tails, 'engine', split_axis=0, concat_axis=0, tiled=T...]
    gather x8 -> x0, local copies, waits for them, and re-layouts: 45.5 us -> none  [the longest x1 18.6 us: body(): conv_tails[src_local]]
    pallas_call x0 -> x10, Pallas kernels: none -> 39.7 us  [the longest x3 12.9 us: place(): pl.pallas_call(functools.partial(place_body, engines, rows, chunks[i]), i...]
    ppermute x0 -> x19, waiting for transfers between devices: none -> 24 us  [the longest x16 24 us: send(): return lax.ppermute(x, 'engine', pairs)]
    dot_general x2 -> x0, matrix products: 20.1 us -> none  [the longest x1 11.4 us: body(): jnp.einsum('srd,gdc->srgc', li_rows, li_piece, preferred_element_type=jnp...]
    ppermute x0 -> x19, starting transfers between devices: none -> 18 us  [the longest x16 13.1 us: send(): return lax.ppermute(x, 'engine', pairs)]
    reshape x4 -> x0, local copies, waits for them, and re-layouts: 16.4 us -> none  [the longest x2 16.3 us: body(): conv_tails[send_index.reshape(-1)].reshape(engines, CAP, tail_len, width)]
  transfers between devices with their start and end apart: 5 -> 19, of which waited for: 3 -> 7; matrix products, arithmetic and copies ran while one was open for 39% -> 0% of each run, Pallas kernels for 0% -> 36%
where the time goes in v2:
time: 85 us; the launch traced here: 84.4 us
  Pallas kernels  39.7 us (47%)
  waiting for transfers between devices  24 us (28%)
  starting transfers between devices  18 us (21%)
  between operations  1.04 us (1%)
    ppermute x16, waiting for transfers between devices, send(): return lax.ppermute(x, 'engine', pairs)  24 us
    ppermute x16, starting transfers between devices, send(): return lax.ppermute(x, 'engine', pairs)  13.1 us
    pallas_call x3, Pallas kernels, place(): pl.pallas_call(functools.partial(place_body, engines, rows, chunks[i]), i...  12.9 us
    pallas_call x1, Pallas kernels, body(): pl.pallas_call(functools.partial(lead_body, engines, rows), in_specs=[SM,...  6.97 us
    pallas_call x1, Pallas kernels, body(): pl.pallas_call(functools.partial(modal_body, engines, rows, [blocks * TB...  5.83 us
    ppermute x3, starting transfers between devices, body(): lax.ppermute(blocks_out[d], 'chan', [(c, (c + d) % chans) for c in range(...  4.89 us
    pallas_call x1, Pallas kernels, body(): pl.pallas_call(functools.partial(pack_body, engines, rows, later, state_c...  4.88 us
    pallas_call x1, Pallas kernels, body(): pl.pallas_call(functools.partial(project_body, engines, rows, slots_here,...  4.28 us
  transfers between devices with their start and end apart: 19, of which 7 were waited for; matrix products, arithmetic and copies ran while one was open for 0% of the time, Pallas kernels for 36%

profile of v2, /device:TPU:0, one launch (start us, length us, event | category | flops | bytes accessed | tf_op | source)
XLA Modules:
  0.0 84.4 jit_solution(4027146523676258423)
XLA Ops:
  0.6 0.0 copy-start
  0.6 0.0 copy-start.2
  0.7 0.0 copy-start.3
  0.7 0.0 copy-start.4
  0.7 0.0 copy-start.7
  0.7 0.8 copy-done.7
  1.5 2.7 %early.1 = (bf16[96,2048]{1,0:T(8,128)(2,1)S(1)}, bf16[96,2048]{1,0:T(8,128)(2,1)S(1)}) custom-call(s32[64]{0:T(128)S(1)} %copy-done.7, bf16[127,16,2048]{2,1,0:T(8,128)(2,1)} %bitcast.3), custom_call_target="tpu_custom_call" | custom-call | tf_op jit(solution)/shard_map/early/pallas_call | solution.py:484
  4.2 3.0 %collective-permute-start.3 = (bf16[96,2048]{1,0:T(8,128)(2,1)S(1)}, bf16[96,2048]{1,0:T(8,128)(2,1)S(1)}, u32[]{:S(2)}, u32[]{:S(2)}) collective-permute-start(bf16[96,2048]{1,0:T(8,128)(2,1)S(1)} %get-tuple-element.36._), channel_id=1, source_target_pairs={{0,8},{4,12},{8,0},{12,4},{1,9},{5,13},{9,1},{13,5},{2,10},{6,14},... | collective-permute-start | bytes 1179656 | tf_op jit(solution)/shard_map/ppermute | solution.py:40
  7.2 0.0 collective-permute-start.4
  7.2 0.0 copy-done
  7.3 0.0 copy-done.2
  7.3 0.0 copy-done.3
  7.3 0.0 copy-done.4
  7.3 7.0 %lead.1 = (f32[4,16,2048]{2,1,0:T(8,128)S(1)}, bf16[8,2048]{1,0:T(8,128)(2,1)S(1)}, bf16[8,2048]{1,0:T(8,128)(2,1)S(1)}, bf16[8,2048]{1,0:T(8,128)(2,1)S(1)}) custom-call(s32[64]{0:T(128)S(1)} %copy-done.7, bf16[127,16,2048]{2,1,0:T(8,128)(2,1)} %bitcast.4, f32[16,16,2048]{2,1,0:T(8,128)S(1)} %copy-done, bf16[128,2048]{1,0:T(8,128)(2,1)S(1)} %copy-done.2, ...), custom_call_target="tpu_custom_call" | custom-call | tf_op jit(solution)/shard_map/lead/pallas_call | solution.py:508
  14.3 0.3 collective-permute-start
  14.5 1.9 %collective-permute-start.1 = (bf16[8,2048]{1,0:T(8,128)(2,1)S(1)}, bf16[8,2048]{1,0:T(8,128)(2,1)S(1)}, u32[]{:S(2)}, u32[]{:S(2)}) collective-permute-start(bf16[8,2048]{1,0:T(8,128)(2,1)S(1)} %get-tuple-element.40), channel_id=1, source_target_pairs={{0,8},{4,12},{8,0},{12,4},{1,9},{5,13},{9,1},{13,5},{2,10},{6,14},... | collective-permute-start | bytes 98312 | tf_op jit(solution)/shard_map/ppermute | solution.py:40
  16.4 0.0 collective-permute-start.2
  16.4 0.0 copy-done.8
  16.5 4.9 %pack.1 = (bf16[288,2048]{1,0:T(8,128)(2,1)S(1)}, bf16[96,2048]{1,0:T(8,128)(2,1)S(1)}, bf16[96,2048]{1,0:T(8,128)(2,1)S(1)}, bf16[96,2048]{1,0:T(8,128)(2,1)S(1...) custom-call(s32[64]{0:T(128)S(1)} %copy-done.8, bf16[127,16,2048]{2,1,0:T(8,128)(2,1)} %bitcast.5, ...), custom_call_target="tpu_custom_call" | custom-call | tf_op jit(solution)/shard_map/pack/pallas_call | solution.py:529
  21.3 0.0 collective-permute-done.refs_0_
  21.4 4.5 %collective-permute-done.1.refs_1_ = bf16[8,2048]{1,0:T(8,128)(2,1)S(1)} collective-permute-done((bf16[8,2048]{1,0:T(8,128)(2,1)S(1)}, bf16[8,2048]{1,0:T(8,128)(2,1)S(1)}, u32[]{:S(2)}, u32[]{:S(2)}) %collective-permute-start.1) | collective-permute-done | bytes 32800 | tf_op jit(solution)/shard_map/ppermute | solution.py:40
  25.8 0.0 collective-permute-done.2.refs_2_
  25.8 0.0 collective-permute-done.3.refs_4_.refs_0_
  25.8 0.0 collective-permute-done.4.refs_5_.refs_1_
  25.9 0.0 copy-done.5
  25.9 1.5 %mix.1 = (bf16[64,2048]{1,0:T(8,128)(2,1)S(1)}, bf16[4,16,2048]{2,1,0:T(8,128)(2,1)S(1)}) custom-call(s32[64]{0:T(128)S(1)} %copy-done.8, f32[4,16,2048]{2,1,0:T(8,128)S(1)} %get-tuple-element.39.parts_in, bf16[2,3,16,2048]{3,2,1,0:T(8,128)(2,1)S(1)} %copy-done.5, bf16[2,3,16,2048]{3,2,1,0:T(8,128)(2,1)S(1)} %copy-done.6, bf16[128,2048]{1,0:T(8,128)(2,1)S(1)} %copy-done.2, ...), custom_call_target="tpu_custom_call" | custom-call | tf_op jit(solution)/shard_map/mix/pallas_call | solution.py:554
  27.3 0.2 collective-permute-start.8
  27.6 0.3 collective-permute-start.5
  27.9 1.7 %collective-permute-start.6 = (bf16[64,2048]{1,0:T(8,128)(2,1)S(1)}, bf16[64,2048]{1,0:T(8,128)(2,1)S(1)}, u32[]{:S(2)}, u32[]{:S(2)}) collective-permute-start(bf16[64,2048]{1,0:T(8,128)(2,1)S(1)} %get-tuple-element.45.refs_0_), channel_id=1, source_target_pairs={{0,8},{4,12},{8,0},{12,4},{1,9},{5,13},{9,1},{13,5},{2,10},{6,14},... | collective-permute-start | bytes 786440 | tf_op jit(solution)/shard_map/ppermute | solution.py:40
  29.6 1.0 %collective-permute-done.5.refs_1_ = bf16[64,2048]{1,0:T(8,128)(2,1)S(1)} collective-permute-done((bf16[64,2048]{1,0:T(8,128)(2,1)S(1)}, bf16[64,2048]{1,0:T(8,128)(2,1)S(1)}, u32[]{:S(2)}, u32[]{:S(2)}) %collective-permute-start.5) | collective-permute-done | bytes 262176 | tf_op jit(solution)/shard_map/ppermute | solution.py:40
  30.6 1.7 %collective-permute-start.12 = (bf16[96,2048]{1,0:T(8,128)(2,1)S(1)}, bf16[96,2048]{1,0:T(8,128)(2,1)S(1)}, u32[]{:S(2)}, u32[]{:S(2)}) collective-permute-start(bf16[96,2048]{1,0:T(8,128)(2,1)S(1)} %get-tuple-element.58), channel_id=1, source_target_pairs={{0,8},{4,12},{8,0},{12,4},{1,9},{5,13},{9,1},{13,5},{2,10},{6,14},... | collective-permute-start | bytes 1179656 | tf_op jit(solution)/shard_map/ppermute | solution.py:40
  32.4 0.0 collective-permute-start.13
  32.4 4.7 %collective-permute-done.6.refs_2_ = bf16[64,2048]{1,0:T(8,128)(2,1)S(1)} collective-permute-done((bf16[64,2048]{1,0:T(8,128)(2,1)S(1)}, bf16[64,2048]{1,0:T(8,128)(2,1)S(1)}, u32[]{:S(2)}, u32[]{:S(2)}) %collective-permute-start.6) | collective-permute-done | bytes 262176 | tf_op jit(solution)/shard_map/ppermute | solution.py:40
  37.1 0.0 collective-permute-start.7
  37.1 0.0 collective-permute-done.8.near
  37.1 4.7 %place.3.refs_6_.refs_2_ = bf16[127,16,2048]{2,1,0:T(8,128)(2,1)} custom-call(bf16[256,352]{1,0:T(8,128)(2,1)S(1)} %get-tuple-element.42.refs_3_.spread.refs_2_, bf16[4,16,2048]{2,1,0:T(8,128)(2,1)S(1)} %get-tuple-element.49.gates, bf16[127,16,2048]{2,1,0:T(8,128)(2,1)} %bitcast.6, bf16[288,2048]{1,0:T(8,128)(2,1)S(1)} %collective-permute-done.8.near, ...), custom_call_target="tpu_custom_call" | custom-call | flops 1 | bytes 1 | tf_op jit(solution)/shard_map/place/pallas_call | solution.py:573
  41.8 0.0 copy-start.9
  41.8 0.0 copy-start.10
  41.8 0.0 collective-permute-done.7.refs_3_
  41.8 4.3 %project.1 = (bf16[32,1024]{1,0:T(8,128)(2,1)S(1)}, bf16[32,1024]{1,0:T(8,128)(2,1)S(1)}, bf16[32,1024]{1,0:T(8,128)(2,1)S(1)}, bf16[32,1024]{1,0:T(8,128)(2,1)S(1)}) custom-call(bf16[64,2048]{1,0:T(8,128)(2,1)S(1)} %get-tuple-element.45.refs_0_, bf16[64,2048]{1,0:T(8,128)(2,1)S(1)} %collective-permute-done.5.refs_1_, ...), custom_call_target="tpu_custom_call" | custom-call | tf_op jit(solution)/shard_map/project/pallas_call | solution.py:593
  46.1 0.5 collective-permute-start.9
  46.7 1.8 %collective-permute-start.10 = (bf16[32,1024]{1,0:T(8,128)(2,1)S(1)}, bf16[32,1024]{1,0:T(8,128)(2,1)S(1)}, u32[]{:S(2)}, u32[]{:S(2)}) collective-permute-start(bf16[32,1024]{1,0:T(8,128)(2,1)S(1)} %get-tuple-element.56), channel_id=1, source_target_pairs={{0,8},{4,12},{8,0},{12,4},{1,9},{5,13},{9,1},{13,5},{2,10},{6,14},... | collective-permute-start | bytes 196616 | tf_op jit(solution)/shard_map/ppermute | solution.py:40
  48.4 0.0 collective-permute-start.11
  48.4 0.0 collective-permute-done.9.refs_1_
  48.4 0.0 collective-permute-done.12.refs_4_.refs_0_
  48.4 4.7 %collective-permute-done.13.refs_5_.refs_1_ = bf16[96,2048]{1,0:T(8,128)(2,1)S(1)} collective-permute-done((bf16[96,2048]{1,0:T(8,128)(2,1)S(1)}, bf16[96,2048]{1,0:T(8,128)(2,1)S(1)}, u32[]{:S(2)}, u32[]{:S(2)}) %collective-permute-start.13) | collective-permute-done | bytes 393248 | tf_op jit(solution)/shard_map/ppermute | solution.py:40
  53.2 2.1 %collective-permute-done.10.refs_2_ = bf16[32,1024]{1,0:T(8,128)(2,1)S(1)} collective-permute-done((bf16[32,1024]{1,0:T(8,128)(2,1)S(1)}, bf16[32,1024]{1,0:T(8,128)(2,1)S(1)}, u32[]{:S(2)}, u32[]{:S(2)}) %collective-permute-start.10) | collective-permute-done | bytes 65568 | tf_op jit(solution)/shard_map/ppermute | solution.py:40
  55.2 0.0 collective-permute-done.11.refs_3_
  55.2 0.7 sort.1
  55.9 3.9 %collective-permute-start.16 = (bf16[32,1024]{1,0:T(8,128)(2,1)S(1)}, bf16[32,1024]{1,0:T(8,128)(2,1)S(1)}, u32[]{:S(2)}, u32[]{:S(2)}) collective-permute-start(bf16[32,1024]{1,0:T(8,128)(2,1)S(1)} %get-tuple-element.63), channel_id=1, source_target_pairs={{0,3},{1,0},{2,1},{3,2},{4,7},{5,4},{6,5},{7,6},{8,11},{9,8},{10,9... | collective-permute-start | bytes 196616 | tf_op jit(solution)/shard_map/ppermute | solution.py:627
  59.8 0.0 collective-permute-start.15
  59.8 1.0 %collective-permute-start.14 = (bf16[32,1024]{1,0:T(8,128)(2,1)S(1)}, bf16[32,1024]{1,0:T(8,128)(2,1)S(1)}, u32[]{:S(2)}, u32[]{:S(2)}) collective-permute-start(bf16[32,1024]{1,0:T(8,128)(2,1)S(1)} %get-tuple-element.61), channel_id=1, source_target_pairs={{0,1},{1,2},{2,3},{3,0},{4,5},{5,6},{6,7},{7,4},{8,9},{9,10},{10,1... | collective-permute-start | bytes 196616 | tf_op jit(solution)/shard_map/ppermute | solution.py:627
  60.8 1.5 %collective-permute-start.17 = (bf16[96,2048]{1,0:T(8,128)(2,1)S(1)}, bf16[96,2048]{1,0:T(8,128)(2,1)S(1)}, u32[]{:S(2)}, u32[]{:S(2)}) collective-permute-start(bf16[96,2048]{1,0:T(8,128)(2,1)S(1)} %get-tuple-element.64), channel_id=1, source_target_pairs={{0,8},{4,12},{8,0},{12,4},{1,9},{5,13},{9,1},{13,5},{2,10},{6,14},... | collective-permute-start | bytes 1179656 | tf_op jit(solution)/shard_map/ppermute | solution.py:40
  62.3 0.0 collective-permute-start.18
  62.3 0.0 copy-done.10
  62.3 3.7 %place.4.refs_2_ = bf16[127,16,2048]{2,1,0:T(8,128)(2,1)} custom-call(bf16[256,352]{1,0:T(8,128)(2,1)S(1)} %get-tuple-element.42.refs_3_.spread.refs_2_, bf16[4,16,2048]{2,1,0:T(8,128)(2,1)S(1)} %get-tuple-element.49.gates, bf16[127,16,2048]{2,1,0:T(8,128)(2,1)} %bitcast.7, ...), custom_call_target="tpu_custom_call", output_to_operand_aliasing={{}: (6, {})} | custom-call | flops 1 | bytes 1 | tf_op jit(solution)/shard_map/place/pallas_call | solution.py:573
  66.0 5.8 %modal.1 = f32[16,16,2048]{2,1,0:T(8,128)} custom-call(s32[64]{0:T(128)S(1)} %copy-done.8, f32[16,16,2048]{2,1,0:T(8,128)S(1)} %copy-done, bf16[4,16,2048]{2,1,0:T(8,128)(2,1)S(1)} %get-tuple-element.49.gates, f32[16,2048]{1,0:T(8,128)S(1)} %copy-done.3, bf16[288,2048]{1,0:T(8,128)(2,1)S(1)} %collective-permute-done.8.near, ...), custom_call_target="tpu_custom_call" | custom-call | flops 1 | bytes 1 | tf_op jit(solution)/shard_map/modal/pallas_call | solution.py:635
  71.9 0.0 collective-permute-done.16
  71.9 0.0 collective-permute-done.15
  71.9 0.0 collective-permute-done.14
  71.9 0.9 %collective-permute-done.17.refs_0_ = bf16[96,2048]{1,0:T(8,128)(2,1)S(1)} collective-permute-done((bf16[96,2048]{1,0:T(8,128)(2,1)S(1)}, bf16[96,2048]{1,0:T(8,128)(2,1)S(1)}, u32[]{:S(2)}, u32[]{:S(2)}) %collective-permute-start.17) | collective-permute-done | bytes 393248 | tf_op jit(solution)/shard_map/ppermute | solution.py:40
  72.8 6.1 %collective-permute-done.18.refs_1_ = bf16[96,2048]{1,0:T(8,128)(2,1)S(1)} collective-permute-done((bf16[96,2048]{1,0:T(8,128)(2,1)S(1)}, bf16[96,2048]{1,0:T(8,128)(2,1)S(1)}, u32[]{:S(2)}, u32[]{:S(2)}) %collective-permute-start.18) | collective-permute-done | bytes 393248 | tf_op jit(solution)/shard_map/ppermute | solution.py:40
  79.0 0.7 multiply_convert_fusion
  79.7 4.5 %place.5 = bf16[127,16,2048]{2,1,0:T(8,128)(2,1)} custom-call(bf16[256,352]{1,0:T(8,128)(2,1)S(1)} %get-tuple-element.42.refs_3_.spread.refs_2_, bf16[4,16,2048]{2,1,0:T(8,128)(2,1)S(1)} %get-tuple-element.49.gates, bf16[127,16,2048]{2,1,0:T(8,128)(2,1)} %bitcast.8, ...), custom_call_target="tpu_custom_call", output_to_operand_aliasing={{}: (6, {})} | custom-call | flops 1 | bytes 1 | tf_op jit(solution)/shard_map/place/pallas_call | solution.py:573
  (9 shorter events, 0.1 us)
Async XLA Ops:
  0.6 6.6 %copy-start = (f32[16,16,2048]{2,1,0:T(8,128)S(1)}, f32[16,16,2048]{2,1,0:T(8,128)}, u32[]{:S(2)}) copy-start(f32[16,16,2048]{2,1,0:T(8,128)} %states.5) | copy-start | bytes 6291460
  0.6 6.6 %copy-start.2 = (bf16[128,2048]{1,0:T(8,128)(2,1)S(1)}, bf16[128,2048]{1,0:T(8,128)(2,1)}, u32[]{:S(2)}) copy-start(bf16[128,2048]{1,0:T(8,128)(2,1)} %filt.3) | copy-start | bytes 1572868
  0.7 6.6 %copy-start.3 = (f32[16,2048]{1,0:T(8,128)S(1)}, f32[16,2048]{1,0:T(8,128)}, u32[]{:S(2)}) copy-start(f32[16,2048]{1,0:T(8,128)} %decay.5) | copy-start | bytes 393220
  0.7 6.6 %copy-start.4 = (f32[16,2048]{1,0:T(8,128)S(1)}, f32[16,2048]{1,0:T(8,128)}, u32[]{:S(2)}) copy-start(f32[16,2048]{1,0:T(8,128)} %resid.3) | copy-start | bytes 393220
  0.7 0.8 copy-start.7
  4.2 21.6 %collective-permute-start.3 = (bf16[96,2048]{1,0:T(8,128)(2,1)S(1)}, bf16[96,2048]{1,0:T(8,128)(2,1)S(1)}, u32[]{:S(2)}, u32[]{:S(2)}) collective-permute-start(bf16[96,2048]{1,0:T(8,128)(2,1)S(1)} %get-tuple-element.36._), channel_id=1, source_target_pairs={{0,8},{4,12},{8,0},{12,4},{1,9},{5,13},{9,1},{13,5},{2,10},{6,14},... | collective-permute-start | bytes 1179656 | tf_op jit(solution)/shard_map/ppermute | solution.py:40
  7.2 9.2 %copy-start.8 = (s32[64]{0:T(128)S(1)}, s32[64]{0:T(128)}, u32[]{:S(2)}) copy-start(s32[64]{0:T(128)} %source.9) | copy-start | bytes 772
  7.2 18.6 %collective-permute-start.4 = (bf16[96,2048]{1,0:T(8,128)(2,1)S(1)}, bf16[96,2048]{1,0:T(8,128)(2,1)S(1)}, u32[]{:S(2)}, u32[]{:S(2)}) collective-permute-start(bf16[96,2048]{1,0:T(8,128)(2,1)S(1)} %get-tuple-element.43), channel_id=1, source_target_pairs={{0,12},{4,8},{8,4},{12,0},{1,13},{5,9},{9,5},{13,1},{2,14},{6,10},... | collective-permute-start | bytes 1179656 | tf_op jit(solution)/shard_map/ppermute | solution.py:40
  14.3 7.1 %collective-permute-start = (bf16[8,2048]{1,0:T(8,128)(2,1)S(1)}, bf16[8,2048]{1,0:T(8,128)(2,1)S(1)}, u32[]{:S(2)}, u32[]{:S(2)}) collective-permute-start(bf16[8,2048]{1,0:T(8,128)(2,1)S(1)} %get-tuple-element.37._), channel_id=1, source_target_pairs={{0,4},{4,0},{8,12},{12,8},{1,5},{5,1},{9,13},{13,9},{2,6},{6,2},{1... | collective-permute-start | bytes 98312 | tf_op jit(solution)/shard_map/ppermute | solution.py:40
  14.5 11.3 %collective-permute-start.1 = (bf16[8,2048]{1,0:T(8,128)(2,1)S(1)}, bf16[8,2048]{1,0:T(8,128)(2,1)S(1)}, u32[]{:S(2)}, u32[]{:S(2)}) collective-permute-start(bf16[8,2048]{1,0:T(8,128)(2,1)S(1)} %get-tuple-element.40), channel_id=1, source_target_pairs={{0,8},{4,12},{8,0},{12,4},{1,9},{5,13},{9,1},{13,5},{2,10},{6,14},... | collective-permute-start | bytes 98312 | tf_op jit(solution)/shard_map/ppermute | solution.py:40
  16.4 9.4 %copy-start.5 = (bf16[2,3,16,2048]{3,2,1,0:T(8,128)(2,1)S(1)}, bf16[2,3,16,2048]{3,2,1,0:T(8,128)(2,1)}, u32[]{:S(2)}) copy-start(bf16[2,3,16,2048]{3,2,1,0:T(8,128)(2,1)} %mr.1) | copy-start | bytes 1179652
  16.4 9.4 %copy-start.6 = (bf16[2,3,16,2048]{3,2,1,0:T(8,128)(2,1)S(1)}, bf16[2,3,16,2048]{3,2,1,0:T(8,128)(2,1)}, u32[]{:S(2)}) copy-start(bf16[2,3,16,2048]{3,2,1,0:T(8,128)(2,1)} %li.1) | copy-start | bytes 1179652
  16.4 9.4 %collective-permute-start.2 = (bf16[8,2048]{1,0:T(8,128)(2,1)S(1)}, bf16[8,2048]{1,0:T(8,128)(2,1)S(1)}, u32[]{:S(2)}, u32[]{:S(2)}) collective-permute-start(bf16[8,2048]{1,0:T(8,128)(2,1)S(1)} %get-tuple-element.41), channel_id=1, source_target_pairs={{0,12},{4,8},{8,4},{12,0},{1,13},{5,9},{9,5},{13,1},{2,14},{6,10},... | collective-permute-start | bytes 98312 | tf_op jit(solution)/shard_map/ppermute | solution.py:40
  27.3 9.7 %collective-permute-start.8 = (bf16[288,2048]{1,0:T(8,128)(2,1)S(1)}, bf16[288,2048]{1,0:T(8,128)(2,1)S(1)}, u32[]{:S(2)}, u32[]{:S(2)}) collective-permute-start(bf16[288,2048]{1,0:T(8,128)(2,1)S(1)} %get-tuple-element.50), channel_id=1, source_target_pairs={{0,4},{4,0},{8,12},{12,8},{1,5},{5,1},{9,13},{13,9},{2,6},{6,2},{1... | collective-permute-start | bytes 3538952 | tf_op jit(solution)/shard_map/ppermute | solution.py:40
  27.6 3.1 %collective-permute-start.5 = (bf16[64,2048]{1,0:T(8,128)(2,1)S(1)}, bf16[64,2048]{1,0:T(8,128)(2,1)S(1)}, u32[]{:S(2)}, u32[]{:S(2)}) collective-permute-start(bf16[64,2048]{1,0:T(8,128)(2,1)S(1)} %get-tuple-element.45.refs_0_), channel_id=1, source_target_pairs={{0,4},{4,0},{8,12},{12,8},{1,5},{5,1},{9,13},{13,9},{2,6},{6,2},{1... | collective-permute-start | bytes 786440 | tf_op jit(solution)/shard_map/ppermute | solution.py:40
  27.9 9.2 %collective-permute-start.6 = (bf16[64,2048]{1,0:T(8,128)(2,1)S(1)}, bf16[64,2048]{1,0:T(8,128)(2,1)S(1)}, u32[]{:S(2)}, u32[]{:S(2)}) collective-permute-start(bf16[64,2048]{1,0:T(8,128)(2,1)S(1)} %get-tuple-element.45.refs_0_), channel_id=1, source_target_pairs={{0,8},{4,12},{8,0},{12,4},{1,9},{5,13},{9,1},{13,5},{2,10},{6,14},... | collective-permute-start | bytes 786440 | tf_op jit(solution)/shard_map/ppermute | solution.py:40
  30.6 17.8 %collective-permute-start.12 = (bf16[96,2048]{1,0:T(8,128)(2,1)S(1)}, bf16[96,2048]{1,0:T(8,128)(2,1)S(1)}, u32[]{:S(2)}, u32[]{:S(2)}) collective-permute-start(bf16[96,2048]{1,0:T(8,128)(2,1)S(1)} %get-tuple-element.58), channel_id=1, source_target_pairs={{0,8},{4,12},{8,0},{12,4},{1,9},{5,13},{9,1},{13,5},{2,10},{6,14},... | collective-permute-start | bytes 1179656 | tf_op jit(solution)/shard_map/ppermute | solution.py:40
  32.4 20.8 %collective-permute-start.13 = (bf16[96,2048]{1,0:T(8,128)(2,1)S(1)}, bf16[96,2048]{1,0:T(8,128)(2,1)S(1)}, u32[]{:S(2)}, u32[]{:S(2)}) collective-permute-start(bf16[96,2048]{1,0:T(8,128)(2,1)S(1)} %get-tuple-element.59), channel_id=1, source_target_pairs={{0,12},{4,8},{8,4},{12,0},{1,13},{5,9},{9,5},{13,1},{2,14},{6,10},... | collective-permute-start | bytes 1179656 | tf_op jit(solution)/shard_map/ppermute | solution.py:40
  37.1 4.8 %collective-permute-start.7 = (bf16[64,2048]{1,0:T(8,128)(2,1)S(1)}, bf16[64,2048]{1,0:T(8,128)(2,1)S(1)}, u32[]{:S(2)}, u32[]{:S(2)}) collective-permute-start(bf16[64,2048]{1,0:T(8,128)(2,1)S(1)} %collective-permute-done.6.refs_2_), channel_id=1, source_target_pairs={{0,4},{4,0},{8,12},{12,8},{1,5},{5,1},{9,13},{13,9},{2,6},{6,2},{1... | collective-permute-start | bytes 786440 | tf_op jit(solution)/shard_map/ppermute | solution.py:40
  37.1 4.8 %copy-start.1 = (bf16[2,2048,512]{2,1,0:T(8,128)(2,1)S(1)}, bf16[2,2048,512]{2,1,0:T(8,128)(2,1)}, u32[]{:S(2)}) copy-start(bf16[2,2048,512]{2,1,0:T(8,128)(2,1)} %refs_4_.1) | copy-start | bytes 12582916
  41.8 13.4 %copy-start.9 = (s32[8]{0:T(128)S(1)}, s32[8]{0:T(128)}, u32[]{:S(2)}) copy-start(s32[8]{0:T(128)} %slot_of.1) | copy-start | bytes 100
  41.8 20.5 %copy-start.10 = (s32[16]{0:T(128)S(1)}, s32[16]{0:T(128)}, u32[]{:S(2)}) copy-start(s32[16]{0:T(128)} %param.17) | copy-start | bytes 196
  46.1 2.3 %collective-permute-start.9 = (bf16[32,1024]{1,0:T(8,128)(2,1)S(1)}, bf16[32,1024]{1,0:T(8,128)(2,1)S(1)}, u32[]{:S(2)}, u32[]{:S(2)}) collective-permute-start(bf16[32,1024]{1,0:T(8,128)(2,1)S(1)} %get-tuple-element.54), channel_id=1, source_target_pairs={{0,4},{4,0},{8,12},{12,8},{1,5},{5,1},{9,13},{13,9},{2,6},{6,2},{1... | collective-permute-start | bytes 196616 | tf_op jit(solution)/shard_map/ppermute | solution.py:40
  46.7 8.6 %collective-permute-start.10 = (bf16[32,1024]{1,0:T(8,128)(2,1)S(1)}, bf16[32,1024]{1,0:T(8,128)(2,1)S(1)}, u32[]{:S(2)}, u32[]{:S(2)}) collective-permute-start(bf16[32,1024]{1,0:T(8,128)(2,1)S(1)} %get-tuple-element.56), channel_id=1, source_target_pairs={{0,8},{4,12},{8,0},{12,4},{1,9},{5,13},{9,1},{13,5},{2,10},{6,14},... | collective-permute-start | bytes 196616 | tf_op jit(solution)/shard_map/ppermute | solution.py:40
  48.4 6.8 %collective-permute-start.11 = (bf16[32,1024]{1,0:T(8,128)(2,1)S(1)}, bf16[32,1024]{1,0:T(8,128)(2,1)S(1)}, u32[]{:S(2)}, u32[]{:S(2)}) collective-permute-start(bf16[32,1024]{1,0:T(8,128)(2,1)S(1)} %get-tuple-element.57), channel_id=1, source_target_pairs={{0,12},{4,8},{8,4},{12,0},{1,13},{5,9},{9,5},{13,1},{2,14},{6,10},... | collective-permute-start | bytes 196616 | tf_op jit(solution)/shard_map/ppermute | solution.py:40
  55.9 15.9 %collective-permute-start.16 = (bf16[32,1024]{1,0:T(8,128)(2,1)S(1)}, bf16[32,1024]{1,0:T(8,128)(2,1)S(1)}, u32[]{:S(2)}, u32[]{:S(2)}) collective-permute-start(bf16[32,1024]{1,0:T(8,128)(2,1)S(1)} %get-tuple-element.63), channel_id=1, source_target_pairs={{0,3},{1,0},{2,1},{3,2},{4,7},{5,4},{6,5},{7,6},{8,11},{9,8},{10,9... | collective-permute-start | bytes 196616 | tf_op jit(solution)/shard_map/ppermute | solution.py:627
  59.8 12.1 %collective-permute-start.15 = (bf16[32,1024]{1,0:T(8,128)(2,1)S(1)}, bf16[32,1024]{1,0:T(8,128)(2,1)S(1)}, u32[]{:S(2)}, u32[]{:S(2)}) collective-permute-start(bf16[32,1024]{1,0:T(8,128)(2,1)S(1)} %get-tuple-element.62), channel_id=1, source_target_pairs={{0,2},{1,3},{2,0},{3,1},{4,6},{5,7},{6,4},{7,5},{8,10},{9,11},{10,... | collective-permute-start | bytes 196616 | tf_op jit(solution)/shard_map/ppermute | solution.py:627
  59.8 12.1 %collective-permute-start.14 = (bf16[32,1024]{1,0:T(8,128)(2,1)S(1)}, bf16[32,1024]{1,0:T(8,128)(2,1)S(1)}, u32[]{:S(2)}, u32[]{:S(2)}) collective-permute-start(bf16[32,1024]{1,0:T(8,128)(2,1)S(1)} %get-tuple-element.61), channel_id=1, source_target_pairs={{0,1},{1,2},{2,3},{3,0},{4,5},{5,6},{6,7},{7,4},{8,9},{9,10},{10,1... | collective-permute-start | bytes 196616 | tf_op jit(solution)/shard_map/ppermute | solution.py:627
  60.8 12.0 %collective-permute-start.17 = (bf16[96,2048]{1,0:T(8,128)(2,1)S(1)}, bf16[96,2048]{1,0:T(8,128)(2,1)S(1)}, u32[]{:S(2)}, u32[]{:S(2)}) collective-permute-start(bf16[96,2048]{1,0:T(8,128)(2,1)S(1)} %get-tuple-element.64), channel_id=1, source_target_pairs={{0,8},{4,12},{8,0},{12,4},{1,9},{5,13},{9,1},{13,5},{2,10},{6,14},... | collective-permute-start | bytes 1179656 | tf_op jit(solution)/shard_map/ppermute | solution.py:40
  62.3 16.6 %collective-permute-start.18 = (bf16[96,2048]{1,0:T(8,128)(2,1)S(1)}, bf16[96,2048]{1,0:T(8,128)(2,1)S(1)}, u32[]{:S(2)}, u32[]{:S(2)}) collective-permute-start(bf16[96,2048]{1,0:T(8,128)(2,1)S(1)} %get-tuple-element.65), channel_id=1, source_target_pairs={{0,12},{4,8},{8,4},{12,0},{1,13},{5,9},{9,5},{13,1},{2,14},{6,10},... | collective-permute-start | bytes 1179656 | tf_op jit(solution)/shard_map/ppermute | solution.py:40

commit v3 on v2

--- a/solution.py
+++ b/solution.py
@@ -166,18 +166,19 @@
     lax.fori_loop(0, rows, modal, 0)
     for rel in range(1, engines):
         for j in range(CAP):
-            one = pl.ds(leave[rel * (CAP + 1) + j], 1)
+            old = leave[rel * (CAP + 1) + j]
             for i in range(4):
-                small[rel - 1][4 * j + i : 4 * j + i + 1, :] = parts[i, one, :].astype(small[rel - 1].dtype)
-
-
-def pack_body(engines, rows, chunks, state_chunk, source, tails, states, _, *refs):
+                small[rel - 1][4 * j + i : 4 * j + i + 1, :] = parts[i, pl.ds(old, 1), :].astype(BF)
+            base = 4 * CAP + j * modes
+            small[rel - 1][base : base + modes, :] = sbuf[old].astype(BF)
+
+
+def pack_body(engines, rows, sends, source, tails, _, *refs):
     far = list(range(2, engines))
     near = refs[0]
-    msgs = refs[1 : 1 + len(far) * len(chunks)]
-    spread, tbuf, sbuf, pick, leave, slots, found, tsem, ssem = refs[1 + len(msgs) :]
+    msgs = refs[1 : 1 + len(sends)]
+    spread, tbuf, pick, leave, slots, found, tsem = refs[1 + len(msgs) :]
     tail_len, _, width = tails.shape
-    modes = states.shape[1]
     chunk = wide_chunk(width)
     me = lax.axis_index("engine")
     total = pl.cdiv(tail_len - 2, TB)
@@ -187,16 +188,9 @@
         n = sent_taps(b, tail_len)
         return pltpu.make_async_copy(tails.at[pl.ds(b * TB, n)], tbuf.at[pl.ds(b * TB, n)], tsem.at[b])
 
-    def fetch_state(rel, j):
-        slot = (rel - 1) * CAP + j
-        return pltpu.make_async_copy(states.at[leave[rel * (CAP + 1) + j]], sbuf.at[slot], ssem.at[slot])
-
     for b in range(total):
         fetch(b).start()
     departures(engines, rows, source, leave, me)
-    for rel in range(1, engines):
-        for j in range(CAP):
-            fetch_state(rel, j).start()
     send_selector([1] + far, rows, leave, pick)
     arrivals(engines, rows, source, slots, found, me)
     height, depth = spread.shape
@@ -215,32 +209,16 @@
     for b in range(total):
         fetch(b).wait()
         n = sent_taps(b, tail_len)
-        home = [i for i, blocks in enumerate(chunks) if b in blocks]
+        home = [(msg, rel, blocks) for msg, (rel, blocks) in zip(msgs, sends) if b in blocks]
         tall = pick.shape[0] if home else TB * CAP
-
         for c in range(0, width, chunk):
             cols = pl.ds(c, chunk)
             old = tbuf[b * TB : b * TB + n, :, cols].reshape(n * rows, chunk)
             rowsel = jnp.dot(pick[0:tall, 0 : n * rows], old, preferred_element_type=F32).astype(BF)
             near[b * TB * CAP : (b + 1) * TB * CAP, cols] = rowsel[0 : TB * CAP]
-            if home:
-                base = (b - chunks[home[0]][0]) * TB * CAP
-                for i in range(len(far)):
-                    msgs[home[0] * len(far) + i][base : base + TB * CAP, cols] = rowsel[
-                        (i + 1) * TB * CAP : (i + 2) * TB * CAP
-                    ]
-    for rel in range(1, engines):
-        for j in range(CAP):
-            fetch_state(rel, j).wait()
-            slot = (rel - 1) * CAP + j
-            if rel == 1:
-                base = total * TB * CAP
-                near[base + j * modes : base + (j + 1) * modes, :] = sbuf[slot].astype(BF)
-            else:
-                base = len(chunks[state_chunk]) * TB * CAP
-                msgs[state_chunk * len(far) + rel - 2][base + j * modes : base + (j + 1) * modes, :] = sbuf[
-                    slot
-                ].astype(BF)
+            for msg, rel, blocks in home:
+                base = (b - blocks[0]) * TB * CAP
+                msg[base : base + TB * CAP, cols] = rowsel[(rel - 1) * TB * CAP : rel * TB * CAP]
 
 
 def arrivals(engines, rows, source, slots, found, me):
@@ -348,110 +326,147 @@
             outs[d][:, h * pw : (h + 1) * pw] = tiles[rel * slots_here + slot % slots_here]
 
 
-def place_body(engines, rows, blocks, spread, gates, tails, near, *refs):
-    others = engines - 1
-    msgs = refs[: others - 1]
-    new_tails = refs[others]
-    tbuf, mbuf, obuf, isem, osem = refs[others + 1 :]
+def place_body(engines, rows, blocks, kept, layout, spread, gates, tails, near, *refs):
+    msgs = refs[: len(layout)]
+    if kept:
+        new, tbuf, isem = refs[len(layout) :]
+    else:
+        new, tbuf, obuf, isem, osem = refs[len(layout) + 1 :]
     tail_len, _, width = tails.shape
-    chunk = lane_chunk(width)
-    first = blocks[0] == 0
-    lead = 2 if first else 0
+    chunk = wide_chunk(width)
+    lead = 2 if blocks[0] == 0 else 0
 
     def fetch(n):
         b = blocks[n]
         taps = sent_taps(b, tail_len)
-        copies = [pltpu.make_async_copy(tails.at[pl.ds(b * TB, taps)], tbuf.at[n, pl.ds(0, taps)], isem.at[n, 0])]
-        for rel in range(1, engines):
-            ref = near if rel == 1 else msgs[rel - 2]
-            base = (b if rel == 1 else n) * TB * CAP
-            copies.append(
-                pltpu.make_async_copy(ref.at[pl.ds(base, TB * CAP)], mbuf.at[n, rel - 1], isem.at[n, rel])
-            )
-        return copies
+        return pltpu.make_async_copy(tails.at[pl.ds(b * TB, taps)], tbuf.at[n, pl.ds(0, taps)], isem.at[n])
 
     def store(n):
         b = blocks[n]
         taps = sent_taps(b, tail_len)
         extra = lead if n == 0 else 0
         return pltpu.make_async_copy(
-            obuf.at[n, pl.ds(2 - extra, taps + extra)], new_tails.at[pl.ds(b * TB + 2 - extra, taps + extra)], osem.at[n]
+            obuf.at[n, pl.ds(2 - extra, taps + extra)], new.at[pl.ds(b * TB + 2 - extra, taps + extra)], osem.at[n]
         )
 
     for n in range(len(blocks)):
-        for copy in fetch(n):
-            copy.start()
+        fetch(n).start()
+    if lead:
+        obuf[0, 0] = gates[1]
+        obuf[0, 1] = gates[0]
     for n, b in enumerate(blocks):
-        for copy in fetch(n):
-            copy.wait()
+        fetch(n).wait()
         taps = sent_taps(b, tail_len)
-        if first and n == 0:
-            obuf[0, 0] = gates[1]
-            obuf[0, 1] = gates[0]
-
+        top = taps * rows
         for c in range(0, width, chunk):
             cols = pl.ds(c, chunk)
-            old = tbuf[n, 0:taps, :, cols].reshape(taps * rows, chunk)
-            got = jnp.concatenate([mbuf[n, i, :, cols] for i in range(others)], axis=0)
-            top = taps * rows
-            new = jnp.dot(spread[0:top, 0:top], old, preferred_element_type=F32) + jnp.dot(
-                spread[0:top, TB * rows :], got, preferred_element_type=F32
+            old = tbuf[n, 0:taps, :, cols].reshape(top, chunk)
+            got = [near[b * TB * CAP : (b + 1) * TB * CAP, cols]]
+            for msg, held in zip(msgs, layout):
+                if b in held:
+                    got.append(msg[(b - held[0]) * TB * CAP : (b - held[0] + 1) * TB * CAP, cols])
+            got = jnp.concatenate(got, axis=0)
+            rest = TB * rows + got.shape[0]
+            value = jnp.dot(spread[0:top, 0:top], old, preferred_element_type=F32) + jnp.dot(
+                spread[0:top, TB * rows : rest], got, preferred_element_type=F32
             )
-            obuf[n, 2 : 2 + taps, :, cols] = new.astype(BF).reshape(taps, rows, chunk)
+            value = value.astype(BF).reshape(taps, rows, chunk)
+            if kept:
+                new[n, 0:taps, :, cols] = value
+            else:
+                obuf[n, 2 : 2 + taps, :, cols] = value
+        if not kept:
+            store(n).start()
+    if not kept:
+        for n in range(len(blocks)):
+            store(n).wait()
+
+
+def last_body(engines, rows, blocks, spread, base, msg, _, new_tails, obuf, osem):
+    tail_len, _, width = new_tails.shape
+    chunk = wide_chunk(width)
+
+    def store(n):
+        b = blocks[n]
+        taps = sent_taps(b, tail_len)
+        return pltpu.make_async_copy(obuf.at[n, pl.ds(0, taps)], new_tails.at[pl.ds(b * TB + 2, taps)], osem.at[n])
+
+    left = spread.shape[1] - TB * CAP
+    for n, b in enumerate(blocks):
+        taps = sent_taps(b, tail_len)
+        top = taps * rows
+        for c in range(0, width, chunk):
+            cols = pl.ds(c, chunk)
+            value = jnp.dot(
+                spread[0:top, left:], msg[n * TB * CAP : (n + 1) * TB * CAP, cols], preferred_element_type=F32
+            )
+            value = value + base[n, 0:taps, :, cols].reshape(top, chunk).astype(F32)
+            obuf[n, 0:taps, :, cols] = value.astype(BF).reshape(taps, rows, chunk)
         store(n).start()
     for n in range(len(blocks)):
         store(n).wait()
 
 
-def modal_body(engines, rows, bases, source, states, gates, decay, near, *refs):
+def modal_body(engines, rows, source, states, gates, decay, *refs):
     others = engines - 1
-    msgs = refs[: others - 1]
-    new_states = refs[others - 1]
-    sbuf, mbuf, slots, found, isem, msem, osem = refs[others:]
+    msgs = refs[:others]
+    new_states = refs[others]
+    sbuf, z, slots, found, isem, osem = refs[others + 1 :]
     modes = states.shape[1]
-    width = states.shape[2]
-    chunk = lane_chunk(width)
     me = lax.axis_index("engine")
 
     def fetch(r):
-        return pltpu.make_async_copy(states.at[source[me * rows + r] % rows], sbuf.at[r], isem.at[r])
-
-    def arrive(rel):
-        ref = near if rel == 1 else msgs[rel - 2]
-        return pltpu.make_async_copy(ref.at[pl.ds(bases[min(rel, 2) - 1], CAP * modes)], mbuf.at[rel - 1], msem.at[rel - 1])
+        return pltpu.make_async_copy(states.at[lax.rem(source[me * rows + r], rows)], sbuf.at[r], isem.at[r])
 
     def store(r):
         return pltpu.make_async_copy(sbuf.at[r], new_states.at[r], osem.at[r])
 
-    for r in range(rows):
-        fetch(r).start()
+    def stays(r):
+        return lax.div(source[me * rows + r], rows) == me
+
+    def begin(r, carry):
+        @pl.when(stays(r))
+        def _():
+            fetch(r).start()
+
+        return carry
+
+    lax.fori_loop(0, rows, begin, 0)
+    z[...] = gates[2:4].astype(F32)
+    arrivals(engines, rows, source, slots, found, me)
+
+    def advance(r, s):
+        d = decay[...]
+        sbuf[r] = d * (d * s + z[0, pl.ds(r, 1), :]) + z[1, pl.ds(r, 1), :]
+        store(r).start()
+
     for rel in range(1, engines):
-        arrive(rel).start()
-    arrivals(engines, rows, source, slots, found, me)
-    for r in range(rows):
-        fetch(r).wait()
-    for rel in range(1, engines):
-        arrive(rel).wait()
         for j in range(CAP):
 
             @pl.when(found[rel] > j)
             def _():
-                sbuf[slots[rel * (CAP + 1) + j]] = mbuf[rel - 1, j * modes : (j + 1) * modes].astype(F32)
-
-    for r in range(rows):
-        for c in range(0, width, chunk):
-            cols = pl.ds(c, chunk)
-            d = decay[:, cols]
-            z0 = gates[2, r : r + 1, cols].astype(F32)
-            z1 = gates[3, r : r + 1, cols].astype(F32)
-            sbuf[r, :, cols] = d * (d * sbuf[r, :, cols] + z0) + z1
-        store(r).start()
-    for r in range(rows):
+                base = 4 * CAP + j * modes
+                advance(slots[rel * (CAP + 1) + j], msgs[rel - 1][base : base + modes, :].astype(F32))
+
+    def work(r, carry):
+        @pl.when(stays(r))
+        def _():
+            fetch(r).wait()
+            advance(r, sbuf[r])
+
+        return carry
+
+    lax.fori_loop(0, rows, work, 0)
+
+    def finish(r, carry):
         store(r).wait()
+        return carry
+
+    lax.fori_loop(0, rows, finish, 0)
 
 
 def split(total):
-    cuts = [0, 3 * total // 8, 5 * total // 8, total]
+    cuts = [0, 2 * total // 8, 5 * total // 8, total]
     return [list(range(a, b)) for a, b in zip(cuts, cuts[1:]) if a < b]
 
 
@@ -473,12 +488,11 @@
     tails = jnp.transpose(conv_tails, (1, 0, 2))
     blocks = pl.cdiv(tail_len - 2, TB)
     chunks = split(blocks)
-    state_chunk = len(chunks) - 2
     table = pltpu.SMEM((engines * (CAP + 1),), jnp.int32)
     tally = pltpu.SMEM((engines,), jnp.int32)
 
     def msg_rows(i):
-        return len(chunks[i]) * TB * CAP + (CAP * modes if i == state_chunk else 0)
+        return len(chunks[i]) * TB * CAP
 
     msgs = {}
     msgs[0] = pl.pallas_call(
@@ -509,7 +523,7 @@
         functools.partial(lead_body, engines, rows),
         in_specs=[SM, ANY, ANY, VM, VM, VM, ANY],
         out_specs=[VM] * (1 + others),
-        out_shape=[sds((4, rows, width), F32)] + [sds((4 * CAP, width), BF)] * others,
+        out_shape=[sds((4, rows, width), F32)] + [sds((CAP * (4 + modes), width), BF)] * others,
         scratch_shapes=[
             pltpu.VMEM((taps + 8, width), F32),
             pltpu.VMEM((tail_len, rows, width), BF),
@@ -525,31 +539,31 @@
     small = lead[1 : 1 + others]
     parts_got = [send(small[rel - 1], engines, *rels[rel]) for rel in range(1, engines)]
 
-    later = chunks[1:]
+    sends = []
+    for i in range(1, len(chunks)):
+        sends += [(rel, chunks[i]) for rel in far]
     packed = pl.pallas_call(
-        functools.partial(pack_body, engines, rows, later, state_chunk - 1),
-        in_specs=[SM, ANY, ANY, ANY],
-        out_specs=[VM] * (2 + len(far) * len(later)),
-        out_shape=[sds((blocks * TB * CAP + CAP * modes, width), BF)]
-        + [sds((msg_rows(i), width), BF) for i in range(1, len(chunks)) for _ in far]
+        functools.partial(pack_body, engines, rows, sends),
+        in_specs=[SM, ANY, ANY],
+        out_specs=[VM] * (2 + len(sends)),
+        out_shape=[sds((blocks * TB * CAP, width), BF)]
+        + [sds((len(group) * TB * CAP, width), BF) for _, group in sends]
         + [sds((TB * rows, TB * rows + others * TB * CAP), BF)],
         scratch_shapes=[
             pltpu.VMEM((tail_len, rows, width), BF),
-            pltpu.VMEM((others * CAP, modes, width), F32),
             pltpu.VMEM((others * TB * CAP, TB * rows), BF),
             table,
             table,
             tally,
             dma((blocks,)),
-            dma((others * CAP,)),
         ],
         compiler_params=params,
         name="pack",
-    )(source, tails, modal_states, small[0])
+    )(source, tails, small[0])
     near_msg = packed[0]
     spread = packed[-1]
-    for i in range(1, len(chunks)):
-        msgs[i] = packed[1 + (i - 1) * len(far) : 1 + i * len(far)]
+    msgs[1] = packed[1 : 1 + len(far)]
+    msgs[2] = packed[1 + len(far) : 1 + 2 * len(far)]
 
     y, gates = pl.pallas_call(
         functools.partial(mix_body, engines, rows),
@@ -569,26 +583,25 @@
         ys += [same_core[k], send(same_core[k], engines, 0, 1)]
     ys[1] = launch(1, ys[1])
 
-    def place(i, new_tails):
+    def place(i, arrays, layout, tails_so_far, kept=False):
+        group = chunks[i]
+        buffer = pltpu.VMEM((len(group), TB, rows, width), BF)
+        carry = [] if kept else [gates if tails_so_far is None else tails_so_far]
         return pl.pallas_call(
-            functools.partial(place_body, engines, rows, chunks[i]),
-            in_specs=[VM, VM] + [ANY] * (2 + len(far) + 1),
-            out_specs=ANY,
-            out_shape=sds((tail_len, rows, width), BF),
-            input_output_aliases={} if i == 0 else {4 + len(far): 0},
-            scratch_shapes=[
-                pltpu.VMEM((len(chunks[i]), TB, rows, width), BF),
-                pltpu.VMEM((len(chunks[i]), others, TB * CAP, width), BF),
-                pltpu.VMEM((len(chunks[i]), TB + 2, rows, width), BF),
-                dma((len(chunks[i]), engines)),
-                dma((len(chunks[i]),)),
-            ],
+            functools.partial(place_body, engines, rows, group, kept, layout),
+            in_specs=[VM, VM, ANY] + [VM] * (1 + len(arrays)) + [ANY] * len(carry),
+            out_specs=VM if kept else ANY,
+            out_shape=sds(buffer.shape if kept else (tail_len, rows, width), BF),
+            input_output_aliases={} if tails_so_far is None else {4 + len(arrays): 0},
+            scratch_shapes=[buffer, dma((len(group),))]
+            if kept
+            else [buffer, pltpu.VMEM((len(group), TB + 2, rows, width), BF), dma((len(group),)), dma((len(group),))],
             compiler_params=params,
             name="place",
- cost_estimate=TINY,
-        )(spread, gates, tails, near_got, *got[i], spread if i == 0 else new_tails)
-
-    new_tails = place(0, None)
+            cost_estimate=TINY,
+        )(spread, gates, tails, near_got, *arrays, *carry)
+
+    new_tails = place(0, got[0], [chunks[0]] * len(far), None)
     depth = 512
     outs = pl.pallas_call(
         functools.partial(project_body, engines, rows, slots_here, depth),
@@ -609,8 +622,27 @@
     back = [outs[0]]
     for k, f in rels[1:]:
         back.append(send(outs[2 * ((chips - k) % chips) + f], engines, k, f))
-    back[1] = launch(2, back[1])
-
+    got[1] = launch(2, got[1])
+
+    new_states = pl.pallas_call(
+        functools.partial(modal_body, engines, rows),
+        in_specs=[SM, ANY, VM, VM] + [VM] * others,
+        out_specs=ANY,
+        out_shape=sds((rows, modes, width), F32),
+        scratch_shapes=[
+            pltpu.VMEM((rows, modes, width), F32),
+            pltpu.VMEM((2, rows, width), F32),
+            table,
+            tally,
+            dma((rows,)),
+            dma((rows,)),
+        ],
+        compiler_params=params,
+        name="modal",
+        cost_estimate=TINY,
+    )(source, modal_states, gates, li_decay, *parts_got)
+
+    back[1], new_states = lax.optimization_barrier((back[1], new_states))
     per_chan = panel_slot.shape[0] // chans
     blocks_out = pl.pallas_call(
         functools.partial(sort_body, engines, chans, slots_here),
@@ -620,38 +652,30 @@
         scratch_shapes=[pltpu.VMEM((engines * slots_here, 2 * rows, pw), BF)],
         compiler_params=params,
         name="sort",
- cost_estimate=TINY,
+        cost_estimate=TINY,
     )(panel_slot, *back, *got[1])
     total = blocks_out[0].astype(F32)
     for d in range(1, chans):
         total = total + lax.ppermute(blocks_out[d], "chan", [(c, (c + d) % chans) for c in range(chans)]).astype(F32)
     steps_ids = jnp.arange(2, dtype=jnp.int32)
     active = (remaining[None, :] > steps_ids[:, None]).astype(F32)
-    total, got[2] = lax.optimization_barrier((total, got[2]))
+    total, got[2][0] = lax.optimization_barrier((total, got[2][0]))
     mixed = (total.reshape(2, rows, per_chan * pw) * active[:, :, None]).astype(BF)
 
-    new_tails = place(1, new_tails)
-    new_tails = place(2, new_tails)
-    new_states = pl.pallas_call(
-        functools.partial(
-            modal_body, engines, rows, [blocks * TB * CAP, len(chunks[state_chunk]) * TB * CAP]
-        ),
-        in_specs=[SM, ANY, VM, VM] + [ANY] * others,
+    new_tails = place(1, got[1], [chunks[1]] * len(far), new_tails)
+    base = place(2, got[2][:-1], [chunks[2]] * (len(far) - 1), None, True)
+    buffer = pltpu.VMEM((len(chunks[2]), TB, rows, width), BF)
+    new_tails = pl.pallas_call(
+        functools.partial(last_body, engines, rows, chunks[2]),
+        in_specs=[VM, VM, VM, ANY],
         out_specs=ANY,
-        out_shape=sds((rows, modes, width), F32),
-        scratch_shapes=[
-            pltpu.VMEM((rows, modes, width), F32),
-            pltpu.VMEM((others, CAP * modes, width), BF),
-            table,
-            tally,
-            dma((rows,)),
-            dma((others,)),
-            dma((rows,)),
-        ],
+        out_shape=sds((tail_len, rows, width), BF),
+        input_output_aliases={3: 0},
+        scratch_shapes=[buffer, dma((len(chunks[2]),))],
         compiler_params=params,
-        name="modal",
- cost_estimate=TINY,
-    )(source, modal_states, gates, li_decay, near_got, *got[state_chunk])
+        name="last",
+        cost_estimate=TINY,
+    )(spread, base, got[2][-1], new_tails)
     return (mixed, jnp.transpose(new_tails, (1, 0, 2)), new_states)
 
 

time: 85 us -> 76.4 us (0.90)
  waiting for transfers between devices: 24 us -> 15 us
  starting transfers between devices: 18 us -> 20.7 us
  Pallas kernels: 39.7 us -> 37.9 us
    ppermute x16, waiting for transfers between devices: 24 us -> 15 us  [send(): return lax.ppermute(x, 'engine', pairs)]
    ppermute x16, starting transfers between devices: 13.1 us -> 15.1 us  [send(): return lax.ppermute(x, 'engine', pairs)]
    pallas_call x5 -> x6, Pallas kernels: 23.6 us -> 22.1 us  [the longest x3 11.3 us: place(): pl.pallas_call(functools.partial(place_body, engines, rows, group, kept,...]
  transfers between devices with their start and end apart: 19 -> 19, of which waited for: 7 -> 8; matrix products, arithmetic and copies ran while one was open for 0% -> 1% of each run, Pallas kernels for 36% -> 42%
where the time goes in v3:
time: 76.4 us; the launch traced here: 76.2 us
  Pallas kernels  37.9 us (50%)
  starting transfers between devices  20.7 us (27%)
  waiting for transfers between devices  15 us (20%)
  between operations  1.04 us (1%)
  local copies, waits for them, and re-layouts  0.85 us (1%)
    ppermute x16, starting transfers between devices, send(): return lax.ppermute(x, 'engine', pairs)  15.1 us
    ppermute x16, waiting for transfers between devices, send(): return lax.ppermute(x, 'engine', pairs)  15 us
    pallas_call x3, Pallas kernels, place(): pl.pallas_call(functools.partial(place_body, engines, rows, group, kept,...  11.3 us
    pallas_call x1, Pallas kernels, body(): pl.pallas_call(functools.partial(lead_body, engines, rows), in_specs=[SM,...  6.99 us
    ppermute x3, starting transfers between devices, body(): lax.ppermute(blocks_out[d], 'chan', [(c, (c + d) % chans) for c in range(...  5.55 us
    pallas_call x1, Pallas kernels, body(): pl.pallas_call(functools.partial(modal_body, engines, rows), in_specs=[SM...  4.42 us
    pallas_call x1, Pallas kernels, body(): pl.pallas_call(functools.partial(pack_body, engines, rows, sends), in_spe...  4.32 us
    pallas_call x1, Pallas kernels, body(): pl.pallas_call(functools.partial(project_body, engines, rows, slots_here,...  4.27 us
  transfers between devices with their start and end apart: 19, of which 8 were waited for; matrix products, arithmetic and copies ran while one was open for 1% of the time, Pallas kernels for 42%

profile of v3, /device:TPU:0, one launch (start us, length us, event | category | flops | bytes accessed | tf_op | source)
XLA Modules:
  0.0 76.2 jit_solution(7648545379920254210)
XLA Ops:
  0.6 0.0 copy-start.3
  0.6 0.0 copy-start.4
  0.7 0.0 copy-start.2
  0.7 0.0 copy-start
  0.7 0.0 copy-start.7
  0.7 0.8 %copy-done.7 = s32[64]{0:T(128)S(1)} copy-done((s32[64]{0:T(128)S(1)}, s32[64]{0:T(128)}, u32[]{:S(2)}) %copy-start.7) | copy-done | bytes 280
  1.5 2.4 %early.1 = (bf16[64,2048]{1,0:T(8,128)(2,1)S(1)}, bf16[64,2048]{1,0:T(8,128)(2,1)S(1)}) custom-call(s32[64]{0:T(128)S(1)} %copy-done.7, bf16[127,16,2048]{2,1,0:T(8,128)(2,1)} %bitcast.3), custom_call_target="tpu_custom_call" | custom-call | tf_op jit(solution)/shard_map/early/pallas_call | solution.py:498
  3.9 2.5 %collective-permute-start.4 = (bf16[64,2048]{1,0:T(8,128)(2,1)S(1)}, bf16[64,2048]{1,0:T(8,128)(2,1)S(1)}, u32[]{:S(2)}, u32[]{:S(2)}) collective-permute-start(bf16[64,2048]{1,0:T(8,128)(2,1)S(1)} %get-tuple-element.45), channel_id=1, source_target_pairs={{0,12},{4,8},{8,4},{12,0},{1,13},{5,9},{9,5},{13,1},{2,14},{6,10},... | collective-permute-start | bytes 786440 | tf_op jit(solution)/shard_map/ppermute | solution.py:40
  6.4 0.6 collective-permute-start.3
  7.0 0.0 copy-done.3
  7.0 0.0 copy-done.4
  7.0 0.0 copy-done.2
  7.0 0.0 copy-done
  7.0 7.0 %lead.1 = (f32[4,16,2048]{2,1,0:T(8,128)S(1)}, bf16[40,2048]{1,0:T(8,128)(2,1)S(1)}, bf16[40,2048]{1,0:T(8,128)(2,1)S(1)}, bf16[40,2048]{1,0:T(8,128)(2,1)S(1)}) custom-call(s32[64]{0:T(128)S(1)} %copy-done.7, bf16[127,16,2048]{2,1,0:T(8,128)(2,1)} %bitcast.4, f32[16,16,2048]{2,1,0:T(8,128)S(1)} %copy-done, bf16[128,2048]{1,0:T(8,128)(2,1)S(1)} %copy-done.2, ...), custom_call_target="tpu_custom_call" | custom-call | tf_op jit(solution)/shard_map/lead/pallas_call | solution.py:522
  14.0 1.5 %collective-permute-start.1 = (bf16[40,2048]{1,0:T(8,128)(2,1)S(1)}, bf16[40,2048]{1,0:T(8,128)(2,1)S(1)}, u32[]{:S(2)}, u32[]{:S(2)}) collective-permute-start(bf16[40,2048]{1,0:T(8,128)(2,1)S(1)} %get-tuple-element.42), channel_id=1, source_target_pairs={{0,8},{4,12},{8,0},{12,4},{1,9},{5,13},{9,1},{13,5},{2,10},{6,14},... | collective-permute-start | bytes 491528 | tf_op jit(solution)/shard_map/ppermute | solution.py:40
  15.5 0.1 collective-permute-start.2
  15.5 0.7 collective-permute-start
  16.2 4.3 %pack.1 = (bf16[256,2048]{1,0:T(8,128)(2,1)S(1)}, bf16[96,2048]{1,0:T(8,128)(2,1)S(1)}, bf16[96,2048]{1,0:T(8,128)(2,1)S(1)}, bf16[96,2048]{1,0:T(8,128)(2,1)S(1...) custom-call(s32[64]{0:T(128)S(1)} %copy-done.7, bf16[127,16,2048]{2,1,0:T(8,128)(2,1)} %bitcast.5, ...), custom_call_target="tpu_custom_call" | custom-call | tf_op jit(solution)/shard_map/pack/pallas_call | solution.py:545
  20.5 2.6 %collective-permute-done.1.refs_1_ = bf16[40,2048]{1,0:T(8,128)(2,1)S(1)} collective-permute-done((bf16[40,2048]{1,0:T(8,128)(2,1)S(1)}, bf16[40,2048]{1,0:T(8,128)(2,1)S(1)}, u32[]{:S(2)}, u32[]{:S(2)}) %collective-permute-start.1) | collective-permute-done | bytes 163872 | tf_op jit(solution)/shard_map/ppermute | solution.py:40
  23.2 2.5 %collective-permute-done.2.refs_2_ = bf16[40,2048]{1,0:T(8,128)(2,1)S(1)} collective-permute-done((bf16[40,2048]{1,0:T(8,128)(2,1)S(1)}, bf16[40,2048]{1,0:T(8,128)(2,1)S(1)}, u32[]{:S(2)}, u32[]{:S(2)}) %collective-permute-start.2) | collective-permute-done | bytes 163872 | tf_op jit(solution)/shard_map/ppermute | solution.py:40
  25.7 0.0 collective-permute-done.refs_0_
  25.7 0.0 collective-permute-done.4.refs_5_.refs_1_
  25.7 0.0 collective-permute-done.3.refs_4_.refs_0_
  25.7 0.0 copy-done.5
  25.7 1.5 %mix.1 = (bf16[64,2048]{1,0:T(8,128)(2,1)S(1)}, bf16[4,16,2048]{2,1,0:T(8,128)(2,1)S(1)}) custom-call(s32[64]{0:T(128)S(1)} %copy-done.7, f32[4,16,2048]{2,1,0:T(8,128)S(1)} %get-tuple-element.41.parts_in, bf16[2,3,16,2048]{3,2,1,0:T(8,128)(2,1)S(1)} %copy-done.5, bf16[2,3,16,2048]{3,2,1,0:T(8,128)(2,1)S(1)} %copy-done.6, bf16[128,2048]{1,0:T(8,128)(2,1)S(1)} %copy-done.2, ...), custom_call_target="tpu_custom_call" | custom-call | tf_op jit(solution)/shard_map/mix/pallas_call | solution.py:568
  27.2 0.2 collective-permute-start.8
  27.3 0.4 collective-permute-start.5
  27.8 2.5 %collective-permute-start.6 = (bf16[64,2048]{1,0:T(8,128)(2,1)S(1)}, bf16[64,2048]{1,0:T(8,128)(2,1)S(1)}, u32[]{:S(2)}, u32[]{:S(2)}) collective-permute-start(bf16[64,2048]{1,0:T(8,128)(2,1)S(1)} %get-tuple-element.47.refs_0_), channel_id=1, source_target_pairs={{0,8},{4,12},{8,0},{12,4},{1,9},{5,13},{9,1},{13,5},{2,10},{6,14},... | collective-permute-start | bytes 786440 | tf_op jit(solution)/shard_map/ppermute | solution.py:40
  30.2 0.1 collective-permute-done.5.refs_1_
  30.3 2.5 %collective-permute-start.12 = (bf16[96,2048]{1,0:T(8,128)(2,1)S(1)}, bf16[96,2048]{1,0:T(8,128)(2,1)S(1)}, u32[]{:S(2)}, u32[]{:S(2)}) collective-permute-start(bf16[96,2048]{1,0:T(8,128)(2,1)S(1)} %get-tuple-element.60), channel_id=1, source_target_pairs={{0,8},{4,12},{8,0},{12,4},{1,9},{5,13},{9,1},{13,5},{2,10},{6,14},... | collective-permute-start | bytes 1179656 | tf_op jit(solution)/shard_map/ppermute | solution.py:40
  32.7 0.0 collective-permute-start.13
  32.7 4.6 %collective-permute-done.6.refs_2_ = bf16[64,2048]{1,0:T(8,128)(2,1)S(1)} collective-permute-done((bf16[64,2048]{1,0:T(8,128)(2,1)S(1)}, bf16[64,2048]{1,0:T(8,128)(2,1)S(1)}, u32[]{:S(2)}, u32[]{:S(2)}) %collective-permute-start.6) | collective-permute-done | bytes 262176 | tf_op jit(solution)/shard_map/ppermute | solution.py:40
  37.3 0.0 collective-permute-start.7
  37.3 0.0 collective-permute-done.8.near
  37.3 3.8 %place.3.refs_6_.refs_2_ = bf16[127,16,2048]{2,1,0:T(8,128)(2,1)} custom-call(bf16[256,352]{1,0:T(8,128)(2,1)S(1)} %get-tuple-element.44.refs_3_.spread, bf16[4,16,2048]{2,1,0:T(8,128)(2,1)S(1)} %get-tuple-element.51.gates.refs_2_, bf16[127,16,2048]{2,1,0:T(8,128)(2,1)} %bitcast.6, bf16[256,2048]{1,0:T(8,128)(2,1)S(1)} %collective-permute-done.8.near, ...), custom_call_target="tpu_custom_call" | custom-call | flops 1 | bytes 1 | tf_op jit(solution)/shard_map/place/pallas_call | solution.py:590
  41.1 0.0 copy-start.8
  41.1 0.0 collective-permute-done.7.refs_3_
  41.1 4.3 %project.1 = (bf16[32,1024]{1,0:T(8,128)(2,1)S(1)}, bf16[32,1024]{1,0:T(8,128)(2,1)S(1)}, bf16[32,1024]{1,0:T(8,128)(2,1)S(1)}, bf16[32,1024]{1,0:T(8,128)(2,1)S(1)}) custom-call(bf16[64,2048]{1,0:T(8,128)(2,1)S(1)} %get-tuple-element.47.refs_0_, bf16[64,2048]{1,0:T(8,128)(2,1)S(1)} %collective-permute-done.5.refs_1_, ...), custom_call_target="tpu_custom_call" | custom-call | tf_op jit(solution)/shard_map/project/pallas_call | solution.py:606
  45.4 0.0 copy-start.9
  45.4 0.0 copy-start.10
  45.4 0.6 collective-permute-start.9
  46.0 2.1 %collective-permute-start.10 = (bf16[32,1024]{1,0:T(8,128)(2,1)S(1)}, bf16[32,1024]{1,0:T(8,128)(2,1)S(1)}, u32[]{:S(2)}, u32[]{:S(2)}) collective-permute-start(bf16[32,1024]{1,0:T(8,128)(2,1)S(1)} %get-tuple-element.56), channel_id=1, source_target_pairs={{0,8},{4,12},{8,0},{12,4},{1,9},{5,13},{9,1},{13,5},{2,10},{6,14},... | collective-permute-start | bytes 196616 | tf_op jit(solution)/shard_map/ppermute | solution.py:40
  48.0 0.0 collective-permute-start.11
  48.0 4.4 %modal.1 = f32[16,16,2048]{2,1,0:T(8,128)} custom-call(s32[64]{0:T(128)S(1)} %copy-done.8, f32[16,16,2048]{2,1,0:T(8,128)S(1)} %copy-done, bf16[4,16,2048]{2,1,0:T(8,128)(2,1)S(1)} %get-tuple-element.51.gates.refs_2_, f32[16,2048]{1,0:T(8,128)S(1)} %copy-done.3, bf16[40,2048]{1,0:T(8,128)(2,1)S(1)} %collective-permute-done.refs_0_, ...), custom_call_target="tpu_custom_call" | custom-call | flops 1 | bytes 1 | tf_op jit(solution)/shard_map/modal/pallas_call | solution.py:627
  52.5 0.0 collective-permute-done.12.refs_4_.refs_0_
  52.5 1.3 %collective-permute-done.13.refs_5_.refs_1_ = bf16[96,2048]{1,0:T(8,128)(2,1)S(1)} collective-permute-done((bf16[96,2048]{1,0:T(8,128)(2,1)S(1)}, bf16[96,2048]{1,0:T(8,128)(2,1)S(1)}, u32[]{:S(2)}, u32[]{:S(2)}) %collective-permute-start.13) | collective-permute-done | bytes 393248 | tf_op jit(solution)/shard_map/ppermute | solution.py:40
  53.7 0.8 %collective-permute-start.17 = (bf16[96,2048]{1,0:T(8,128)(2,1)S(1)}, bf16[96,2048]{1,0:T(8,128)(2,1)S(1)}, u32[]{:S(2)}, u32[]{:S(2)}) collective-permute-start(bf16[96,2048]{1,0:T(8,128)(2,1)S(1)} %get-tuple-element.68), channel_id=1, source_target_pairs={{0,8},{4,12},{8,0},{12,4},{1,9},{5,13},{9,1},{13,5},{2,10},{6,14},... | collective-permute-start | bytes 1179656 | tf_op jit(solution)/shard_map/ppermute | solution.py:40
  54.6 0.0 collective-permute-done.9.refs_1_
  54.6 1.0 %collective-permute-done.10.refs_2_ = bf16[32,1024]{1,0:T(8,128)(2,1)S(1)} collective-permute-done((bf16[32,1024]{1,0:T(8,128)(2,1)S(1)}, bf16[32,1024]{1,0:T(8,128)(2,1)S(1)}, u32[]{:S(2)}, u32[]{:S(2)}) %collective-permute-start.10) | collective-permute-done | bytes 65568 | tf_op jit(solution)/shard_map/ppermute | solution.py:40
  55.6 0.4 collective-permute-done.11.refs_3_
  55.9 0.7 sort.1
  56.6 1.6 %collective-permute-start.14 = (bf16[32,1024]{1,0:T(8,128)(2,1)S(1)}, bf16[32,1024]{1,0:T(8,128)(2,1)S(1)}, u32[]{:S(2)}, u32[]{:S(2)}) collective-permute-start(bf16[32,1024]{1,0:T(8,128)(2,1)S(1)} %get-tuple-element.65), channel_id=1, source_target_pairs={{0,1},{1,2},{2,3},{3,0},{4,5},{5,6},{6,7},{7,4},{8,9},{9,10},{10,1... | collective-permute-start | bytes 196616 | tf_op jit(solution)/shard_map/ppermute | solution.py:659
  58.2 2.6 %collective-permute-start.15 = (bf16[32,1024]{1,0:T(8,128)(2,1)S(1)}, bf16[32,1024]{1,0:T(8,128)(2,1)S(1)}, u32[]{:S(2)}, u32[]{:S(2)}) collective-permute-start(bf16[32,1024]{1,0:T(8,128)(2,1)S(1)} %get-tuple-element.66), channel_id=1, source_target_pairs={{0,2},{1,3},{2,0},{3,1},{4,6},{5,7},{6,4},{7,5},{8,10},{9,11},{10,... | collective-permute-start | bytes 196616 | tf_op jit(solution)/shard_map/ppermute | solution.py:659
  60.8 1.3 %collective-permute-start.16 = (bf16[32,1024]{1,0:T(8,128)(2,1)S(1)}, bf16[32,1024]{1,0:T(8,128)(2,1)S(1)}, u32[]{:S(2)}, u32[]{:S(2)}) collective-permute-start(bf16[32,1024]{1,0:T(8,128)(2,1)S(1)} %get-tuple-element.67), channel_id=1, source_target_pairs={{0,3},{1,0},{2,1},{3,2},{4,7},{5,4},{6,5},{7,6},{8,11},{9,8},{10,9... | collective-permute-start | bytes 196616 | tf_op jit(solution)/shard_map/ppermute | solution.py:659
  62.2 0.9 %collective-permute-start.18 = (bf16[96,2048]{1,0:T(8,128)(2,1)S(1)}, bf16[96,2048]{1,0:T(8,128)(2,1)S(1)}, u32[]{:S(2)}, u32[]{:S(2)}) collective-permute-start(bf16[96,2048]{1,0:T(8,128)(2,1)S(1)} %get-tuple-element.71), channel_id=1, source_target_pairs={{0,12},{4,8},{8,4},{12,0},{1,13},{5,9},{9,5},{13,1},{2,14},{6,10},... | collective-permute-start | bytes 1179656 | tf_op jit(solution)/shard_map/ppermute | solution.py:40
  63.0 4.3 %place.5._ = bf16[127,16,2048]{2,1,0:T(8,128)(2,1)} custom-call(bf16[256,352]{1,0:T(8,128)(2,1)S(1)} %get-tuple-element.44.refs_3_.spread, bf16[4,16,2048]{2,1,0:T(8,128)(2,1)S(1)} %get-tuple-element.51.gates.refs_2_, bf16[127,16,2048]{2,1,0:T(8,128)(2,1)} %bitcast.7, ...), custom_call_target="tpu_custom_call", output_to_operand_aliasing={{}: (6, {})} | custom-call | flops 1 | bytes 1 | tf_op jit(solution)/shard_map/place/pallas_call | solution.py:590
  67.4 0.0 collective-permute-done.14
  67.4 0.0 collective-permute-done.15
  67.4 0.0 collective-permute-done.16
  67.4 0.0 collective-permute-done.17.refs_0_
  67.4 3.2 %place.4.base = bf16[3,16,16,2048]{3,2,1,0:T(8,128)(2,1)S(1)} custom-call(bf16[256,352]{1,0:T(8,128)(2,1)S(1)} %get-tuple-element.44.refs_3_.spread, bf16[4,16,2048]{2,1,0:T(8,128)(2,1)S(1)} %get-tuple-element.51.gates.refs_2_, bf16[127,16,2048]{2,1,0:T(8,128)(2,1)} %bitcast.8, bf16[256,2048]{1,0:T(8,128)(2,1)S(1)} %collective-permute-done.8.near, ...), custom_call_target="tpu_custom_call" | custom-call | flops 1 | bytes 1 | tf_op jit(solution)/shard_map/place/pallas_call | solution.py:590
  70.7 0.7 multiply_convert_fusion
  71.4 2.5 %collective-permute-done.18.msg = bf16[96,2048]{1,0:T(8,128)(2,1)S(1)} collective-permute-done((bf16[96,2048]{1,0:T(8,128)(2,1)S(1)}, bf16[96,2048]{1,0:T(8,128)(2,1)S(1)}, u32[]{:S(2)}, u32[]{:S(2)}) %collective-permute-start.18) | collective-permute-done | bytes 393248 | tf_op jit(solution)/shard_map/ppermute | solution.py:40
  73.9 2.1 %last.1 = bf16[127,16,2048]{2,1,0:T(8,128)(2,1)} custom-call(bf16[256,352]{1,0:T(8,128)(2,1)S(1)} %get-tuple-element.44.refs_3_.spread, bf16[3,16,16,2048]{3,2,1,0:T(8,128)(2,1)S(1)} %place.4.base, bf16[96,2048]{1,0:T(8,128)(2,1)S(1)} %collective-permute-done.18.msg, bf16[127,16,2048]{2,1,0:T(8,128)(2,1)} %place.5._), custom_call_target="tpu_custom_call", output_to_operand_aliasing={{}: (3, {})} | custom-call | flops 1 | bytes 1 | tf_op jit(solution)/shard_map/last/pallas_call | solution.py:668
  (10 shorter events, 0.1 us)
Async XLA Ops:
  0.6 6.4 %copy-start.3 = (f32[16,2048]{1,0:T(8,128)S(1)}, f32[16,2048]{1,0:T(8,128)}, u32[]{:S(2)}) copy-start(f32[16,2048]{1,0:T(8,128)} %decay.5) | copy-start | bytes 393220
  0.6 6.4 %copy-start.4 = (f32[16,2048]{1,0:T(8,128)S(1)}, f32[16,2048]{1,0:T(8,128)}, u32[]{:S(2)}) copy-start(f32[16,2048]{1,0:T(8,128)} %resid.3) | copy-start | bytes 393220
  0.7 6.4 %copy-start.2 = (bf16[128,2048]{1,0:T(8,128)(2,1)S(1)}, bf16[128,2048]{1,0:T(8,128)(2,1)}, u32[]{:S(2)}) copy-start(bf16[128,2048]{1,0:T(8,128)(2,1)} %filt.3) | copy-start | bytes 1572868
  0.7 6.3 %copy-start = (f32[16,16,2048]{2,1,0:T(8,128)S(1)}, f32[16,16,2048]{2,1,0:T(8,128)}, u32[]{:S(2)}) copy-start(f32[16,16,2048]{2,1,0:T(8,128)} %states.3) | copy-start | bytes 6291460
  0.7 0.8 %copy-start.7 = (s32[64]{0:T(128)S(1)}, s32[64]{0:T(128)}, u32[]{:S(2)}) copy-start(s32[64]{0:T(128)} %source.9) | copy-start | bytes 772
  3.9 21.8 %collective-permute-start.4 = (bf16[64,2048]{1,0:T(8,128)(2,1)S(1)}, bf16[64,2048]{1,0:T(8,128)(2,1)S(1)}, u32[]{:S(2)}, u32[]{:S(2)}) collective-permute-start(bf16[64,2048]{1,0:T(8,128)(2,1)S(1)} %get-tuple-element.45), channel_id=1, source_target_pairs={{0,12},{4,8},{8,4},{12,0},{1,13},{5,9},{9,5},{13,1},{2,14},{6,10},... | collective-permute-start | bytes 786440 | tf_op jit(solution)/shard_map/ppermute | solution.py:40
  6.4 19.3 %collective-permute-start.3 = (bf16[64,2048]{1,0:T(8,128)(2,1)S(1)}, bf16[64,2048]{1,0:T(8,128)(2,1)S(1)}, u32[]{:S(2)}, u32[]{:S(2)}) collective-permute-start(bf16[64,2048]{1,0:T(8,128)(2,1)S(1)} %get-tuple-element.38._), channel_id=1, source_target_pairs={{0,8},{4,12},{8,0},{12,4},{1,9},{5,13},{9,1},{13,5},{2,10},{6,14},... | collective-permute-start | bytes 786440 | tf_op jit(solution)/shard_map/ppermute | solution.py:40
  14.0 9.2 %collective-permute-start.1 = (bf16[40,2048]{1,0:T(8,128)(2,1)S(1)}, bf16[40,2048]{1,0:T(8,128)(2,1)S(1)}, u32[]{:S(2)}, u32[]{:S(2)}) collective-permute-start(bf16[40,2048]{1,0:T(8,128)(2,1)S(1)} %get-tuple-element.42), channel_id=1, source_target_pairs={{0,8},{4,12},{8,0},{12,4},{1,9},{5,13},{9,1},{13,5},{2,10},{6,14},... | collective-permute-start | bytes 491528 | tf_op jit(solution)/shard_map/ppermute | solution.py:40
  15.5 10.2 %collective-permute-start.2 = (bf16[40,2048]{1,0:T(8,128)(2,1)S(1)}, bf16[40,2048]{1,0:T(8,128)(2,1)S(1)}, u32[]{:S(2)}, u32[]{:S(2)}) collective-permute-start(bf16[40,2048]{1,0:T(8,128)(2,1)S(1)} %get-tuple-element.43), channel_id=1, source_target_pairs={{0,12},{4,8},{8,4},{12,0},{1,13},{5,9},{9,5},{13,1},{2,14},{6,10},... | collective-permute-start | bytes 491528 | tf_op jit(solution)/shard_map/ppermute | solution.py:40
  15.5 10.2 %copy-start.5 = (bf16[2,3,16,2048]{3,2,1,0:T(8,128)(2,1)S(1)}, bf16[2,3,16,2048]{3,2,1,0:T(8,128)(2,1)}, u32[]{:S(2)}) copy-start(bf16[2,3,16,2048]{3,2,1,0:T(8,128)(2,1)} %mr.1) | copy-start | bytes 1179652
  15.5 10.2 %copy-start.6 = (bf16[2,3,16,2048]{3,2,1,0:T(8,128)(2,1)S(1)}, bf16[2,3,16,2048]{3,2,1,0:T(8,128)(2,1)}, u32[]{:S(2)}) copy-start(bf16[2,3,16,2048]{3,2,1,0:T(8,128)(2,1)} %li.1) | copy-start | bytes 1179652
  15.5 10.2 %collective-permute-start = (bf16[40,2048]{1,0:T(8,128)(2,1)S(1)}, bf16[40,2048]{1,0:T(8,128)(2,1)S(1)}, u32[]{:S(2)}, u32[]{:S(2)}) collective-permute-start(bf16[40,2048]{1,0:T(8,128)(2,1)S(1)} %get-tuple-element.39._), channel_id=1, source_target_pairs={{0,4},{4,0},{8,12},{12,8},{1,5},{5,1},{9,13},{13,9},{2,6},{6,2},{1... | collective-permute-start | bytes 491528 | tf_op jit(solution)/shard_map/ppermute | solution.py:40
  27.2 10.1 %collective-permute-start.8 = (bf16[256,2048]{1,0:T(8,128)(2,1)S(1)}, bf16[256,2048]{1,0:T(8,128)(2,1)S(1)}, u32[]{:S(2)}, u32[]{:S(2)}) collective-permute-start(bf16[256,2048]{1,0:T(8,128)(2,1)S(1)} %get-tuple-element.52), channel_id=1, source_target_pairs={{0,4},{4,0},{8,12},{12,8},{1,5},{5,1},{9,13},{13,9},{2,6},{6,2},{1... | collective-permute-start | bytes 3145736 | tf_op jit(solution)/shard_map/ppermute | solution.py:40
  27.3 2.9 %collective-permute-start.5 = (bf16[64,2048]{1,0:T(8,128)(2,1)S(1)}, bf16[64,2048]{1,0:T(8,128)(2,1)S(1)}, u32[]{:S(2)}, u32[]{:S(2)}) collective-permute-start(bf16[64,2048]{1,0:T(8,128)(2,1)S(1)} %get-tuple-element.47.refs_0_), channel_id=1, source_target_pairs={{0,4},{4,0},{8,12},{12,8},{1,5},{5,1},{9,13},{13,9},{2,6},{6,2},{1... | collective-permute-start | bytes 786440 | tf_op jit(solution)/shard_map/ppermute | solution.py:40
  27.8 9.5 %collective-permute-start.6 = (bf16[64,2048]{1,0:T(8,128)(2,1)S(1)}, bf16[64,2048]{1,0:T(8,128)(2,1)S(1)}, u32[]{:S(2)}, u32[]{:S(2)}) collective-permute-start(bf16[64,2048]{1,0:T(8,128)(2,1)S(1)} %get-tuple-element.47.refs_0_), channel_id=1, source_target_pairs={{0,8},{4,12},{8,0},{12,4},{1,9},{5,13},{9,1},{13,5},{2,10},{6,14},... | collective-permute-start | bytes 786440 | tf_op jit(solution)/shard_map/ppermute | solution.py:40
  30.3 22.2 %collective-permute-start.12 = (bf16[96,2048]{1,0:T(8,128)(2,1)S(1)}, bf16[96,2048]{1,0:T(8,128)(2,1)S(1)}, u32[]{:S(2)}, u32[]{:S(2)}) collective-permute-start(bf16[96,2048]{1,0:T(8,128)(2,1)S(1)} %get-tuple-element.60), channel_id=1, source_target_pairs={{0,8},{4,12},{8,0},{12,4},{1,9},{5,13},{9,1},{13,5},{2,10},{6,14},... | collective-permute-start | bytes 1179656 | tf_op jit(solution)/shard_map/ppermute | solution.py:40
  32.7 21.0 %collective-permute-start.13 = (bf16[96,2048]{1,0:T(8,128)(2,1)S(1)}, bf16[96,2048]{1,0:T(8,128)(2,1)S(1)}, u32[]{:S(2)}, u32[]{:S(2)}) collective-permute-start(bf16[96,2048]{1,0:T(8,128)(2,1)S(1)} %get-tuple-element.61), channel_id=1, source_target_pairs={{0,12},{4,8},{8,4},{12,0},{1,13},{5,9},{9,5},{13,1},{2,14},{6,10},... | collective-permute-start | bytes 1179656 | tf_op jit(solution)/shard_map/ppermute | solution.py:40
  37.3 3.8 %collective-permute-start.7 = (bf16[64,2048]{1,0:T(8,128)(2,1)S(1)}, bf16[64,2048]{1,0:T(8,128)(2,1)S(1)}, u32[]{:S(2)}, u32[]{:S(2)}) collective-permute-start(bf16[64,2048]{1,0:T(8,128)(2,1)S(1)} %collective-permute-done.6.refs_2_), channel_id=1, source_target_pairs={{0,4},{4,0},{8,12},{12,8},{1,5},{5,1},{9,13},{13,9},{2,6},{6,2},{1... | collective-permute-start | bytes 786440 | tf_op jit(solution)/shard_map/ppermute | solution.py:40
  37.3 3.8 %copy-start.1 = (bf16[2,2048,512]{2,1,0:T(8,128)(2,1)S(1)}, bf16[2,2048,512]{2,1,0:T(8,128)(2,1)}, u32[]{:S(2)}) copy-start(bf16[2,2048,512]{2,1,0:T(8,128)(2,1)} %refs_4_.1) | copy-start | bytes 12582916
  41.1 7.0 %copy-start.8 = (s32[64]{0:T(128)S(1)}, s32[64]{0:T(128)}, u32[]{:S(2)}) copy-start(s32[64]{0:T(128)} %source.9) | copy-start | bytes 772
  45.4 10.5 %copy-start.9 = (s32[8]{0:T(128)S(1)}, s32[8]{0:T(128)}, u32[]{:S(2)}) copy-start(s32[8]{0:T(128)} %slot_of.1) | copy-start | bytes 100
  45.4 16.8 %copy-start.10 = (s32[16]{0:T(128)S(1)}, s32[16]{0:T(128)}, u32[]{:S(2)}) copy-start(s32[16]{0:T(128)} %param.17) | copy-start | bytes 196
  45.4 9.1 %collective-permute-start.9 = (bf16[32,1024]{1,0:T(8,128)(2,1)S(1)}, bf16[32,1024]{1,0:T(8,128)(2,1)S(1)}, u32[]{:S(2)}, u32[]{:S(2)}) collective-permute-start(bf16[32,1024]{1,0:T(8,128)(2,1)S(1)} %get-tuple-element.54), channel_id=1, source_target_pairs={{0,4},{4,0},{8,12},{12,8},{1,5},{5,1},{9,13},{13,9},{2,6},{6,2},{1... | collective-permute-start | bytes 196616 | tf_op jit(solution)/shard_map/ppermute | solution.py:40
  46.0 9.6 %collective-permute-start.10 = (bf16[32,1024]{1,0:T(8,128)(2,1)S(1)}, bf16[32,1024]{1,0:T(8,128)(2,1)S(1)}, u32[]{:S(2)}, u32[]{:S(2)}) collective-permute-start(bf16[32,1024]{1,0:T(8,128)(2,1)S(1)} %get-tuple-element.56), channel_id=1, source_target_pairs={{0,8},{4,12},{8,0},{12,4},{1,9},{5,13},{9,1},{13,5},{2,10},{6,14},... | collective-permute-start | bytes 196616 | tf_op jit(solution)/shard_map/ppermute | solution.py:40
  48.0 7.9 %collective-permute-start.11 = (bf16[32,1024]{1,0:T(8,128)(2,1)S(1)}, bf16[32,1024]{1,0:T(8,128)(2,1)S(1)}, u32[]{:S(2)}, u32[]{:S(2)}) collective-permute-start(bf16[32,1024]{1,0:T(8,128)(2,1)S(1)} %get-tuple-element.57), channel_id=1, source_target_pairs={{0,12},{4,8},{8,4},{12,0},{1,13},{5,9},{9,5},{13,1},{2,14},{6,10},... | collective-permute-start | bytes 196616 | tf_op jit(solution)/shard_map/ppermute | solution.py:40
  53.7 13.7 %collective-permute-start.17 = (bf16[96,2048]{1,0:T(8,128)(2,1)S(1)}, bf16[96,2048]{1,0:T(8,128)(2,1)S(1)}, u32[]{:S(2)}, u32[]{:S(2)}) collective-permute-start(bf16[96,2048]{1,0:T(8,128)(2,1)S(1)} %get-tuple-element.68), channel_id=1, source_target_pairs={{0,8},{4,12},{8,0},{12,4},{1,9},{5,13},{9,1},{13,5},{2,10},{6,14},... | collective-permute-start | bytes 1179656 | tf_op jit(solution)/shard_map/ppermute | solution.py:40
  56.6 10.7 %collective-permute-start.14 = (bf16[32,1024]{1,0:T(8,128)(2,1)S(1)}, bf16[32,1024]{1,0:T(8,128)(2,1)S(1)}, u32[]{:S(2)}, u32[]{:S(2)}) collective-permute-start(bf16[32,1024]{1,0:T(8,128)(2,1)S(1)} %get-tuple-element.65), channel_id=1, source_target_pairs={{0,1},{1,2},{2,3},{3,0},{4,5},{5,6},{6,7},{7,4},{8,9},{9,10},{10,1... | collective-permute-start | bytes 196616 | tf_op jit(solution)/shard_map/ppermute | solution.py:659
  58.2 9.1 %collective-permute-start.15 = (bf16[32,1024]{1,0:T(8,128)(2,1)S(1)}, bf16[32,1024]{1,0:T(8,128)(2,1)S(1)}, u32[]{:S(2)}, u32[]{:S(2)}) collective-permute-start(bf16[32,1024]{1,0:T(8,128)(2,1)S(1)} %get-tuple-element.66), channel_id=1, source_target_pairs={{0,2},{1,3},{2,0},{3,1},{4,6},{5,7},{6,4},{7,5},{8,10},{9,11},{10,... | collective-permute-start | bytes 196616 | tf_op jit(solution)/shard_map/ppermute | solution.py:659
  60.8 6.6 %collective-permute-start.16 = (bf16[32,1024]{1,0:T(8,128)(2,1)S(1)}, bf16[32,1024]{1,0:T(8,128)(2,1)S(1)}, u32[]{:S(2)}, u32[]{:S(2)}) collective-permute-start(bf16[32,1024]{1,0:T(8,128)(2,1)S(1)} %get-tuple-element.67), channel_id=1, source_target_pairs={{0,3},{1,0},{2,1},{3,2},{4,7},{5,4},{6,5},{7,6},{8,11},{9,8},{10,9... | collective-permute-start | bytes 196616 | tf_op jit(solution)/shard_map/ppermute | solution.py:659
  62.2 11.7 %collective-permute-start.18 = (bf16[96,2048]{1,0:T(8,128)(2,1)S(1)}, bf16[96,2048]{1,0:T(8,128)(2,1)S(1)}, u32[]{:S(2)}, u32[]{:S(2)}) collective-permute-start(bf16[96,2048]{1,0:T(8,128)(2,1)S(1)} %get-tuple-element.71), channel_id=1, source_target_pairs={{0,12},{4,8},{8,4},{12,0},{1,13},{5,9},{9,5},{13,1},{2,14},{6,10},... | collective-permute-start | bytes 1179656 | tf_op jit(solution)/shard_map/ppermute | solution.py:40

commit v4 on v3

--- a/solution.py
+++ b/solution.py
@@ -84,10 +84,10 @@
     return min(TB, tail_len - 2 - b * TB)
 
 
-def early_body(engines, rows, blocks, source, tails, *refs):
+def early_body(engines, rows, blocks, source_far, tails, *refs):
     far = list(range(2, engines))
     msgs = refs[: len(far)]
-    tbuf, pick, leave, tsem = refs[len(far) :]
+    source, tbuf, pick, leave, tsem, source_sem = refs[len(far) :]
     tail_len, _, width = tails.shape
     chunk = wide_chunk(width)
     me = lax.axis_index("engine")
@@ -95,8 +95,11 @@
     def fetch(n):
         return pltpu.make_async_copy(tails.at[pl.ds(blocks[n] * TB, TB)], tbuf.at[pl.ds(n * TB, TB)], tsem.at[n])
 
+    read = pltpu.make_async_copy(source_far, source, source_sem)
+    read.start()
     for n in range(len(blocks)):
         fetch(n).start()
+    read.wait()
     departures(engines, rows, source, leave, me)
     send_selector(far, rows, leave, pick)
     for n in range(len(blocks)):
@@ -173,11 +176,11 @@
             small[rel - 1][base : base + modes, :] = sbuf[old].astype(BF)
 
 
-def pack_body(engines, rows, sends, source, tails, _, *refs):
+def pack_body(engines, rows, sends, source, tails, parts_in, *refs):
     far = list(range(2, engines))
     near = refs[0]
     msgs = refs[1 : 1 + len(sends)]
-    spread, tbuf, pick, leave, slots, found, tsem = refs[1 + len(msgs) :]
+    spread, parts, tbuf, pick, leave, slots, found, tsem = refs[1 + len(msgs) :]
     tail_len, _, width = tails.shape
     chunk = wide_chunk(width)
     me = lax.axis_index("engine")
@@ -206,6 +209,14 @@
             row = jnp.where(found[rel] > j, slots[rel * (CAP + 1) + j], -1)
             want = jnp.where(new_row == row, TB * rows + (rel - 1) * TB * CAP + CAP * tap + j, want)
     spread[...] = (lax.broadcasted_iota(jnp.int32, (height, depth), 1) == want).astype(F32).astype(BF)
+
+    def stay(r, carry):
+        old = lax.rem(source[me * rows + r], rows)
+        for i in range(4):
+            parts[i, pl.ds(r, 1), :] = parts_in[i, pl.ds(old, 1), :]
+        return carry
+
+    lax.fori_loop(0, rows, stay, 0)
     for b in range(total):
         fetch(b).wait()
         n = sent_taps(b, tail_len)
@@ -239,13 +250,7 @@
     me = lax.axis_index("engine")
     arrivals(engines, rows, source, slots, found, me)
 
-    def stay(r, carry):
-        old = source[me * rows + r] % rows
-        for i in range(4):
-            parts[i, pl.ds(r, 1), :] = parts_in[i, pl.ds(old, 1), :]
-        return carry
-
-    lax.fori_loop(0, rows, stay, 0)
+    parts[...] = parts_in[...]
     for rel in range(1, engines):
         for j in range(CAP):
 
@@ -497,18 +502,20 @@
     msgs = {}
     msgs[0] = pl.pallas_call(
         functools.partial(early_body, engines, rows, chunks[0]),
-        in_specs=[SM, ANY],
+        in_specs=[ANY, ANY],
         out_specs=[VM] * len(far),
         out_shape=[sds((msg_rows(0), width), BF)] * len(far),
         scratch_shapes=[
+            pltpu.SMEM(source.shape, jnp.int32),
             pltpu.VMEM((len(chunks[0]) * TB, rows, width), BF),
             pltpu.VMEM((len(far) * TB * CAP, TB * rows), BF),
             table,
             dma((len(chunks[0]),)),
+            dma(()),
         ],
         compiler_params=params,
         name="early",
-    )(source, tails)
+    )(pltpu.with_memory_space_constraint(source, pltpu.HBM), tails)
     got = {}
 
     def launch(i, token=None):
@@ -535,7 +542,6 @@
         compiler_params=params,
         name="lead",
     )(source, tails, modal_states, mr_filter, li_decay, li_residue, msgs[0][0])
-    parts = lead[0]
     small = lead[1 : 1 + others]
     parts_got = [send(small[rel - 1], engines, *rels[rel]) for rel in range(1, engines)]
 
@@ -544,11 +550,11 @@
         sends += [(rel, chunks[i]) for rel in far]
     packed = pl.pallas_call(
         functools.partial(pack_body, engines, rows, sends),
-        in_specs=[SM, ANY, ANY],
-        out_specs=[VM] * (2 + len(sends)),
+        in_specs=[SM, ANY, VM],
+        out_specs=[VM] * (3 + len(sends)),
         out_shape=[sds((blocks * TB * CAP, width), BF)]
         + [sds((len(group) * TB * CAP, width), BF) for _, group in sends]
-        + [sds((TB * rows, TB * rows + others * TB * CAP), BF)],
+        + [sds((TB * rows, TB * rows + others * TB * CAP), BF), sds((4, rows, width), F32)],
         scratch_shapes=[
             pltpu.VMEM((tail_len, rows, width), BF),
             pltpu.VMEM((others * TB * CAP, TB * rows), BF),
@@ -559,9 +565,9 @@
         ],
         compiler_params=params,
         name="pack",
-    )(source, tails, small[0])
+    )(source, tails, lead[0])
     near_msg = packed[0]
-    spread = packed[-1]
+    spread, parts = packed[-2:]
     msgs[1] = packed[1 : 1 + len(far)]
     msgs[2] = packed[1 + len(far) : 1 + 2 * len(far)]
 

time: 76.4 us -> 74.8 us (0.979)
  local copies, waits for them, and re-layouts: 0.85 us -> 0.04 us
  Pallas kernels: 37.9 us -> 37.1 us
    unnamed x22 -> x20, local copies, waits for them, and re-layouts: 0.85 us -> 0.04 us
  transfers between devices with their start and end apart: 19 -> 19, of which waited for: 8 -> 8; matrix products, arithmetic and copies ran while one was open for 1% -> 1% of each run, Pallas kernels for 42% -> 43%
where the time goes in v4:
time: 74.8 us; the launch traced here: 74.6 us
  Pallas kernels  37.1 us (50%)
  starting transfers between devices  20.4 us (27%)
  waiting for transfers between devices  15.3 us (20%)
  between operations  1.04 us (1%)
  other arithmetic  0.75 us (1%)
    ppermute x16, waiting for transfers between devices, send(): return lax.ppermute(x, 'engine', pairs)  15.3 us
    ppermute x16, starting transfers between devices, send(): return lax.ppermute(x, 'engine', pairs)  14.9 us
    pallas_call x3, Pallas kernels, place(): pl.pallas_call(functools.partial(place_body, engines, rows, group, kept,...  11.3 us
    pallas_call x1, Pallas kernels, body(): pl.pallas_call(functools.partial(lead_body, engines, rows), in_specs=[SM,...  6.93 us
    ppermute x3, starting transfers between devices, body(): lax.ppermute(blocks_out[d], 'chan', [(c, (c + d) % chans) for c in range(...  5.55 us
    pallas_call x1, Pallas kernels, body(): pl.pallas_call(functools.partial(modal_body, engines, rows), in_specs=[SM...  4.41 us
    pallas_call x1, Pallas kernels, body(): pl.pallas_call(functools.partial(pack_body, engines, rows, sends), in_spe...  4.31 us
    pallas_call x1, Pallas kernels, body(): pl.pallas_call(functools.partial(project_body, engines, rows, slots_here,...  4.27 us
  transfers between devices with their start and end apart: 19, of which 8 were waited for; matrix products, arithmetic and copies ran while one was open for 1% of the time, Pallas kernels for 43%

profile of v4, /device:TPU:0, one launch (start us, length us, event | category | flops | bytes accessed | tf_op | source)
XLA Modules:
  0.0 74.6 jit_solution(477614290445349425)
XLA Ops:
  0.6 0.0 copy-start.7
  0.6 0.0 copy-start.3
  0.7 0.0 copy-start.4
  0.7 0.0 copy-start.2
  0.7 0.0 copy-start
  0.7 2.0 %early.1 = (bf16[64,2048]{1,0:T(8,128)(2,1)S(1)}, bf16[64,2048]{1,0:T(8,128)(2,1)S(1)}) custom-call(s32[64]{0:T(128)} %source.7, bf16[127,16,2048]{2,1,0:T(8,128)(2,1)} %bitcast.3), custom_call_target="tpu_custom_call" | custom-call | tf_op jit(solution)/shard_map/early/pallas_call | solution.py:503
  2.7 2.5 %collective-permute-start.4 = (bf16[64,2048]{1,0:T(8,128)(2,1)S(1)}, bf16[64,2048]{1,0:T(8,128)(2,1)S(1)}, u32[]{:S(2)}, u32[]{:S(2)}) collective-permute-start(bf16[64,2048]{1,0:T(8,128)(2,1)S(1)} %get-tuple-element.47), channel_id=1, source_target_pairs={{0,12},{4,8},{8,4},{12,0},{1,13},{5,9},{9,5},{13,1},{2,14},{6,10},... | collective-permute-start | bytes 786440 | tf_op jit(solution)/shard_map/ppermute | solution.py:40
  5.2 0.6 collective-permute-start.3
  5.8 0.0 copy-done.7
  5.8 0.0 copy-done.3
  5.8 0.0 copy-done.4
  5.8 0.0 copy-done.2
  5.8 0.0 copy-done
  5.8 6.9 %lead.1 = (f32[4,16,2048]{2,1,0:T(8,128)S(1)}, bf16[40,2048]{1,0:T(8,128)(2,1)S(1)}, bf16[40,2048]{1,0:T(8,128)(2,1)S(1)}, bf16[40,2048]{1,0:T(8,128)(2,1)S(1)}) custom-call(s32[64]{0:T(128)S(1)} %copy-done.7, bf16[127,16,2048]{2,1,0:T(8,128)(2,1)} %bitcast.4, f32[16,16,2048]{2,1,0:T(8,128)S(1)} %copy-done, bf16[128,2048]{1,0:T(8,128)(2,1)S(1)} %copy-done.2, ...), custom_call_target="tpu_custom_call" | custom-call | tf_op jit(solution)/shard_map/lead/pallas_call | solution.py:529
  12.8 0.1 collective-permute-start
  12.9 1.7 %collective-permute-start.1 = (bf16[40,2048]{1,0:T(8,128)(2,1)S(1)}, bf16[40,2048]{1,0:T(8,128)(2,1)S(1)}, u32[]{:S(2)}, u32[]{:S(2)}) collective-permute-start(bf16[40,2048]{1,0:T(8,128)(2,1)S(1)} %get-tuple-element.44), channel_id=1, source_target_pairs={{0,8},{4,12},{8,0},{12,4},{1,9},{5,13},{9,1},{13,5},{2,10},{6,14},... | collective-permute-start | bytes 491528 | tf_op jit(solution)/shard_map/ppermute | solution.py:40
  14.6 0.1 collective-permute-start.2
  14.7 4.3 %pack.1 = (bf16[256,2048]{1,0:T(8,128)(2,1)S(1)}, bf16[96,2048]{1,0:T(8,128)(2,1)S(1)}, bf16[96,2048]{1,0:T(8,128)(2,1)S(1)}, bf16[96,2048]{1,0:T(8,128)(2,1)S(1...) custom-call(s32[64]{0:T(128)S(1)} %copy-done.7, ...), custom_call_target="tpu_custom_call" | custom-call | tf_op jit(solution)/shard_map/pack/pallas_call | solution.py:551
  19.0 0.0 collective-permute-done.refs_0_
  19.1 2.9 %collective-permute-done.1.refs_1_ = bf16[40,2048]{1,0:T(8,128)(2,1)S(1)} collective-permute-done((bf16[40,2048]{1,0:T(8,128)(2,1)S(1)}, bf16[40,2048]{1,0:T(8,128)(2,1)S(1)}, u32[]{:S(2)}, u32[]{:S(2)}) %collective-permute-start.1) | collective-permute-done | bytes 163872 | tf_op jit(solution)/shard_map/ppermute | solution.py:40
  22.0 2.5 %collective-permute-done.2.refs_2_ = bf16[40,2048]{1,0:T(8,128)(2,1)S(1)} collective-permute-done((bf16[40,2048]{1,0:T(8,128)(2,1)S(1)}, bf16[40,2048]{1,0:T(8,128)(2,1)S(1)}, u32[]{:S(2)}, u32[]{:S(2)}) %collective-permute-start.2) | collective-permute-done | bytes 163872 | tf_op jit(solution)/shard_map/ppermute | solution.py:40
  24.5 0.0 collective-permute-done.4.refs_5_.refs_1_
  24.5 0.0 collective-permute-done.3.refs_4_.refs_0_
  24.5 0.0 copy-done.5
  24.5 1.1 %mix.1 = (bf16[64,2048]{1,0:T(8,128)(2,1)S(1)}, bf16[4,16,2048]{2,1,0:T(8,128)(2,1)S(1)}) custom-call(s32[64]{0:T(128)S(1)} %copy-done.7, f32[4,16,2048]{2,1,0:T(8,128)S(1)} %get-tuple-element.42.parts_in, bf16[2,3,16,2048]{3,2,1,0:T(8,128)(2,1)S(1)} %copy-done.5, bf16[2,3,16,2048]{3,2,1,0:T(8,128)(2,1)S(1)} %copy-done.6, bf16[128,2048]{1,0:T(8,128)(2,1)S(1)} %copy-done.2, ...), custom_call_target="tpu_custom_call" | custom-call | tf_op jit(solution)/shard_map/mix/pallas_call | solution.py:574
  25.6 0.2 collective-permute-start.8
  25.8 0.4 collective-permute-start.5
  26.2 2.5 %collective-permute-start.6 = (bf16[64,2048]{1,0:T(8,128)(2,1)S(1)}, bf16[64,2048]{1,0:T(8,128)(2,1)S(1)}, u32[]{:S(2)}, u32[]{:S(2)}) collective-permute-start(bf16[64,2048]{1,0:T(8,128)(2,1)S(1)} %get-tuple-element.49.refs_0_), channel_id=1, source_target_pairs={{0,8},{4,12},{8,0},{12,4},{1,9},{5,13},{9,1},{13,5},{2,10},{6,14},... | collective-permute-start | bytes 786440 | tf_op jit(solution)/shard_map/ppermute | solution.py:40
  28.7 0.1 collective-permute-done.5.refs_1_
  28.7 2.5 %collective-permute-start.12 = (bf16[96,2048]{1,0:T(8,128)(2,1)S(1)}, bf16[96,2048]{1,0:T(8,128)(2,1)S(1)}, u32[]{:S(2)}, u32[]{:S(2)}) collective-permute-start(bf16[96,2048]{1,0:T(8,128)(2,1)S(1)} %get-tuple-element.62), channel_id=1, source_target_pairs={{0,8},{4,12},{8,0},{12,4},{1,9},{5,13},{9,1},{13,5},{2,10},{6,14},... | collective-permute-start | bytes 1179656 | tf_op jit(solution)/shard_map/ppermute | solution.py:40
  31.2 0.0 collective-permute-start.13
  31.2 4.6 %collective-permute-done.6.refs_2_ = bf16[64,2048]{1,0:T(8,128)(2,1)S(1)} collective-permute-done((bf16[64,2048]{1,0:T(8,128)(2,1)S(1)}, bf16[64,2048]{1,0:T(8,128)(2,1)S(1)}, u32[]{:S(2)}, u32[]{:S(2)}) %collective-permute-start.6) | collective-permute-done | bytes 262176 | tf_op jit(solution)/shard_map/ppermute | solution.py:40
  35.8 0.0 collective-permute-start.7
  35.8 0.0 collective-permute-done.8.near
  35.8 3.8 %place.3.refs_6_.refs_2_ = bf16[127,16,2048]{2,1,0:T(8,128)(2,1)} custom-call(bf16[256,352]{1,0:T(8,128)(2,1)S(1)} %get-tuple-element.46.refs_3_.spread, bf16[4,16,2048]{2,1,0:T(8,128)(2,1)S(1)} %get-tuple-element.53.gates.refs_2_, bf16[127,16,2048]{2,1,0:T(8,128)(2,1)} %bitcast.6, bf16[256,2048]{1,0:T(8,128)(2,1)S(1)} %collective-permute-done.8.near, ...), custom_call_target="tpu_custom_call" | custom-call | flops 1 | bytes 1 | tf_op jit(solution)/shard_map/place/pallas_call | solution.py:596
  39.5 0.0 collective-permute-done.7.refs_3_
  39.5 0.0 copy-done.1
  39.6 4.3 %project.1 = (bf16[32,1024]{1,0:T(8,128)(2,1)S(1)}, bf16[32,1024]{1,0:T(8,128)(2,1)S(1)}, bf16[32,1024]{1,0:T(8,128)(2,1)S(1)}, bf16[32,1024]{1,0:T(8,128)(2,1)S(1)}) custom-call(bf16[64,2048]{1,0:T(8,128)(2,1)S(1)} %get-tuple-element.49.refs_0_, bf16[64,2048]{1,0:T(8,128)(2,1)S(1)} %collective-permute-done.5.refs_1_, ...), custom_call_target="tpu_custom_call" | custom-call | tf_op jit(solution)/shard_map/project/pallas_call | solution.py:612
  43.8 0.0 copy-start.8
  43.8 0.0 copy-start.9
  43.9 0.6 collective-permute-start.9
  44.4 2.1 %collective-permute-start.10 = (bf16[32,1024]{1,0:T(8,128)(2,1)S(1)}, bf16[32,1024]{1,0:T(8,128)(2,1)S(1)}, u32[]{:S(2)}, u32[]{:S(2)}) collective-permute-start(bf16[32,1024]{1,0:T(8,128)(2,1)S(1)} %get-tuple-element.58), channel_id=1, source_target_pairs={{0,8},{4,12},{8,0},{12,4},{1,9},{5,13},{9,1},{13,5},{2,10},{6,14},... | collective-permute-start | bytes 196616 | tf_op jit(solution)/shard_map/ppermute | solution.py:40
  46.5 0.0 collective-permute-start.11
  46.5 4.4 %modal.1 = f32[16,16,2048]{2,1,0:T(8,128)} custom-call(s32[64]{0:T(128)S(1)} %copy-done.7, f32[16,16,2048]{2,1,0:T(8,128)S(1)} %copy-done, bf16[4,16,2048]{2,1,0:T(8,128)(2,1)S(1)} %get-tuple-element.53.gates.refs_2_, f32[16,2048]{1,0:T(8,128)S(1)} %copy-done.3, bf16[40,2048]{1,0:T(8,128)(2,1)S(1)} %collective-permute-done.refs_0_, ...), custom_call_target="tpu_custom_call" | custom-call | flops 1 | bytes 1 | tf_op jit(solution)/shard_map/modal/pallas_call | solution.py:633
  50.9 0.0 collective-permute-done.12.refs_4_.refs_0_
  50.9 1.3 %collective-permute-done.13.refs_5_.refs_1_ = bf16[96,2048]{1,0:T(8,128)(2,1)S(1)} collective-permute-done((bf16[96,2048]{1,0:T(8,128)(2,1)S(1)}, bf16[96,2048]{1,0:T(8,128)(2,1)S(1)}, u32[]{:S(2)}, u32[]{:S(2)}) %collective-permute-start.13) | collective-permute-done | bytes 393248 | tf_op jit(solution)/shard_map/ppermute | solution.py:40
  52.2 0.8 %collective-permute-start.17 = (bf16[96,2048]{1,0:T(8,128)(2,1)S(1)}, bf16[96,2048]{1,0:T(8,128)(2,1)S(1)}, u32[]{:S(2)}, u32[]{:S(2)}) collective-permute-start(bf16[96,2048]{1,0:T(8,128)(2,1)S(1)} %get-tuple-element.70), channel_id=1, source_target_pairs={{0,8},{4,12},{8,0},{12,4},{1,9},{5,13},{9,1},{13,5},{2,10},{6,14},... | collective-permute-start | bytes 1179656 | tf_op jit(solution)/shard_map/ppermute | solution.py:40
  53.0 0.0 collective-permute-done.9.refs_1_
  53.0 1.0 %collective-permute-done.10.refs_2_ = bf16[32,1024]{1,0:T(8,128)(2,1)S(1)} collective-permute-done((bf16[32,1024]{1,0:T(8,128)(2,1)S(1)}, bf16[32,1024]{1,0:T(8,128)(2,1)S(1)}, u32[]{:S(2)}, u32[]{:S(2)}) %collective-permute-start.10) | collective-permute-done | bytes 65568 | tf_op jit(solution)/shard_map/ppermute | solution.py:40
  54.0 0.4 collective-permute-done.11.refs_3_
  54.4 0.7 sort.1
  55.1 1.6 %collective-permute-start.14 = (bf16[32,1024]{1,0:T(8,128)(2,1)S(1)}, bf16[32,1024]{1,0:T(8,128)(2,1)S(1)}, u32[]{:S(2)}, u32[]{:S(2)}) collective-permute-start(bf16[32,1024]{1,0:T(8,128)(2,1)S(1)} %get-tuple-element.67), channel_id=1, source_target_pairs={{0,1},{1,2},{2,3},{3,0},{4,5},{5,6},{6,7},{7,4},{8,9},{9,10},{10,1... | collective-permute-start | bytes 196616 | tf_op jit(solution)/shard_map/ppermute | solution.py:665
  56.7 2.6 %collective-permute-start.15 = (bf16[32,1024]{1,0:T(8,128)(2,1)S(1)}, bf16[32,1024]{1,0:T(8,128)(2,1)S(1)}, u32[]{:S(2)}, u32[]{:S(2)}) collective-permute-start(bf16[32,1024]{1,0:T(8,128)(2,1)S(1)} %get-tuple-element.68), channel_id=1, source_target_pairs={{0,2},{1,3},{2,0},{3,1},{4,6},{5,7},{6,4},{7,5},{8,10},{9,11},{10,... | collective-permute-start | bytes 196616 | tf_op jit(solution)/shard_map/ppermute | solution.py:665
  59.3 1.3 %collective-permute-start.16 = (bf16[32,1024]{1,0:T(8,128)(2,1)S(1)}, bf16[32,1024]{1,0:T(8,128)(2,1)S(1)}, u32[]{:S(2)}, u32[]{:S(2)}) collective-permute-start(bf16[32,1024]{1,0:T(8,128)(2,1)S(1)} %get-tuple-element.69), channel_id=1, source_target_pairs={{0,3},{1,0},{2,1},{3,2},{4,7},{5,4},{6,5},{7,6},{8,11},{9,8},{10,9... | collective-permute-start | bytes 196616 | tf_op jit(solution)/shard_map/ppermute | solution.py:665
  60.6 0.9 %collective-permute-start.18 = (bf16[96,2048]{1,0:T(8,128)(2,1)S(1)}, bf16[96,2048]{1,0:T(8,128)(2,1)S(1)}, u32[]{:S(2)}, u32[]{:S(2)}) collective-permute-start(bf16[96,2048]{1,0:T(8,128)(2,1)S(1)} %get-tuple-element.73), channel_id=1, source_target_pairs={{0,12},{4,8},{8,4},{12,0},{1,13},{5,9},{9,5},{13,1},{2,14},{6,10},... | collective-permute-start | bytes 1179656 | tf_op jit(solution)/shard_map/ppermute | solution.py:40
  61.5 4.3 %place.5._ = bf16[127,16,2048]{2,1,0:T(8,128)(2,1)} custom-call(bf16[256,352]{1,0:T(8,128)(2,1)S(1)} %get-tuple-element.46.refs_3_.spread, bf16[4,16,2048]{2,1,0:T(8,128)(2,1)S(1)} %get-tuple-element.53.gates.refs_2_, bf16[127,16,2048]{2,1,0:T(8,128)(2,1)} %bitcast.7, ...), custom_call_target="tpu_custom_call", output_to_operand_aliasing={{}: (6, {})} | custom-call | flops 1 | bytes 1 | tf_op jit(solution)/shard_map/place/pallas_call | solution.py:596
  65.8 0.0 collective-permute-done.14
  65.8 0.0 collective-permute-done.15
  65.8 0.0 collective-permute-done.16
  65.9 0.0 collective-permute-done.17.refs_0_
  65.9 3.2 %place.4.base = bf16[3,16,16,2048]{3,2,1,0:T(8,128)(2,1)S(1)} custom-call(bf16[256,352]{1,0:T(8,128)(2,1)S(1)} %get-tuple-element.46.refs_3_.spread, bf16[4,16,2048]{2,1,0:T(8,128)(2,1)S(1)} %get-tuple-element.53.gates.refs_2_, bf16[127,16,2048]{2,1,0:T(8,128)(2,1)} %bitcast.8, bf16[256,2048]{1,0:T(8,128)(2,1)S(1)} %collective-permute-done.8.near, ...), custom_call_target="tpu_custom_call" | custom-call | flops 1 | bytes 1 | tf_op jit(solution)/shard_map/place/pallas_call | solution.py:596
  69.1 0.7 multiply_convert_fusion
  69.8 2.5 %collective-permute-done.18.msg = bf16[96,2048]{1,0:T(8,128)(2,1)S(1)} collective-permute-done((bf16[96,2048]{1,0:T(8,128)(2,1)S(1)}, bf16[96,2048]{1,0:T(8,128)(2,1)S(1)}, u32[]{:S(2)}, u32[]{:S(2)}) %collective-permute-start.18) | collective-permute-done | bytes 393248 | tf_op jit(solution)/shard_map/ppermute | solution.py:40
  72.4 2.1 %last.1 = bf16[127,16,2048]{2,1,0:T(8,128)(2,1)} custom-call(bf16[256,352]{1,0:T(8,128)(2,1)S(1)} %get-tuple-element.46.refs_3_.spread, bf16[3,16,16,2048]{3,2,1,0:T(8,128)(2,1)S(1)} %place.4.base, bf16[96,2048]{1,0:T(8,128)(2,1)S(1)} %collective-permute-done.18.msg, bf16[127,16,2048]{2,1,0:T(8,128)(2,1)} %place.5._), custom_call_target="tpu_custom_call", output_to_operand_aliasing={{}: (3, {})} | custom-call | flops 1 | bytes 1 | tf_op jit(solution)/shard_map/last/pallas_call | solution.py:674
  (8 shorter events, 0.1 us)
Async XLA Ops:
  0.6 5.2 %copy-start.7 = (s32[64]{0:T(128)S(1)}, s32[64]{0:T(128)}, u32[]{:S(2)}) copy-start(s32[64]{0:T(128)} %source.7) | copy-start | bytes 772
  0.6 5.2 %copy-start.3 = (f32[16,2048]{1,0:T(8,128)S(1)}, f32[16,2048]{1,0:T(8,128)}, u32[]{:S(2)}) copy-start(f32[16,2048]{1,0:T(8,128)} %decay.5) | copy-start | bytes 393220
  0.7 5.2 %copy-start.4 = (f32[16,2048]{1,0:T(8,128)S(1)}, f32[16,2048]{1,0:T(8,128)}, u32[]{:S(2)}) copy-start(f32[16,2048]{1,0:T(8,128)} %resid.3) | copy-start | bytes 393220
  0.7 5.2 %copy-start.2 = (bf16[128,2048]{1,0:T(8,128)(2,1)S(1)}, bf16[128,2048]{1,0:T(8,128)(2,1)}, u32[]{:S(2)}) copy-start(bf16[128,2048]{1,0:T(8,128)(2,1)} %filt.3) | copy-start | bytes 1572868
  0.7 5.2 %copy-start = (f32[16,16,2048]{2,1,0:T(8,128)S(1)}, f32[16,16,2048]{2,1,0:T(8,128)}, u32[]{:S(2)}) copy-start(f32[16,16,2048]{2,1,0:T(8,128)} %states.3) | copy-start | bytes 6291460
  2.7 21.8 %collective-permute-start.4 = (bf16[64,2048]{1,0:T(8,128)(2,1)S(1)}, bf16[64,2048]{1,0:T(8,128)(2,1)S(1)}, u32[]{:S(2)}, u32[]{:S(2)}) collective-permute-start(bf16[64,2048]{1,0:T(8,128)(2,1)S(1)} %get-tuple-element.47), channel_id=1, source_target_pairs={{0,12},{4,8},{8,4},{12,0},{1,13},{5,9},{9,5},{13,1},{2,14},{6,10},... | collective-permute-start | bytes 786440 | tf_op jit(solution)/shard_map/ppermute | solution.py:40
  5.2 19.3 %collective-permute-start.3 = (bf16[64,2048]{1,0:T(8,128)(2,1)S(1)}, bf16[64,2048]{1,0:T(8,128)(2,1)S(1)}, u32[]{:S(2)}, u32[]{:S(2)}) collective-permute-start(bf16[64,2048]{1,0:T(8,128)(2,1)S(1)} %get-tuple-element.39._), channel_id=1, source_target_pairs={{0,8},{4,12},{8,0},{12,4},{1,9},{5,13},{9,1},{13,5},{2,10},{6,14},... | collective-permute-start | bytes 786440 | tf_op jit(solution)/shard_map/ppermute | solution.py:40
  12.8 6.3 %collective-permute-start = (bf16[40,2048]{1,0:T(8,128)(2,1)S(1)}, bf16[40,2048]{1,0:T(8,128)(2,1)S(1)}, u32[]{:S(2)}, u32[]{:S(2)}) collective-permute-start(bf16[40,2048]{1,0:T(8,128)(2,1)S(1)} %get-tuple-element.43), channel_id=1, source_target_pairs={{0,4},{4,0},{8,12},{12,8},{1,5},{5,1},{9,13},{13,9},{2,6},{6,2},{1... | collective-permute-start | bytes 491528 | tf_op jit(solution)/shard_map/ppermute | solution.py:40
  12.9 9.1 %collective-permute-start.1 = (bf16[40,2048]{1,0:T(8,128)(2,1)S(1)}, bf16[40,2048]{1,0:T(8,128)(2,1)S(1)}, u32[]{:S(2)}, u32[]{:S(2)}) collective-permute-start(bf16[40,2048]{1,0:T(8,128)(2,1)S(1)} %get-tuple-element.44), channel_id=1, source_target_pairs={{0,8},{4,12},{8,0},{12,4},{1,9},{5,13},{9,1},{13,5},{2,10},{6,14},... | collective-permute-start | bytes 491528 | tf_op jit(solution)/shard_map/ppermute | solution.py:40
  14.6 9.9 %collective-permute-start.2 = (bf16[40,2048]{1,0:T(8,128)(2,1)S(1)}, bf16[40,2048]{1,0:T(8,128)(2,1)S(1)}, u32[]{:S(2)}, u32[]{:S(2)}) collective-permute-start(bf16[40,2048]{1,0:T(8,128)(2,1)S(1)} %get-tuple-element.45), channel_id=1, source_target_pairs={{0,12},{4,8},{8,4},{12,0},{1,13},{5,9},{9,5},{13,1},{2,14},{6,10},... | collective-permute-start | bytes 491528 | tf_op jit(solution)/shard_map/ppermute | solution.py:40
  14.7 9.8 %copy-start.5 = (bf16[2,3,16,2048]{3,2,1,0:T(8,128)(2,1)S(1)}, bf16[2,3,16,2048]{3,2,1,0:T(8,128)(2,1)}, u32[]{:S(2)}) copy-start(bf16[2,3,16,2048]{3,2,1,0:T(8,128)(2,1)} %mr.1) | copy-start | bytes 1179652
  14.7 9.8 %copy-start.6 = (bf16[2,3,16,2048]{3,2,1,0:T(8,128)(2,1)S(1)}, bf16[2,3,16,2048]{3,2,1,0:T(8,128)(2,1)}, u32[]{:S(2)}) copy-start(bf16[2,3,16,2048]{3,2,1,0:T(8,128)(2,1)} %li.1) | copy-start | bytes 1179652
  25.6 10.1 %collective-permute-start.8 = (bf16[256,2048]{1,0:T(8,128)(2,1)S(1)}, bf16[256,2048]{1,0:T(8,128)(2,1)S(1)}, u32[]{:S(2)}, u32[]{:S(2)}) collective-permute-start(bf16[256,2048]{1,0:T(8,128)(2,1)S(1)} %get-tuple-element.54), channel_id=1, source_target_pairs={{0,4},{4,0},{8,12},{12,8},{1,5},{5,1},{9,13},{13,9},{2,6},{6,2},{1... | collective-permute-start | bytes 3145736 | tf_op jit(solution)/shard_map/ppermute | solution.py:40
  25.8 2.9 %collective-permute-start.5 = (bf16[64,2048]{1,0:T(8,128)(2,1)S(1)}, bf16[64,2048]{1,0:T(8,128)(2,1)S(1)}, u32[]{:S(2)}, u32[]{:S(2)}) collective-permute-start(bf16[64,2048]{1,0:T(8,128)(2,1)S(1)} %get-tuple-element.49.refs_0_), channel_id=1, source_target_pairs={{0,4},{4,0},{8,12},{12,8},{1,5},{5,1},{9,13},{13,9},{2,6},{6,2},{1... | collective-permute-start | bytes 786440 | tf_op jit(solution)/shard_map/ppermute | solution.py:40
  26.2 9.5 %collective-permute-start.6 = (bf16[64,2048]{1,0:T(8,128)(2,1)S(1)}, bf16[64,2048]{1,0:T(8,128)(2,1)S(1)}, u32[]{:S(2)}, u32[]{:S(2)}) collective-permute-start(bf16[64,2048]{1,0:T(8,128)(2,1)S(1)} %get-tuple-element.49.refs_0_), channel_id=1, source_target_pairs={{0,8},{4,12},{8,0},{12,4},{1,9},{5,13},{9,1},{13,5},{2,10},{6,14},... | collective-permute-start | bytes 786440 | tf_op jit(solution)/shard_map/ppermute | solution.py:40
  28.7 22.2 %collective-permute-start.12 = (bf16[96,2048]{1,0:T(8,128)(2,1)S(1)}, bf16[96,2048]{1,0:T(8,128)(2,1)S(1)}, u32[]{:S(2)}, u32[]{:S(2)}) collective-permute-start(bf16[96,2048]{1,0:T(8,128)(2,1)S(1)} %get-tuple-element.62), channel_id=1, source_target_pairs={{0,8},{4,12},{8,0},{12,4},{1,9},{5,13},{9,1},{13,5},{2,10},{6,14},... | collective-permute-start | bytes 1179656 | tf_op jit(solution)/shard_map/ppermute | solution.py:40
  31.2 21.0 %collective-permute-start.13 = (bf16[96,2048]{1,0:T(8,128)(2,1)S(1)}, bf16[96,2048]{1,0:T(8,128)(2,1)S(1)}, u32[]{:S(2)}, u32[]{:S(2)}) collective-permute-start(bf16[96,2048]{1,0:T(8,128)(2,1)S(1)} %get-tuple-element.63), channel_id=1, source_target_pairs={{0,12},{4,8},{8,4},{12,0},{1,13},{5,9},{9,5},{13,1},{2,14},{6,10},... | collective-permute-start | bytes 1179656 | tf_op jit(solution)/shard_map/ppermute | solution.py:40
  35.8 3.8 %collective-permute-start.7 = (bf16[64,2048]{1,0:T(8,128)(2,1)S(1)}, bf16[64,2048]{1,0:T(8,128)(2,1)S(1)}, u32[]{:S(2)}, u32[]{:S(2)}) collective-permute-start(bf16[64,2048]{1,0:T(8,128)(2,1)S(1)} %collective-permute-done.6.refs_2_), channel_id=1, source_target_pairs={{0,4},{4,0},{8,12},{12,8},{1,5},{5,1},{9,13},{13,9},{2,6},{6,2},{1... | collective-permute-start | bytes 786440 | tf_op jit(solution)/shard_map/ppermute | solution.py:40
  35.8 3.8 %copy-start.1 = (bf16[2,2048,512]{2,1,0:T(8,128)(2,1)S(1)}, bf16[2,2048,512]{2,1,0:T(8,128)(2,1)}, u32[]{:S(2)}) copy-start(bf16[2,2048,512]{2,1,0:T(8,128)(2,1)} %refs_4_.1) | copy-start | bytes 12582916
  43.8 10.6 %copy-start.8 = (s32[8]{0:T(128)S(1)}, s32[8]{0:T(128)}, u32[]{:S(2)}) copy-start(s32[8]{0:T(128)} %slot_of.1) | copy-start | bytes 100
  43.8 16.8 %copy-start.9 = (s32[16]{0:T(128)S(1)}, s32[16]{0:T(128)}, u32[]{:S(2)}) copy-start(s32[16]{0:T(128)} %param.17) | copy-start | bytes 196
  43.9 9.2 %collective-permute-start.9 = (bf16[32,1024]{1,0:T(8,128)(2,1)S(1)}, bf16[32,1024]{1,0:T(8,128)(2,1)S(1)}, u32[]{:S(2)}, u32[]{:S(2)}) collective-permute-start(bf16[32,1024]{1,0:T(8,128)(2,1)S(1)} %get-tuple-element.56), channel_id=1, source_target_pairs={{0,4},{4,0},{8,12},{12,8},{1,5},{5,1},{9,13},{13,9},{2,6},{6,2},{1... | collective-permute-start | bytes 196616 | tf_op jit(solution)/shard_map/ppermute | solution.py:40
  44.4 9.6 %collective-permute-start.10 = (bf16[32,1024]{1,0:T(8,128)(2,1)S(1)}, bf16[32,1024]{1,0:T(8,128)(2,1)S(1)}, u32[]{:S(2)}, u32[]{:S(2)}) collective-permute-start(bf16[32,1024]{1,0:T(8,128)(2,1)S(1)} %get-tuple-element.58), channel_id=1, source_target_pairs={{0,8},{4,12},{8,0},{12,4},{1,9},{5,13},{9,1},{13,5},{2,10},{6,14},... | collective-permute-start | bytes 196616 | tf_op jit(solution)/shard_map/ppermute | solution.py:40
  46.5 7.9 %collective-permute-start.11 = (bf16[32,1024]{1,0:T(8,128)(2,1)S(1)}, bf16[32,1024]{1,0:T(8,128)(2,1)S(1)}, u32[]{:S(2)}, u32[]{:S(2)}) collective-permute-start(bf16[32,1024]{1,0:T(8,128)(2,1)S(1)} %get-tuple-element.59), channel_id=1, source_target_pairs={{0,12},{4,8},{8,4},{12,0},{1,13},{5,9},{9,5},{13,1},{2,14},{6,10},... | collective-permute-start | bytes 196616 | tf_op jit(solution)/shard_map/ppermute | solution.py:40
  52.2 13.7 %collective-permute-start.17 = (bf16[96,2048]{1,0:T(8,128)(2,1)S(1)}, bf16[96,2048]{1,0:T(8,128)(2,1)S(1)}, u32[]{:S(2)}, u32[]{:S(2)}) collective-permute-start(bf16[96,2048]{1,0:T(8,128)(2,1)S(1)} %get-tuple-element.70), channel_id=1, source_target_pairs={{0,8},{4,12},{8,0},{12,4},{1,9},{5,13},{9,1},{13,5},{2,10},{6,14},... | collective-permute-start | bytes 1179656 | tf_op jit(solution)/shard_map/ppermute | solution.py:40
  55.1 10.7 %collective-permute-start.14 = (bf16[32,1024]{1,0:T(8,128)(2,1)S(1)}, bf16[32,1024]{1,0:T(8,128)(2,1)S(1)}, u32[]{:S(2)}, u32[]{:S(2)}) collective-permute-start(bf16[32,1024]{1,0:T(8,128)(2,1)S(1)} %get-tuple-element.67), channel_id=1, source_target_pairs={{0,1},{1,2},{2,3},{3,0},{4,5},{5,6},{6,7},{7,4},{8,9},{9,10},{10,1... | collective-permute-start | bytes 196616 | tf_op jit(solution)/shard_map/ppermute | solution.py:665
  56.7 9.1 %collective-permute-start.15 = (bf16[32,1024]{1,0:T(8,128)(2,1)S(1)}, bf16[32,1024]{1,0:T(8,128)(2,1)S(1)}, u32[]{:S(2)}, u32[]{:S(2)}) collective-permute-start(bf16[32,1024]{1,0:T(8,128)(2,1)S(1)} %get-tuple-element.68), channel_id=1, source_target_pairs={{0,2},{1,3},{2,0},{3,1},{4,6},{5,7},{6,4},{7,5},{8,10},{9,11},{10,... | collective-permute-start | bytes 196616 | tf_op jit(solution)/shard_map/ppermute | solution.py:665
  59.3 6.6 %collective-permute-start.16 = (bf16[32,1024]{1,0:T(8,128)(2,1)S(1)}, bf16[32,1024]{1,0:T(8,128)(2,1)S(1)}, u32[]{:S(2)}, u32[]{:S(2)}) collective-permute-start(bf16[32,1024]{1,0:T(8,128)(2,1)S(1)} %get-tuple-element.69), channel_id=1, source_target_pairs={{0,3},{1,0},{2,1},{3,2},{4,7},{5,4},{6,5},{7,6},{8,11},{9,8},{10,9... | collective-permute-start | bytes 196616 | tf_op jit(solution)/shard_map/ppermute | solution.py:665
  60.6 11.7 %collective-permute-start.18 = (bf16[96,2048]{1,0:T(8,128)(2,1)S(1)}, bf16[96,2048]{1,0:T(8,128)(2,1)S(1)}, u32[]{:S(2)}, u32[]{:S(2)}) collective-permute-start(bf16[96,2048]{1,0:T(8,128)(2,1)S(1)} %get-tuple-element.73), channel_id=1, source_target_pairs={{0,12},{4,8},{8,4},{12,0},{1,13},{5,9},{9,5},{13,1},{2,14},{6,10},... | collective-permute-start | bytes 1179656 | tf_op jit(solution)/shard_map/ppermute | solution.py:40

commit v5 on v4

--- a/solution.py
+++ b/solution.py
@@ -81,7 +81,7 @@
 
 
 def sent_taps(b, tail_len):
-    return min(TB, tail_len - 2 - b * TB)
+    return min(TB, tail_len - 3 - b * TB)
 
 
 def early_body(engines, rows, blocks, source_far, tails, *refs):
@@ -157,6 +157,7 @@
                 second += t * fbuf[b * TB + i + 2 : b * TB + i + 3, cols]
             parts[0, :, cols] = first
             parts[1, :, cols] = second
+    parts[4] = tbuf[tail_len - 3].astype(F32)
     load_states.wait()
 
     def modal(r, carry):
@@ -170,10 +171,10 @@
     for rel in range(1, engines):
         for j in range(CAP):
             old = leave[rel * (CAP + 1) + j]
-            for i in range(4):
-                small[rel - 1][4 * j + i : 4 * j + i + 1, :] = parts[i, pl.ds(old, 1), :].astype(BF)
-            base = 4 * CAP + j * modes
-            small[rel - 1][base : base + modes, :] = sbuf[old].astype(BF)
+            small[rel - 1][j * modes : (j + 1) * modes, :] = sbuf[old].astype(BF)
+            for n, i in enumerate((0, 1, 4)):
+                at = CAP * modes + 3 * j + n
+                small[rel - 1][at : at + 1, :] = parts[i, pl.ds(old, 1), :].astype(BF)
 
 
 def pack_body(engines, rows, sends, source, tails, parts_in, *refs):
@@ -184,7 +185,7 @@
     tail_len, _, width = tails.shape
     chunk = wide_chunk(width)
     me = lax.axis_index("engine")
-    total = pl.cdiv(tail_len - 2, TB)
+    total = pl.cdiv(tail_len - 3, TB)
     others = engines - 1
 
     def fetch(b):
@@ -212,7 +213,7 @@
 
     def stay(r, carry):
         old = lax.rem(source[me * rows + r], rows)
-        for i in range(4):
+        for i in range(5):
             parts[i, pl.ds(r, 1), :] = parts_in[i, pl.ds(old, 1), :]
         return carry
 
@@ -229,7 +230,7 @@
             near[b * TB * CAP : (b + 1) * TB * CAP, cols] = rowsel[0 : TB * CAP]
             for msg, rel, blocks in home:
                 base = (b - blocks[0]) * TB * CAP
-                msg[base : base + TB * CAP, cols] = rowsel[(rel - 1) * TB * CAP : rel * TB * CAP]
+                msg[base : base + n * CAP, cols] = rowsel[(rel - 1) * TB * CAP : (rel - 1) * TB * CAP + n * CAP]
 
 
 def arrivals(engines, rows, source, slots, found, me):
@@ -246,6 +247,7 @@
     got = refs[: engines - 1]
     y, gates, parts, slots, found = refs[-5:]
     width = y.shape[1]
+    modes = decay.shape[0]
     chunk = lane_chunk(width)
     me = lax.axis_index("engine")
     arrivals(engines, rows, source, slots, found, me)
@@ -257,9 +259,17 @@
             @pl.when(found[rel] > j)
             def _():
                 one = pl.ds(slots[rel * (CAP + 1) + j], 1)
-                for i in range(4):
-                    parts[i, one, :] = got[rel - 1][4 * j + i : 4 * j + i + 1, :].astype(F32)
-
+                for n, i in enumerate((0, 1, 4)):
+                    at = CAP * modes + 3 * j + n
+                    parts[i, one, :] = got[rel - 1][at : at + 1, :].astype(F32)
+                for c in range(0, width, chunk):
+                    cols = pl.ds(c, chunk)
+                    d = decay[:, cols]
+                    a = resid[:, cols] * (d * got[rel - 1][j * modes : (j + 1) * modes, cols].astype(F32))
+                    parts[2, one, cols] = jnp.sum(a, axis=0, keepdims=True)
+                    parts[3, one, cols] = jnp.sum(a * d, axis=0, keepdims=True)
+
+    gates[4] = parts[4].astype(BF)
     for c in range(0, width, chunk):
         cols = pl.ds(c, chunk)
         f = filt[0:16, cols].astype(F32)
@@ -359,6 +369,8 @@
     if lead:
         obuf[0, 0] = gates[1]
         obuf[0, 1] = gates[0]
+        edge = pltpu.make_async_copy(gates.at[4], new.at[tail_len - 1], osem.at[len(blocks)])
+        edge.start()
     for n, b in enumerate(blocks):
         fetch(n).wait()
         taps = sent_taps(b, tail_len)
@@ -366,15 +378,19 @@
         for c in range(0, width, chunk):
             cols = pl.ds(c, chunk)
             old = tbuf[n, 0:taps, :, cols].reshape(top, chunk)
-            got = [near[b * TB * CAP : (b + 1) * TB * CAP, cols]]
+            pieces = [near[b * TB * CAP : b * TB * CAP + taps * CAP, cols]]
             for msg, held in zip(msgs, layout):
                 if b in held:
-                    got.append(msg[(b - held[0]) * TB * CAP : (b - held[0] + 1) * TB * CAP, cols])
-            got = jnp.concatenate(got, axis=0)
-            rest = TB * rows + got.shape[0]
-            value = jnp.dot(spread[0:top, 0:top], old, preferred_element_type=F32) + jnp.dot(
-                spread[0:top, TB * rows : rest], got, preferred_element_type=F32
-            )
+                    base = (b - held[0]) * TB * CAP
+                    pieces.append(msg[base : base + taps * CAP, cols])
+            if taps == TB:
+                pieces = [jnp.concatenate(pieces, axis=0)]
+            value = jnp.dot(spread[0:top, 0:top], old, preferred_element_type=F32)
+            for i, piece in enumerate(pieces):
+                left = TB * rows + i * TB * CAP
+                value += jnp.dot(
+                    spread[0:top, left : left + piece.shape[0]], piece, preferred_element_type=F32
+                )
             value = value.astype(BF).reshape(taps, rows, chunk)
             if kept:
                 new[n, 0:taps, :, cols] = value
@@ -385,6 +401,8 @@
     if not kept:
         for n in range(len(blocks)):
             store(n).wait()
+    if lead:
+        edge.wait()
 
 
 def last_body(engines, rows, blocks, spread, base, msg, _, new_tails, obuf, osem):
@@ -403,7 +421,9 @@
         for c in range(0, width, chunk):
             cols = pl.ds(c, chunk)
             value = jnp.dot(
-                spread[0:top, left:], msg[n * TB * CAP : (n + 1) * TB * CAP, cols], preferred_element_type=F32
+                spread[0:top, left : left + taps * CAP],
+                msg[n * TB * CAP : n * TB * CAP + taps * CAP, cols],
+                preferred_element_type=F32,
             )
             value = value + base[n, 0:taps, :, cols].reshape(top, chunk).astype(F32)
             obuf[n, 0:taps, :, cols] = value.astype(BF).reshape(taps, rows, chunk)
@@ -450,7 +470,7 @@
 
             @pl.when(found[rel] > j)
             def _():
-                base = 4 * CAP + j * modes
+                base = j * modes
                 advance(slots[rel * (CAP + 1) + j], msgs[rel - 1][base : base + modes, :].astype(F32))
 
     def work(r, carry):
@@ -491,7 +511,7 @@
     dma = pltpu.SemaphoreType.DMA
     params = pltpu.CompilerParams(vmem_limit_bytes=VLIM)
     tails = jnp.transpose(conv_tails, (1, 0, 2))
-    blocks = pl.cdiv(tail_len - 2, TB)
+    blocks = pl.cdiv(tail_len - 3, TB)
     chunks = split(blocks)
     table = pltpu.SMEM((engines * (CAP + 1),), jnp.int32)
     tally = pltpu.SMEM((engines,), jnp.int32)
@@ -530,7 +550,7 @@
         functools.partial(lead_body, engines, rows),
         in_specs=[SM, ANY, ANY, VM, VM, VM, ANY],
         out_specs=[VM] * (1 + others),
-        out_shape=[sds((4, rows, width), F32)] + [sds((CAP * (4 + modes), width), BF)] * others,
+        out_shape=[sds((5, rows, width), F32)] + [sds((pl.cdiv(CAP * (3 + modes), 8) * 8, width), BF)] * others,
         scratch_shapes=[
             pltpu.VMEM((taps + 8, width), F32),
             pltpu.VMEM((tail_len, rows, width), BF),
@@ -553,8 +573,8 @@
         in_specs=[SM, ANY, VM],
         out_specs=[VM] * (3 + len(sends)),
         out_shape=[sds((blocks * TB * CAP, width), BF)]
-        + [sds((len(group) * TB * CAP, width), BF) for _, group in sends]
-        + [sds((TB * rows, TB * rows + others * TB * CAP), BF), sds((4, rows, width), F32)],
+        + [sds((CAP * sum(sent_taps(b, tail_len) for b in group), width), BF) for _, group in sends]
+        + [sds((TB * rows, TB * rows + others * TB * CAP), BF), sds((5, rows, width), F32)],
         scratch_shapes=[
             pltpu.VMEM((tail_len, rows, width), BF),
             pltpu.VMEM((others * TB * CAP, TB * rows), BF),
@@ -575,8 +595,8 @@
         functools.partial(mix_body, engines, rows),
         in_specs=[SM] + [VM] * (6 + others) + [ANY] * (1 + len(far)),
         out_specs=[VM, VM],
-        out_shape=[sds((4 * rows, width), BF), sds((4, rows, width), BF)],
-        scratch_shapes=[pltpu.VMEM((4, rows, width), F32), table, tally],
+        out_shape=[sds((4 * rows, width), BF), sds((5, rows, width), BF)],
+        scratch_shapes=[pltpu.VMEM((5, rows, width), F32), table, tally],
         compiler_params=params,
         name="mix",
     )(source, parts, mr_qkv, li_qkv, mr_filter, li_decay, li_residue, *parts_got, spread, *got[0])
@@ -601,7 +621,7 @@
             input_output_aliases={} if tails_so_far is None else {4 + len(arrays): 0},
             scratch_shapes=[buffer, dma((len(group),))]
             if kept
-            else [buffer, pltpu.VMEM((len(group), TB + 2, rows, width), BF), dma((len(group),)), dma((len(group),))],
+            else [buffer, pltpu.VMEM((len(group), TB + 2, rows, width), BF), dma((len(group),)), dma((len(group) + 1,))],
             compiler_params=params,
             name="place",
             cost_estimate=TINY,

time: 74.8 us -> 74.1 us (level)
  waiting for transfers between devices: 15.3 us -> 14.1 us
    ppermute x16, waiting for transfers between devices: 15.3 us -> 14.1 us  [send(): return lax.ppermute(x, 'engine', pairs)]
where the time goes in v5:
time: 74.1 us; the launch traced here: 73.9 us
  Pallas kernels  37.5 us (51%)
  starting transfers between devices  20.6 us (28%)
  waiting for transfers between devices  14.1 us (19%)
  between operations  1.04 us (1%)
  other arithmetic  0.75 us (1%)
    ppermute x16, starting transfers between devices, send(): return lax.ppermute(x, 'engine', pairs)  14.9 us
    ppermute x16, waiting for transfers between devices, send(): return lax.ppermute(x, 'engine', pairs)  14.1 us
    pallas_call x3, Pallas kernels, place(): pl.pallas_call(functools.partial(place_body, engines, rows, group, kept,...  11.5 us
    pallas_call x1, Pallas kernels, body(): pl.pallas_call(functools.partial(lead_body, engines, rows), in_specs=[SM,...  6.82 us
    ppermute x3, starting transfers between devices, body(): lax.ppermute(blocks_out[d], 'chan', [(c, (c + d) % chans) for c in range(...  5.73 us
    pallas_call x1, Pallas kernels, body(): pl.pallas_call(functools.partial(modal_body, engines, rows), in_specs=[SM...  4.42 us
    pallas_call x1, Pallas kernels, body(): pl.pallas_call(functools.partial(pack_body, engines, rows, sends), in_spe...  4.31 us
    pallas_call x1, Pallas kernels, body(): pl.pallas_call(functools.partial(project_body, engines, rows, slots_here,...  4.28 us
  transfers between devices with their start and end apart: 19, of which 8 were waited for; matrix products, arithmetic and copies ran while one was open for 1% of the time, Pallas kernels for 43%

profile of v5, /device:TPU:0, one launch (start us, length us, event | category | flops | bytes accessed | tf_op | source)
XLA Modules:
  0.0 73.9 jit_solution(12775133971543167765)
XLA Ops:
  0.6 0.0 copy-start.7
  0.6 0.0 copy-start.3
  0.7 0.0 copy-start.4
  0.7 0.0 copy-start.2
  0.7 0.0 copy-start
  0.7 2.0 %early.1 = (bf16[64,2048]{1,0:T(8,128)(2,1)S(1)}, bf16[64,2048]{1,0:T(8,128)(2,1)S(1)}) custom-call(s32[64]{0:T(128)} %source.7, bf16[127,16,2048]{2,1,0:T(8,128)(2,1)} %bitcast.3), custom_call_target="tpu_custom_call" | custom-call | tf_op jit(solution)/shard_map/early/pallas_call | solution.py:523
  2.7 2.5 %collective-permute-start.4 = (bf16[64,2048]{1,0:T(8,128)(2,1)S(1)}, bf16[64,2048]{1,0:T(8,128)(2,1)S(1)}, u32[]{:S(2)}, u32[]{:S(2)}) collective-permute-start(bf16[64,2048]{1,0:T(8,128)(2,1)S(1)} %get-tuple-element.47), channel_id=1, source_target_pairs={{0,12},{4,8},{8,4},{12,0},{1,13},{5,9},{9,5},{13,1},{2,14},{6,10},... | collective-permute-start | bytes 786440 | tf_op jit(solution)/shard_map/ppermute | solution.py:40
  5.2 0.6 collective-permute-start.3
  5.8 0.0 copy-done.7
  5.8 0.0 copy-done.3
  5.8 0.0 copy-done.4
  5.8 0.0 copy-done.2
  5.8 0.0 copy-done
  5.8 6.8 %lead.1 = (f32[5,16,2048]{2,1,0:T(8,128)S(1)}, bf16[40,2048]{1,0:T(8,128)(2,1)S(1)}, bf16[40,2048]{1,0:T(8,128)(2,1)S(1)}, bf16[40,2048]{1,0:T(8,128)(2,1)S(1)}) custom-call(s32[64]{0:T(128)S(1)} %copy-done.7, bf16[127,16,2048]{2,1,0:T(8,128)(2,1)} %bitcast.4, f32[16,16,2048]{2,1,0:T(8,128)S(1)} %copy-done, bf16[128,2048]{1,0:T(8,128)(2,1)S(1)} %copy-done.2, ...), custom_call_target="tpu_custom_call" | custom-call | tf_op jit(solution)/shard_map/lead/pallas_call | solution.py:549
  12.7 0.1 collective-permute-start
  12.8 1.7 %collective-permute-start.1 = (bf16[40,2048]{1,0:T(8,128)(2,1)S(1)}, bf16[40,2048]{1,0:T(8,128)(2,1)S(1)}, u32[]{:S(2)}, u32[]{:S(2)}) collective-permute-start(bf16[40,2048]{1,0:T(8,128)(2,1)S(1)} %get-tuple-element.44), channel_id=1, source_target_pairs={{0,8},{4,12},{8,0},{12,4},{1,9},{5,13},{9,1},{13,5},{2,10},{6,14},... | collective-permute-start | bytes 491528 | tf_op jit(solution)/shard_map/ppermute | solution.py:40
  14.5 0.1 collective-permute-start.2
  14.6 4.3 %pack.1 = (bf16[256,2048]{1,0:T(8,128)(2,1)S(1)}, bf16[96,2048]{1,0:T(8,128)(2,1)S(1)}, bf16[96,2048]{1,0:T(8,128)(2,1)S(1)}, bf16[88,2048]{1,0:T(8,128)(2,1)S(1...) custom-call(s32[64]{0:T(128)S(1)} %copy-done.7, ...), custom_call_target="tpu_custom_call" | custom-call | tf_op jit(solution)/shard_map/pack/pallas_call | solution.py:571
  18.9 0.0 collective-permute-done.refs_0_
  18.9 3.1 %collective-permute-done.1.refs_1_ = bf16[40,2048]{1,0:T(8,128)(2,1)S(1)} collective-permute-done((bf16[40,2048]{1,0:T(8,128)(2,1)S(1)}, bf16[40,2048]{1,0:T(8,128)(2,1)S(1)}, u32[]{:S(2)}, u32[]{:S(2)}) %collective-permute-start.1) | collective-permute-done | bytes 163872 | tf_op jit(solution)/shard_map/ppermute | solution.py:40
  22.0 2.5 %collective-permute-done.2.refs_2_ = bf16[40,2048]{1,0:T(8,128)(2,1)S(1)} collective-permute-done((bf16[40,2048]{1,0:T(8,128)(2,1)S(1)}, bf16[40,2048]{1,0:T(8,128)(2,1)S(1)}, u32[]{:S(2)}, u32[]{:S(2)}) %collective-permute-start.2) | collective-permute-done | bytes 163872 | tf_op jit(solution)/shard_map/ppermute | solution.py:40
  24.5 0.0 collective-permute-done.4.refs_5_.refs_1_
  24.5 0.0 collective-permute-done.3.refs_4_.refs_0_
  24.5 0.0 copy-done.5
  24.5 1.4 %mix.1 = (bf16[64,2048]{1,0:T(8,128)(2,1)S(1)}, bf16[5,16,2048]{2,1,0:T(8,128)(2,1)S(1)}) custom-call(s32[64]{0:T(128)S(1)} %copy-done.7, f32[5,16,2048]{2,1,0:T(8,128)S(1)} %get-tuple-element.42.parts_in, bf16[2,3,16,2048]{3,2,1,0:T(8,128)(2,1)S(1)} %copy-done.5, bf16[2,3,16,2048]{3,2,1,0:T(8,128)(2,1)S(1)} %copy-done.6, bf16[128,2048]{1,0:T(8,128)(2,1)S(1)} %copy-done.2, ...), custom_call_target="tpu_custom_call" | custom-call | tf_op jit(solution)/shard_map/mix/pallas_call | solution.py:594
  26.0 0.2 collective-permute-start.8
  26.1 0.4 collective-permute-start.5
  26.6 2.5 %collective-permute-start.6 = (bf16[64,2048]{1,0:T(8,128)(2,1)S(1)}, bf16[64,2048]{1,0:T(8,128)(2,1)S(1)}, u32[]{:S(2)}, u32[]{:S(2)}) collective-permute-start(bf16[64,2048]{1,0:T(8,128)(2,1)S(1)} %get-tuple-element.49.refs_0_), channel_id=1, source_target_pairs={{0,8},{4,12},{8,0},{12,4},{1,9},{5,13},{9,1},{13,5},{2,10},{6,14},... | collective-permute-start | bytes 786440 | tf_op jit(solution)/shard_map/ppermute | solution.py:40
  29.0 0.1 collective-permute-done.5.refs_1_
  29.1 2.5 %collective-permute-start.12 = (bf16[96,2048]{1,0:T(8,128)(2,1)S(1)}, bf16[96,2048]{1,0:T(8,128)(2,1)S(1)}, u32[]{:S(2)}, u32[]{:S(2)}) collective-permute-start(bf16[96,2048]{1,0:T(8,128)(2,1)S(1)} %get-tuple-element.62), channel_id=1, source_target_pairs={{0,8},{4,12},{8,0},{12,4},{1,9},{5,13},{9,1},{13,5},{2,10},{6,14},... | collective-permute-start | bytes 1179656 | tf_op jit(solution)/shard_map/ppermute | solution.py:40
  31.5 0.0 collective-permute-start.13
  31.5 4.6 %collective-permute-done.6.refs_2_ = bf16[64,2048]{1,0:T(8,128)(2,1)S(1)} collective-permute-done((bf16[64,2048]{1,0:T(8,128)(2,1)S(1)}, bf16[64,2048]{1,0:T(8,128)(2,1)S(1)}, u32[]{:S(2)}, u32[]{:S(2)}) %collective-permute-start.6) | collective-permute-done | bytes 262176 | tf_op jit(solution)/shard_map/ppermute | solution.py:40
  36.1 0.0 collective-permute-start.7
  36.1 0.0 collective-permute-done.8.near
  36.1 3.8 %place.3.refs_6_.refs_2_ = bf16[127,16,2048]{2,1,0:T(8,128)(2,1)} custom-call(bf16[256,352]{1,0:T(8,128)(2,1)S(1)} %get-tuple-element.46.refs_3_.spread, bf16[5,16,2048]{2,1,0:T(8,128)(2,1)S(1)} %get-tuple-element.53.gates.refs_2_, bf16[127,16,2048]{2,1,0:T(8,128)(2,1)} %bitcast.6, bf16[256,2048]{1,0:T(8,128)(2,1)S(1)} %collective-permute-done.8.near, ...), custom_call_target="tpu_custom_call" | custom-call | flops 1 | bytes 1 | tf_op jit(solution)/shard_map/place/pallas_call | solution.py:616
  39.9 0.0 collective-permute-done.7.refs_3_
  39.9 4.3 %project.1 = (bf16[32,1024]{1,0:T(8,128)(2,1)S(1)}, bf16[32,1024]{1,0:T(8,128)(2,1)S(1)}, bf16[32,1024]{1,0:T(8,128)(2,1)S(1)}, bf16[32,1024]{1,0:T(8,128)(2,1)S(1)}) custom-call(bf16[64,2048]{1,0:T(8,128)(2,1)S(1)} %get-tuple-element.49.refs_0_, bf16[64,2048]{1,0:T(8,128)(2,1)S(1)} %collective-permute-done.5.refs_1_, ...), custom_call_target="tpu_custom_call" | custom-call | tf_op jit(solution)/shard_map/project/pallas_call | solution.py:632
  44.2 0.0 copy-start.8
  44.2 0.0 copy-start.9
  44.2 0.6 collective-permute-start.9
  44.8 2.1 %collective-permute-start.10 = (bf16[32,1024]{1,0:T(8,128)(2,1)S(1)}, bf16[32,1024]{1,0:T(8,128)(2,1)S(1)}, u32[]{:S(2)}, u32[]{:S(2)}) collective-permute-start(bf16[32,1024]{1,0:T(8,128)(2,1)S(1)} %get-tuple-element.58), channel_id=1, source_target_pairs={{0,8},{4,12},{8,0},{12,4},{1,9},{5,13},{9,1},{13,5},{2,10},{6,14},... | collective-permute-start | bytes 196616 | tf_op jit(solution)/shard_map/ppermute | solution.py:40
  46.9 0.0 collective-permute-start.11
  46.9 4.4 %modal.1 = f32[16,16,2048]{2,1,0:T(8,128)} custom-call(s32[64]{0:T(128)S(1)} %copy-done.7, f32[16,16,2048]{2,1,0:T(8,128)S(1)} %copy-done, bf16[5,16,2048]{2,1,0:T(8,128)(2,1)S(1)} %get-tuple-element.53.gates.refs_2_, f32[16,2048]{1,0:T(8,128)S(1)} %copy-done.3, bf16[40,2048]{1,0:T(8,128)(2,1)S(1)} %collective-permute-done.refs_0_, ...), custom_call_target="tpu_custom_call" | custom-call | flops 1 | bytes 1 | tf_op jit(solution)/shard_map/modal/pallas_call | solution.py:653
  51.3 0.0 collective-permute-done.12.refs_4_.refs_0_
  51.3 1.2 %collective-permute-done.13.refs_5_.refs_1_ = bf16[96,2048]{1,0:T(8,128)(2,1)S(1)} collective-permute-done((bf16[96,2048]{1,0:T(8,128)(2,1)S(1)}, bf16[96,2048]{1,0:T(8,128)(2,1)S(1)}, u32[]{:S(2)}, u32[]{:S(2)}) %collective-permute-start.13) | collective-permute-done | bytes 393248 | tf_op jit(solution)/shard_map/ppermute | solution.py:40
  52.5 0.8 %collective-permute-start.17 = (bf16[88,2048]{1,0:T(8,128)(2,1)S(1)}, bf16[88,2048]{1,0:T(8,128)(2,1)S(1)}, u32[]{:S(2)}, u32[]{:S(2)}) collective-permute-start(bf16[88,2048]{1,0:T(8,128)(2,1)S(1)} %get-tuple-element.70), channel_id=1, source_target_pairs={{0,8},{4,12},{8,0},{12,4},{1,9},{5,13},{9,1},{13,5},{2,10},{6,14},... | collective-permute-start | bytes 1081352 | tf_op jit(solution)/shard_map/ppermute | solution.py:40
  53.4 0.0 collective-permute-done.9.refs_1_
  53.4 1.0 %collective-permute-done.10.refs_2_ = bf16[32,1024]{1,0:T(8,128)(2,1)S(1)} collective-permute-done((bf16[32,1024]{1,0:T(8,128)(2,1)S(1)}, bf16[32,1024]{1,0:T(8,128)(2,1)S(1)}, u32[]{:S(2)}, u32[]{:S(2)}) %collective-permute-start.10) | collective-permute-done | bytes 65568 | tf_op jit(solution)/shard_map/ppermute | solution.py:40
  54.4 0.4 collective-permute-done.11.refs_3_
  54.7 0.7 sort.1
  55.4 1.8 %collective-permute-start.14 = (bf16[32,1024]{1,0:T(8,128)(2,1)S(1)}, bf16[32,1024]{1,0:T(8,128)(2,1)S(1)}, u32[]{:S(2)}, u32[]{:S(2)}) collective-permute-start(bf16[32,1024]{1,0:T(8,128)(2,1)S(1)} %get-tuple-element.67), channel_id=1, source_target_pairs={{0,1},{1,2},{2,3},{3,0},{4,5},{5,6},{6,7},{7,4},{8,9},{9,10},{10,1... | collective-permute-start | bytes 196616 | tf_op jit(solution)/shard_map/ppermute | solution.py:685
  57.2 2.6 %collective-permute-start.15 = (bf16[32,1024]{1,0:T(8,128)(2,1)S(1)}, bf16[32,1024]{1,0:T(8,128)(2,1)S(1)}, u32[]{:S(2)}, u32[]{:S(2)}) collective-permute-start(bf16[32,1024]{1,0:T(8,128)(2,1)S(1)} %get-tuple-element.68), channel_id=1, source_target_pairs={{0,2},{1,3},{2,0},{3,1},{4,6},{5,7},{6,4},{7,5},{8,10},{9,11},{10,... | collective-permute-start | bytes 196616 | tf_op jit(solution)/shard_map/ppermute | solution.py:685
  59.8 1.3 %collective-permute-start.16 = (bf16[32,1024]{1,0:T(8,128)(2,1)S(1)}, bf16[32,1024]{1,0:T(8,128)(2,1)S(1)}, u32[]{:S(2)}, u32[]{:S(2)}) collective-permute-start(bf16[32,1024]{1,0:T(8,128)(2,1)S(1)} %get-tuple-element.69), channel_id=1, source_target_pairs={{0,3},{1,0},{2,1},{3,2},{4,7},{5,4},{6,5},{7,6},{8,11},{9,8},{10,9... | collective-permute-start | bytes 196616 | tf_op jit(solution)/shard_map/ppermute | solution.py:685
  61.1 0.0 copy-done.9
  61.1 0.9 %collective-permute-start.18 = (bf16[88,2048]{1,0:T(8,128)(2,1)S(1)}, bf16[88,2048]{1,0:T(8,128)(2,1)S(1)}, u32[]{:S(2)}, u32[]{:S(2)}) collective-permute-start(bf16[88,2048]{1,0:T(8,128)(2,1)S(1)} %get-tuple-element.73), channel_id=1, source_target_pairs={{0,12},{4,8},{8,4},{12,0},{1,13},{5,9},{9,5},{13,1},{2,14},{6,10},... | collective-permute-start | bytes 1081352 | tf_op jit(solution)/shard_map/ppermute | solution.py:40
  62.0 4.3 %place.5._ = bf16[127,16,2048]{2,1,0:T(8,128)(2,1)} custom-call(bf16[256,352]{1,0:T(8,128)(2,1)S(1)} %get-tuple-element.46.refs_3_.spread, bf16[5,16,2048]{2,1,0:T(8,128)(2,1)S(1)} %get-tuple-element.53.gates.refs_2_, bf16[127,16,2048]{2,1,0:T(8,128)(2,1)} %bitcast.7, ...), custom_call_target="tpu_custom_call", output_to_operand_aliasing={{}: (6, {})} | custom-call | flops 1 | bytes 1 | tf_op jit(solution)/shard_map/place/pallas_call | solution.py:616
  66.3 0.0 collective-permute-done.14
  66.4 0.0 collective-permute-done.15
  66.4 0.0 collective-permute-done.16
  66.4 0.0 collective-permute-done.17.refs_0_
  66.4 3.4 %place.4.base = bf16[3,16,16,2048]{3,2,1,0:T(8,128)(2,1)S(1)} custom-call(bf16[256,352]{1,0:T(8,128)(2,1)S(1)} %get-tuple-element.46.refs_3_.spread, bf16[5,16,2048]{2,1,0:T(8,128)(2,1)S(1)} %get-tuple-element.53.gates.refs_2_, bf16[127,16,2048]{2,1,0:T(8,128)(2,1)} %bitcast.8, bf16[256,2048]{1,0:T(8,128)(2,1)S(1)} %collective-permute-done.8.near, ...), custom_call_target="tpu_custom_call" | custom-call | flops 1 | bytes 1 | tf_op jit(solution)/shard_map/place/pallas_call | solution.py:616
  69.8 0.7 multiply_convert_fusion
  70.5 1.2 %collective-permute-done.18.msg = bf16[88,2048]{1,0:T(8,128)(2,1)S(1)} collective-permute-done((bf16[88,2048]{1,0:T(8,128)(2,1)S(1)}, bf16[88,2048]{1,0:T(8,128)(2,1)S(1)}, u32[]{:S(2)}, u32[]{:S(2)}) %collective-permute-start.18) | collective-permute-done | bytes 360480 | tf_op jit(solution)/shard_map/ppermute | solution.py:40
  71.7 2.1 %last.1 = bf16[127,16,2048]{2,1,0:T(8,128)(2,1)} custom-call(bf16[256,352]{1,0:T(8,128)(2,1)S(1)} %get-tuple-element.46.refs_3_.spread, bf16[3,16,16,2048]{3,2,1,0:T(8,128)(2,1)S(1)} %place.4.base, bf16[88,2048]{1,0:T(8,128)(2,1)S(1)} %collective-permute-done.18.msg, bf16[127,16,2048]{2,1,0:T(8,128)(2,1)} %place.5._), custom_call_target="tpu_custom_call", output_to_operand_aliasing={{}: (3, {})} | custom-call | flops 1 | bytes 1 | tf_op jit(solution)/shard_map/last/pallas_call | solution.py:694
  (8 shorter events, 0.1 us)
Async XLA Ops:
  0.6 5.2 %copy-start.7 = (s32[64]{0:T(128)S(1)}, s32[64]{0:T(128)}, u32[]{:S(2)}) copy-start(s32[64]{0:T(128)} %source.7) | copy-start | bytes 772
  0.6 5.2 %copy-start.3 = (f32[16,2048]{1,0:T(8,128)S(1)}, f32[16,2048]{1,0:T(8,128)}, u32[]{:S(2)}) copy-start(f32[16,2048]{1,0:T(8,128)} %decay.5) | copy-start | bytes 393220
  0.7 5.2 %copy-start.4 = (f32[16,2048]{1,0:T(8,128)S(1)}, f32[16,2048]{1,0:T(8,128)}, u32[]{:S(2)}) copy-start(f32[16,2048]{1,0:T(8,128)} %resid.3) | copy-start | bytes 393220
  0.7 5.2 %copy-start.2 = (bf16[128,2048]{1,0:T(8,128)(2,1)S(1)}, bf16[128,2048]{1,0:T(8,128)(2,1)}, u32[]{:S(2)}) copy-start(bf16[128,2048]{1,0:T(8,128)(2,1)} %filt.3) | copy-start | bytes 1572868
  0.7 5.2 %copy-start = (f32[16,16,2048]{2,1,0:T(8,128)S(1)}, f32[16,16,2048]{2,1,0:T(8,128)}, u32[]{:S(2)}) copy-start(f32[16,16,2048]{2,1,0:T(8,128)} %states.3) | copy-start | bytes 6291460
  2.7 21.8 %collective-permute-start.4 = (bf16[64,2048]{1,0:T(8,128)(2,1)S(1)}, bf16[64,2048]{1,0:T(8,128)(2,1)S(1)}, u32[]{:S(2)}, u32[]{:S(2)}) collective-permute-start(bf16[64,2048]{1,0:T(8,128)(2,1)S(1)} %get-tuple-element.47), channel_id=1, source_target_pairs={{0,12},{4,8},{8,4},{12,0},{1,13},{5,9},{9,5},{13,1},{2,14},{6,10},... | collective-permute-start | bytes 786440 | tf_op jit(solution)/shard_map/ppermute | solution.py:40
  5.2 19.3 %collective-permute-start.3 = (bf16[64,2048]{1,0:T(8,128)(2,1)S(1)}, bf16[64,2048]{1,0:T(8,128)(2,1)S(1)}, u32[]{:S(2)}, u32[]{:S(2)}) collective-permute-start(bf16[64,2048]{1,0:T(8,128)(2,1)S(1)} %get-tuple-element.39._), channel_id=1, source_target_pairs={{0,8},{4,12},{8,0},{12,4},{1,9},{5,13},{9,1},{13,5},{2,10},{6,14},... | collective-permute-start | bytes 786440 | tf_op jit(solution)/shard_map/ppermute | solution.py:40
  12.7 6.3 %collective-permute-start = (bf16[40,2048]{1,0:T(8,128)(2,1)S(1)}, bf16[40,2048]{1,0:T(8,128)(2,1)S(1)}, u32[]{:S(2)}, u32[]{:S(2)}) collective-permute-start(bf16[40,2048]{1,0:T(8,128)(2,1)S(1)} %get-tuple-element.43), channel_id=1, source_target_pairs={{0,4},{4,0},{8,12},{12,8},{1,5},{5,1},{9,13},{13,9},{2,6},{6,2},{1... | collective-permute-start | bytes 491528 | tf_op jit(solution)/shard_map/ppermute | solution.py:40
  12.8 9.2 %collective-permute-start.1 = (bf16[40,2048]{1,0:T(8,128)(2,1)S(1)}, bf16[40,2048]{1,0:T(8,128)(2,1)S(1)}, u32[]{:S(2)}, u32[]{:S(2)}) collective-permute-start(bf16[40,2048]{1,0:T(8,128)(2,1)S(1)} %get-tuple-element.44), channel_id=1, source_target_pairs={{0,8},{4,12},{8,0},{12,4},{1,9},{5,13},{9,1},{13,5},{2,10},{6,14},... | collective-permute-start | bytes 491528 | tf_op jit(solution)/shard_map/ppermute | solution.py:40
  14.5 10.0 %collective-permute-start.2 = (bf16[40,2048]{1,0:T(8,128)(2,1)S(1)}, bf16[40,2048]{1,0:T(8,128)(2,1)S(1)}, u32[]{:S(2)}, u32[]{:S(2)}) collective-permute-start(bf16[40,2048]{1,0:T(8,128)(2,1)S(1)} %get-tuple-element.45), channel_id=1, source_target_pairs={{0,12},{4,8},{8,4},{12,0},{1,13},{5,9},{9,5},{13,1},{2,14},{6,10},... | collective-permute-start | bytes 491528 | tf_op jit(solution)/shard_map/ppermute | solution.py:40
  14.6 9.9 %copy-start.5 = (bf16[2,3,16,2048]{3,2,1,0:T(8,128)(2,1)S(1)}, bf16[2,3,16,2048]{3,2,1,0:T(8,128)(2,1)}, u32[]{:S(2)}) copy-start(bf16[2,3,16,2048]{3,2,1,0:T(8,128)(2,1)} %mr.1) | copy-start | bytes 1179652
  14.6 9.9 %copy-start.6 = (bf16[2,3,16,2048]{3,2,1,0:T(8,128)(2,1)S(1)}, bf16[2,3,16,2048]{3,2,1,0:T(8,128)(2,1)}, u32[]{:S(2)}) copy-start(bf16[2,3,16,2048]{3,2,1,0:T(8,128)(2,1)} %li.1) | copy-start | bytes 1179652
  26.0 10.1 %collective-permute-start.8 = (bf16[256,2048]{1,0:T(8,128)(2,1)S(1)}, bf16[256,2048]{1,0:T(8,128)(2,1)S(1)}, u32[]{:S(2)}, u32[]{:S(2)}) collective-permute-start(bf16[256,2048]{1,0:T(8,128)(2,1)S(1)} %get-tuple-element.54), channel_id=1, source_target_pairs={{0,4},{4,0},{8,12},{12,8},{1,5},{5,1},{9,13},{13,9},{2,6},{6,2},{1... | collective-permute-start | bytes 3145736 | tf_op jit(solution)/shard_map/ppermute | solution.py:40
  26.1 2.9 %collective-permute-start.5 = (bf16[64,2048]{1,0:T(8,128)(2,1)S(1)}, bf16[64,2048]{1,0:T(8,128)(2,1)S(1)}, u32[]{:S(2)}, u32[]{:S(2)}) collective-permute-start(bf16[64,2048]{1,0:T(8,128)(2,1)S(1)} %get-tuple-element.49.refs_0_), channel_id=1, source_target_pairs={{0,4},{4,0},{8,12},{12,8},{1,5},{5,1},{9,13},{13,9},{2,6},{6,2},{1... | collective-permute-start | bytes 786440 | tf_op jit(solution)/shard_map/ppermute | solution.py:40
  26.6 9.5 %collective-permute-start.6 = (bf16[64,2048]{1,0:T(8,128)(2,1)S(1)}, bf16[64,2048]{1,0:T(8,128)(2,1)S(1)}, u32[]{:S(2)}, u32[]{:S(2)}) collective-permute-start(bf16[64,2048]{1,0:T(8,128)(2,1)S(1)} %get-tuple-element.49.refs_0_), channel_id=1, source_target_pairs={{0,8},{4,12},{8,0},{12,4},{1,9},{5,13},{9,1},{13,5},{2,10},{6,14},... | collective-permute-start | bytes 786440 | tf_op jit(solution)/shard_map/ppermute | solution.py:40
  29.1 22.2 %collective-permute-start.12 = (bf16[96,2048]{1,0:T(8,128)(2,1)S(1)}, bf16[96,2048]{1,0:T(8,128)(2,1)S(1)}, u32[]{:S(2)}, u32[]{:S(2)}) collective-permute-start(bf16[96,2048]{1,0:T(8,128)(2,1)S(1)} %get-tuple-element.62), channel_id=1, source_target_pairs={{0,8},{4,12},{8,0},{12,4},{1,9},{5,13},{9,1},{13,5},{2,10},{6,14},... | collective-permute-start | bytes 1179656 | tf_op jit(solution)/shard_map/ppermute | solution.py:40
  31.5 21.0 %collective-permute-start.13 = (bf16[96,2048]{1,0:T(8,128)(2,1)S(1)}, bf16[96,2048]{1,0:T(8,128)(2,1)S(1)}, u32[]{:S(2)}, u32[]{:S(2)}) collective-permute-start(bf16[96,2048]{1,0:T(8,128)(2,1)S(1)} %get-tuple-element.63), channel_id=1, source_target_pairs={{0,12},{4,8},{8,4},{12,0},{1,13},{5,9},{9,5},{13,1},{2,14},{6,10},... | collective-permute-start | bytes 1179656 | tf_op jit(solution)/shard_map/ppermute | solution.py:40
  36.1 3.8 %collective-permute-start.7 = (bf16[64,2048]{1,0:T(8,128)(2,1)S(1)}, bf16[64,2048]{1,0:T(8,128)(2,1)S(1)}, u32[]{:S(2)}, u32[]{:S(2)}) collective-permute-start(bf16[64,2048]{1,0:T(8,128)(2,1)S(1)} %collective-permute-done.6.refs_2_), channel_id=1, source_target_pairs={{0,4},{4,0},{8,12},{12,8},{1,5},{5,1},{9,13},{13,9},{2,6},{6,2},{1... | collective-permute-start | bytes 786440 | tf_op jit(solution)/shard_map/ppermute | solution.py:40
  36.1 3.8 %copy-start.1 = (bf16[2,2048,512]{2,1,0:T(8,128)(2,1)S(1)}, bf16[2,2048,512]{2,1,0:T(8,128)(2,1)}, u32[]{:S(2)}) copy-start(bf16[2,2048,512]{2,1,0:T(8,128)(2,1)} %refs_4_.1) | copy-start | bytes 12582916
  44.2 10.5 %copy-start.8 = (s32[8]{0:T(128)S(1)}, s32[8]{0:T(128)}, u32[]{:S(2)}) copy-start(s32[8]{0:T(128)} %slot_of.1) | copy-start | bytes 100
  44.2 16.9 %copy-start.9 = (s32[16]{0:T(128)S(1)}, s32[16]{0:T(128)}, u32[]{:S(2)}) copy-start(s32[16]{0:T(128)} %param.17) | copy-start | bytes 196
  44.2 9.1 %collective-permute-start.9 = (bf16[32,1024]{1,0:T(8,128)(2,1)S(1)}, bf16[32,1024]{1,0:T(8,128)(2,1)S(1)}, u32[]{:S(2)}, u32[]{:S(2)}) collective-permute-start(bf16[32,1024]{1,0:T(8,128)(2,1)S(1)} %get-tuple-element.56), channel_id=1, source_target_pairs={{0,4},{4,0},{8,12},{12,8},{1,5},{5,1},{9,13},{13,9},{2,6},{6,2},{1... | collective-permute-start | bytes 196616 | tf_op jit(solution)/shard_map/ppermute | solution.py:40
  44.8 9.6 %collective-permute-start.10 = (bf16[32,1024]{1,0:T(8,128)(2,1)S(1)}, bf16[32,1024]{1,0:T(8,128)(2,1)S(1)}, u32[]{:S(2)}, u32[]{:S(2)}) collective-permute-start(bf16[32,1024]{1,0:T(8,128)(2,1)S(1)} %get-tuple-element.58), channel_id=1, source_target_pairs={{0,8},{4,12},{8,0},{12,4},{1,9},{5,13},{9,1},{13,5},{2,10},{6,14},... | collective-permute-start | bytes 196616 | tf_op jit(solution)/shard_map/ppermute | solution.py:40
  46.9 7.9 %collective-permute-start.11 = (bf16[32,1024]{1,0:T(8,128)(2,1)S(1)}, bf16[32,1024]{1,0:T(8,128)(2,1)S(1)}, u32[]{:S(2)}, u32[]{:S(2)}) collective-permute-start(bf16[32,1024]{1,0:T(8,128)(2,1)S(1)} %get-tuple-element.59), channel_id=1, source_target_pairs={{0,12},{4,8},{8,4},{12,0},{1,13},{5,9},{9,5},{13,1},{2,14},{6,10},... | collective-permute-start | bytes 196616 | tf_op jit(solution)/shard_map/ppermute | solution.py:40
  52.5 13.9 %collective-permute-start.17 = (bf16[88,2048]{1,0:T(8,128)(2,1)S(1)}, bf16[88,2048]{1,0:T(8,128)(2,1)S(1)}, u32[]{:S(2)}, u32[]{:S(2)}) collective-permute-start(bf16[88,2048]{1,0:T(8,128)(2,1)S(1)} %get-tuple-element.70), channel_id=1, source_target_pairs={{0,8},{4,12},{8,0},{12,4},{1,9},{5,13},{9,1},{13,5},{2,10},{6,14},... | collective-permute-start | bytes 1081352 | tf_op jit(solution)/shard_map/ppermute | solution.py:40
  55.4 10.9 %collective-permute-start.14 = (bf16[32,1024]{1,0:T(8,128)(2,1)S(1)}, bf16[32,1024]{1,0:T(8,128)(2,1)S(1)}, u32[]{:S(2)}, u32[]{:S(2)}) collective-permute-start(bf16[32,1024]{1,0:T(8,128)(2,1)S(1)} %get-tuple-element.67), channel_id=1, source_target_pairs={{0,1},{1,2},{2,3},{3,0},{4,5},{5,6},{6,7},{7,4},{8,9},{9,10},{10,1... | collective-permute-start | bytes 196616 | tf_op jit(solution)/shard_map/ppermute | solution.py:685
  57.2 9.2 %collective-permute-start.15 = (bf16[32,1024]{1,0:T(8,128)(2,1)S(1)}, bf16[32,1024]{1,0:T(8,128)(2,1)S(1)}, u32[]{:S(2)}, u32[]{:S(2)}) collective-permute-start(bf16[32,1024]{1,0:T(8,128)(2,1)S(1)} %get-tuple-element.68), channel_id=1, source_target_pairs={{0,2},{1,3},{2,0},{3,1},{4,6},{5,7},{6,4},{7,5},{8,10},{9,11},{10,... | collective-permute-start | bytes 196616 | tf_op jit(solution)/shard_map/ppermute | solution.py:685
  59.8 6.6 %collective-permute-start.16 = (bf16[32,1024]{1,0:T(8,128)(2,1)S(1)}, bf16[32,1024]{1,0:T(8,128)(2,1)S(1)}, u32[]{:S(2)}, u32[]{:S(2)}) collective-permute-start(bf16[32,1024]{1,0:T(8,128)(2,1)S(1)} %get-tuple-element.69), channel_id=1, source_target_pairs={{0,3},{1,0},{2,1},{3,2},{4,7},{5,4},{6,5},{7,6},{8,11},{9,8},{10,9... | collective-permute-start | bytes 196616 | tf_op jit(solution)/shard_map/ppermute | solution.py:685
  61.1 10.6 %collective-permute-start.18 = (bf16[88,2048]{1,0:T(8,128)(2,1)S(1)}, bf16[88,2048]{1,0:T(8,128)(2,1)S(1)}, u32[]{:S(2)}, u32[]{:S(2)}) collective-permute-start(bf16[88,2048]{1,0:T(8,128)(2,1)S(1)} %get-tuple-element.73), channel_id=1, source_target_pairs={{0,12},{4,8},{8,4},{12,0},{1,13},{5,9},{9,5},{13,1},{2,14},{6,10},... | collective-permute-start | bytes 1081352 | tf_op jit(solution)/shard_map/ppermute | solution.py:40

commit v6 on v5

--- a/solution.py
+++ b/solution.py
@@ -181,7 +181,7 @@
     far = list(range(2, engines))
     near = refs[0]
     msgs = refs[1 : 1 + len(sends)]
-    spread, parts, tbuf, pick, leave, slots, found, tsem = refs[1 + len(msgs) :]
+    spread, parts, slots, found, tbuf, pick, leave, tsem = refs[1 + len(msgs) :]
     tail_len, _, width = tails.shape
     chunk = wide_chunk(width)
     me = lax.axis_index("engine")
@@ -243,14 +243,12 @@
         found[rel] = at + 1
 
 
-def mix_body(engines, rows, source, parts_in, mr, li, filt, decay, resid, *refs):
+def mix_body(engines, rows, slots, found, parts_in, mr, li, filt, decay, resid, *refs):
     got = refs[: engines - 1]
-    y, gates, parts, slots, found = refs[-5:]
+    y, gates, parts = refs[-3:]
     width = y.shape[1]
     modes = decay.shape[0]
     chunk = lane_chunk(width)
-    me = lax.axis_index("engine")
-    arrivals(engines, rows, source, slots, found, me)
 
     parts[...] = parts_in[...]
     for rel in range(1, engines):
@@ -262,8 +260,8 @@
                 for n, i in enumerate((0, 1, 4)):
                     at = CAP * modes + 3 * j + n
                     parts[i, one, :] = got[rel - 1][at : at + 1, :].astype(F32)
-                for c in range(0, width, chunk):
-                    cols = pl.ds(c, chunk)
+                for c in range(0, width, wide_chunk(width)):
+                    cols = pl.ds(c, wide_chunk(width))
                     d = decay[:, cols]
                     a = resid[:, cols] * (d * got[rel - 1][j * modes : (j + 1) * modes, cols].astype(F32))
                     parts[2, one, cols] = jnp.sum(a, axis=0, keepdims=True)
@@ -432,11 +430,11 @@
         store(n).wait()
 
 
-def modal_body(engines, rows, source, states, gates, decay, *refs):
+def modal_body(engines, rows, source, slots, found, states, gates, decay, *refs):
     others = engines - 1
     msgs = refs[:others]
     new_states = refs[others]
-    sbuf, z, slots, found, isem, osem = refs[others + 1 :]
+    sbuf, z, isem, osem = refs[others + 1 :]
     modes = states.shape[1]
     me = lax.axis_index("engine")
 
@@ -458,7 +456,6 @@
 
     lax.fori_loop(0, rows, begin, 0)
     z[...] = gates[2:4].astype(F32)
-    arrivals(engines, rows, source, slots, found, me)
 
     def advance(r, s):
         d = decay[...]
@@ -571,35 +568,34 @@
     packed = pl.pallas_call(
         functools.partial(pack_body, engines, rows, sends),
         in_specs=[SM, ANY, VM],
-        out_specs=[VM] * (3 + len(sends)),
+        out_specs=[VM] * (3 + len(sends)) + [SM, SM],
         out_shape=[sds((blocks * TB * CAP, width), BF)]
         + [sds((CAP * sum(sent_taps(b, tail_len) for b in group), width), BF) for _, group in sends]
-        + [sds((TB * rows, TB * rows + others * TB * CAP), BF), sds((5, rows, width), F32)],
+        + [sds((TB * rows, TB * rows + others * TB * CAP), BF), sds((5, rows, width), F32)]
+        + [sds((engines * (CAP + 1),), jnp.int32), sds((engines,), jnp.int32)],
         scratch_shapes=[
             pltpu.VMEM((tail_len, rows, width), BF),
             pltpu.VMEM((others * TB * CAP, TB * rows), BF),
             table,
-            table,
-            tally,
             dma((blocks,)),
         ],
         compiler_params=params,
         name="pack",
     )(source, tails, lead[0])
     near_msg = packed[0]
-    spread, parts = packed[-2:]
+    spread, parts, arrive_slots, arrive_counts = packed[-4:]
     msgs[1] = packed[1 : 1 + len(far)]
     msgs[2] = packed[1 + len(far) : 1 + 2 * len(far)]
 
     y, gates = pl.pallas_call(
         functools.partial(mix_body, engines, rows),
-        in_specs=[SM] + [VM] * (6 + others) + [ANY] * (1 + len(far)),
+        in_specs=[SM, SM] + [VM] * (6 + others) + [ANY] * (1 + len(far)),
         out_specs=[VM, VM],
         out_shape=[sds((4 * rows, width), BF), sds((5, rows, width), BF)],
-        scratch_shapes=[pltpu.VMEM((5, rows, width), F32), table, tally],
+        scratch_shapes=[pltpu.VMEM((5, rows, width), F32)],
         compiler_params=params,
         name="mix",
-    )(source, parts, mr_qkv, li_qkv, mr_filter, li_decay, li_residue, *parts_got, spread, *got[0])
+    )(arrive_slots, arrive_counts, parts, mr_qkv, li_qkv, mr_filter, li_decay, li_residue, *parts_got, spread, *got[0])
 
     near_msg, y = lax.optimization_barrier((near_msg, y))
     near_got = send(near_msg, engines, 0, 1)
@@ -652,21 +648,19 @@
 
     new_states = pl.pallas_call(
         functools.partial(modal_body, engines, rows),
-        in_specs=[SM, ANY, VM, VM] + [VM] * others,
+        in_specs=[SM, SM, SM, ANY, VM, VM] + [VM] * others,
         out_specs=ANY,
         out_shape=sds((rows, modes, width), F32),
         scratch_shapes=[
             pltpu.VMEM((rows, modes, width), F32),
             pltpu.VMEM((2, rows, width), F32),
-            table,
-            tally,
             dma((rows,)),
             dma((rows,)),
         ],
         compiler_params=params,
         name="modal",
         cost_estimate=TINY,
-    )(source, modal_states, gates, li_decay, *parts_got)
+    )(source, arrive_slots, arrive_counts, modal_states, gates, li_decay, *parts_got)
 
     back[1], new_states = lax.optimization_barrier((back[1], new_states))
     per_chan = panel_slot.shape[0] // chans

time: 74.1 us -> 73.8 us (level)
  transfers between devices with their start and end apart: 19 -> 19, of which waited for: 8 -> 8; matrix products, arithmetic and copies ran while one was open for 1% -> 1% of each run, Pallas kernels for 43% -> 44%
where the time goes in v6:
time: 73.8 us; the launch traced here: 73.6 us
  Pallas kernels  37.5 us (51%)
  starting transfers between devices  20.4 us (28%)
  waiting for transfers between devices  13.9 us (19%)
  between operations  1.04 us (1%)
  other arithmetic  0.75 us (1%)
    ppermute x16, starting transfers between devices, send(): return lax.ppermute(x, 'engine', pairs)  14.9 us
    ppermute x16, waiting for transfers between devices, send(): return lax.ppermute(x, 'engine', pairs)  13.9 us
    pallas_call x3, Pallas kernels, place(): pl.pallas_call(functools.partial(place_body, engines, rows, group, kept,...  11.5 us
    pallas_call x1, Pallas kernels, body(): pl.pallas_call(functools.partial(lead_body, engines, rows), in_specs=[SM,...  6.82 us
    ppermute x3, starting transfers between devices, body(): lax.ppermute(blocks_out[d], 'chan', [(c, (c + d) % chans) for c in range(...  5.55 us
    pallas_call x1, Pallas kernels, body(): pl.pallas_call(functools.partial(pack_body, engines, rows, sends), in_spe...  4.64 us
    pallas_call x1, Pallas kernels, body(): pl.pallas_call(functools.partial(project_body, engines, rows, slots_here,...  4.28 us
    pallas_call x1, Pallas kernels, body(): pl.pallas_call(functools.partial(modal_body, engines, rows), in_specs=[SM...  4.26 us
  transfers between devices with their start and end apart: 19, of which 8 were waited for; matrix products, arithmetic and copies ran while one was open for 1% of the time, Pallas kernels for 44%

profile of v6, /device:TPU:0, one launch (start us, length us, event | category | flops | bytes accessed | tf_op | source)
XLA Modules:
  0.0 73.6 jit_solution(16734855006838875262)
XLA Ops:
  0.6 0.0 copy-start.7
  0.6 0.0 copy-start.3
  0.7 0.0 copy-start.4
  0.7 0.0 copy-start.2
  0.7 0.0 copy-start
  0.7 2.0 %early.1 = (bf16[64,2048]{1,0:T(8,128)(2,1)S(1)}, bf16[64,2048]{1,0:T(8,128)(2,1)S(1)}) custom-call(s32[64]{0:T(128)} %source.5, bf16[127,16,2048]{2,1,0:T(8,128)(2,1)} %bitcast.3), custom_call_target="tpu_custom_call" | custom-call | tf_op jit(solution)/shard_map/early/pallas_call | solution.py:520
  2.7 2.5 %collective-permute-start.4 = (bf16[64,2048]{1,0:T(8,128)(2,1)S(1)}, bf16[64,2048]{1,0:T(8,128)(2,1)S(1)}, u32[]{:S(2)}, u32[]{:S(2)}) collective-permute-start(bf16[64,2048]{1,0:T(8,128)(2,1)S(1)} %get-tuple-element.51), channel_id=1, source_target_pairs={{0,12},{4,8},{8,4},{12,0},{1,13},{5,9},{9,5},{13,1},{2,14},{6,10},... | collective-permute-start | bytes 786440 | tf_op jit(solution)/shard_map/ppermute | solution.py:40
  5.2 0.6 collective-permute-start.3
  5.8 0.0 copy-done.7
  5.8 0.0 copy-done.3
  5.8 0.0 copy-done.4
  5.8 0.0 copy-done.2
  5.8 0.0 copy-done
  5.8 6.8 %lead.1 = (f32[5,16,2048]{2,1,0:T(8,128)S(1)}, bf16[40,2048]{1,0:T(8,128)(2,1)S(1)}, bf16[40,2048]{1,0:T(8,128)(2,1)S(1)}, bf16[40,2048]{1,0:T(8,128)(2,1)S(1)}) custom-call(s32[64]{0:T(128)S(1)} %copy-done.7, bf16[127,16,2048]{2,1,0:T(8,128)(2,1)} %bitcast.4, f32[16,16,2048]{2,1,0:T(8,128)S(1)} %copy-done, bf16[128,2048]{1,0:T(8,128)(2,1)S(1)} %copy-done.2, ...), custom_call_target="tpu_custom_call" | custom-call | tf_op jit(solution)/shard_map/lead/pallas_call | solution.py:546
  12.7 0.1 collective-permute-start
  12.8 1.7 %collective-permute-start.1 = (bf16[40,2048]{1,0:T(8,128)(2,1)S(1)}, bf16[40,2048]{1,0:T(8,128)(2,1)S(1)}, u32[]{:S(2)}, u32[]{:S(2)}) collective-permute-start(bf16[40,2048]{1,0:T(8,128)(2,1)S(1)} %get-tuple-element.48), channel_id=1, source_target_pairs={{0,8},{4,12},{8,0},{12,4},{1,9},{5,13},{9,1},{13,5},{2,10},{6,14},... | collective-permute-start | bytes 491528 | tf_op jit(solution)/shard_map/ppermute | solution.py:40
  14.5 0.1 collective-permute-start.2
  14.6 4.6 %pack.1 = (bf16[256,2048]{1,0:T(8,128)(2,1)S(1)}, bf16[96,2048]{1,0:T(8,128)(2,1)S(1)}, bf16[96,2048]{1,0:T(8,128)(2,1)S(1)}, bf16[88,2048]{1,0:T(8,128)(2,1)S(1...) custom-call(s32[64]{0:T(128)S(1)} %copy-done.7, ...), custom_call_target="tpu_custom_call" | custom-call | tf_op jit(solution)/shard_map/pack/pallas_call | solution.py:568
  19.3 0.0 collective-permute-done.refs_0_
  19.3 2.7 %collective-permute-done.1.refs_1_ = bf16[40,2048]{1,0:T(8,128)(2,1)S(1)} collective-permute-done((bf16[40,2048]{1,0:T(8,128)(2,1)S(1)}, bf16[40,2048]{1,0:T(8,128)(2,1)S(1)}, u32[]{:S(2)}, u32[]{:S(2)}) %collective-permute-start.1) | collective-permute-done | bytes 163872 | tf_op jit(solution)/shard_map/ppermute | solution.py:40
  22.0 2.5 %collective-permute-done.2.refs_2_ = bf16[40,2048]{1,0:T(8,128)(2,1)S(1)} collective-permute-done((bf16[40,2048]{1,0:T(8,128)(2,1)S(1)}, bf16[40,2048]{1,0:T(8,128)(2,1)S(1)}, u32[]{:S(2)}, u32[]{:S(2)}) %collective-permute-start.2) | collective-permute-done | bytes 163872 | tf_op jit(solution)/shard_map/ppermute | solution.py:40
  24.5 0.0 collective-permute-done.4.refs_5_.refs_1_
  24.5 0.0 collective-permute-done.3.refs_4_.refs_0_
  24.5 0.0 copy-done.5
  24.5 1.3 %mix.1 = (bf16[64,2048]{1,0:T(8,128)(2,1)S(1)}, bf16[5,16,2048]{2,1,0:T(8,128)(2,1)S(1)}) custom-call(s32[12]{0:T(128)S(1)} %get-tuple-element.44.slots, s32[4]{0:T(128)S(1)} %get-tuple-element.45.found, f32[5,16,2048]{2,1,0:T(8,128)S(1)} %get-tuple-element.46.parts_in, bf16[2,3,16,2048]{3,2,1,0:T(8,128)(2,1)S(1)} %copy-done.5, ...), custom_call_target="tpu_custom_call" | custom-call | tf_op jit(solution)/shard_map/mix/pallas_call | solution.py:590
  25.8 0.2 collective-permute-start.8
  26.0 0.4 collective-permute-start.5
  26.4 2.5 %collective-permute-start.6 = (bf16[64,2048]{1,0:T(8,128)(2,1)S(1)}, bf16[64,2048]{1,0:T(8,128)(2,1)S(1)}, u32[]{:S(2)}, u32[]{:S(2)}) collective-permute-start(bf16[64,2048]{1,0:T(8,128)(2,1)S(1)} %get-tuple-element.53.refs_0_), channel_id=1, source_target_pairs={{0,8},{4,12},{8,0},{12,4},{1,9},{5,13},{9,1},{13,5},{2,10},{6,14},... | collective-permute-start | bytes 786440 | tf_op jit(solution)/shard_map/ppermute | solution.py:40
  28.9 0.1 collective-permute-done.5.refs_1_
  28.9 2.5 %collective-permute-start.12 = (bf16[96,2048]{1,0:T(8,128)(2,1)S(1)}, bf16[96,2048]{1,0:T(8,128)(2,1)S(1)}, u32[]{:S(2)}, u32[]{:S(2)}) collective-permute-start(bf16[96,2048]{1,0:T(8,128)(2,1)S(1)} %get-tuple-element.66), channel_id=1, source_target_pairs={{0,8},{4,12},{8,0},{12,4},{1,9},{5,13},{9,1},{13,5},{2,10},{6,14},... | collective-permute-start | bytes 1179656 | tf_op jit(solution)/shard_map/ppermute | solution.py:40
  31.4 0.0 collective-permute-start.13
  31.4 4.6 %collective-permute-done.6.refs_2_ = bf16[64,2048]{1,0:T(8,128)(2,1)S(1)} collective-permute-done((bf16[64,2048]{1,0:T(8,128)(2,1)S(1)}, bf16[64,2048]{1,0:T(8,128)(2,1)S(1)}, u32[]{:S(2)}, u32[]{:S(2)}) %collective-permute-start.6) | collective-permute-done | bytes 262176 | tf_op jit(solution)/shard_map/ppermute | solution.py:40
  35.9 0.0 collective-permute-start.7
  36.0 0.0 collective-permute-done.8.near
  36.0 3.8 %place.3.refs_6_.refs_2_ = bf16[127,16,2048]{2,1,0:T(8,128)(2,1)} custom-call(bf16[256,352]{1,0:T(8,128)(2,1)S(1)} %get-tuple-element.50.refs_3_.spread, bf16[5,16,2048]{2,1,0:T(8,128)(2,1)S(1)} %get-tuple-element.57.gates.refs_2_, bf16[127,16,2048]{2,1,0:T(8,128)(2,1)} %bitcast.6, bf16[256,2048]{1,0:T(8,128)(2,1)S(1)} %collective-permute-done.8.near, ...), custom_call_target="tpu_custom_call" | custom-call | flops 1 | bytes 1 | tf_op jit(solution)/shard_map/place/pallas_call | solution.py:612
  39.7 0.0 collective-permute-done.7.refs_3_
  39.8 0.0 copy-done.1
  39.8 4.3 %project.1 = (bf16[32,1024]{1,0:T(8,128)(2,1)S(1)}, bf16[32,1024]{1,0:T(8,128)(2,1)S(1)}, bf16[32,1024]{1,0:T(8,128)(2,1)S(1)}, bf16[32,1024]{1,0:T(8,128)(2,1)S(1)}) custom-call(bf16[64,2048]{1,0:T(8,128)(2,1)S(1)} %get-tuple-element.53.refs_0_, bf16[64,2048]{1,0:T(8,128)(2,1)S(1)} %collective-permute-done.5.refs_1_, ...), custom_call_target="tpu_custom_call" | custom-call | tf_op jit(solution)/shard_map/project/pallas_call | solution.py:628
  44.0 0.0 copy-start.8
  44.1 0.0 copy-start.9
  44.1 0.6 collective-permute-start.9
  44.6 2.1 %collective-permute-start.10 = (bf16[32,1024]{1,0:T(8,128)(2,1)S(1)}, bf16[32,1024]{1,0:T(8,128)(2,1)S(1)}, u32[]{:S(2)}, u32[]{:S(2)}) collective-permute-start(bf16[32,1024]{1,0:T(8,128)(2,1)S(1)} %get-tuple-element.62), channel_id=1, source_target_pairs={{0,8},{4,12},{8,0},{12,4},{1,9},{5,13},{9,1},{13,5},{2,10},{6,14},... | collective-permute-start | bytes 196616 | tf_op jit(solution)/shard_map/ppermute | solution.py:40
  46.7 0.0 collective-permute-start.11
  46.7 4.3 %modal.1 = f32[16,16,2048]{2,1,0:T(8,128)} custom-call(s32[64]{0:T(128)S(1)} %copy-done.7, s32[12]{0:T(128)S(1)} %get-tuple-element.44.slots, s32[4]{0:T(128)S(1)} %get-tuple-element.45.found, f32[16,16,2048]{2,1,0:T(8,128)S(1)} %copy-done, bf16[5,16,2048]{2,1,0:T(8,128)(2,1)S(1)} %get-tuple-element.57.gates.refs_2_, f32[16,2048]{1,0:T(8,128)S(1)} %copy-done.3, ...), custom_call_target="tpu_custom_call" | custom-call | flops 1 | bytes 1 | tf_op jit(solution)/shard_map/modal/pallas_call | solution.py:649
  51.0 0.0 collective-permute-done.12.refs_4_.refs_0_
  51.0 1.4 %collective-permute-done.13.refs_5_.refs_1_ = bf16[96,2048]{1,0:T(8,128)(2,1)S(1)} collective-permute-done((bf16[96,2048]{1,0:T(8,128)(2,1)S(1)}, bf16[96,2048]{1,0:T(8,128)(2,1)S(1)}, u32[]{:S(2)}, u32[]{:S(2)}) %collective-permute-start.13) | collective-permute-done | bytes 393248 | tf_op jit(solution)/shard_map/ppermute | solution.py:40
  52.4 0.8 %collective-permute-start.17 = (bf16[88,2048]{1,0:T(8,128)(2,1)S(1)}, bf16[88,2048]{1,0:T(8,128)(2,1)S(1)}, u32[]{:S(2)}, u32[]{:S(2)}) collective-permute-start(bf16[88,2048]{1,0:T(8,128)(2,1)S(1)} %get-tuple-element.74), channel_id=1, source_target_pairs={{0,8},{4,12},{8,0},{12,4},{1,9},{5,13},{9,1},{13,5},{2,10},{6,14},... | collective-permute-start | bytes 1081352 | tf_op jit(solution)/shard_map/ppermute | solution.py:40
  53.2 0.0 collective-permute-done.9.refs_1_
  53.2 1.0 %collective-permute-done.10.refs_2_ = bf16[32,1024]{1,0:T(8,128)(2,1)S(1)} collective-permute-done((bf16[32,1024]{1,0:T(8,128)(2,1)S(1)}, bf16[32,1024]{1,0:T(8,128)(2,1)S(1)}, u32[]{:S(2)}, u32[]{:S(2)}) %collective-permute-start.10) | collective-permute-done | bytes 65568 | tf_op jit(solution)/shard_map/ppermute | solution.py:40
  54.2 0.4 collective-permute-done.11.refs_3_
  54.6 0.7 sort.1
  55.3 1.6 %collective-permute-start.14 = (bf16[32,1024]{1,0:T(8,128)(2,1)S(1)}, bf16[32,1024]{1,0:T(8,128)(2,1)S(1)}, u32[]{:S(2)}, u32[]{:S(2)}) collective-permute-start(bf16[32,1024]{1,0:T(8,128)(2,1)S(1)} %get-tuple-element.71), channel_id=1, source_target_pairs={{0,1},{1,2},{2,3},{3,0},{4,5},{5,6},{6,7},{7,4},{8,9},{9,10},{10,1... | collective-permute-start | bytes 196616 | tf_op jit(solution)/shard_map/ppermute | solution.py:679
  56.9 2.6 %collective-permute-start.15 = (bf16[32,1024]{1,0:T(8,128)(2,1)S(1)}, bf16[32,1024]{1,0:T(8,128)(2,1)S(1)}, u32[]{:S(2)}, u32[]{:S(2)}) collective-permute-start(bf16[32,1024]{1,0:T(8,128)(2,1)S(1)} %get-tuple-element.72), channel_id=1, source_target_pairs={{0,2},{1,3},{2,0},{3,1},{4,6},{5,7},{6,4},{7,5},{8,10},{9,11},{10,... | collective-permute-start | bytes 196616 | tf_op jit(solution)/shard_map/ppermute | solution.py:679
  59.5 1.3 %collective-permute-start.16 = (bf16[32,1024]{1,0:T(8,128)(2,1)S(1)}, bf16[32,1024]{1,0:T(8,128)(2,1)S(1)}, u32[]{:S(2)}, u32[]{:S(2)}) collective-permute-start(bf16[32,1024]{1,0:T(8,128)(2,1)S(1)} %get-tuple-element.73), channel_id=1, source_target_pairs={{0,3},{1,0},{2,1},{3,2},{4,7},{5,4},{6,5},{7,6},{8,11},{9,8},{10,9... | collective-permute-start | bytes 196616 | tf_op jit(solution)/shard_map/ppermute | solution.py:679
  60.8 0.9 %collective-permute-start.18 = (bf16[88,2048]{1,0:T(8,128)(2,1)S(1)}, bf16[88,2048]{1,0:T(8,128)(2,1)S(1)}, u32[]{:S(2)}, u32[]{:S(2)}) collective-permute-start(bf16[88,2048]{1,0:T(8,128)(2,1)S(1)} %get-tuple-element.77), channel_id=1, source_target_pairs={{0,12},{4,8},{8,4},{12,0},{1,13},{5,9},{9,5},{13,1},{2,14},{6,10},... | collective-permute-start | bytes 1081352 | tf_op jit(solution)/shard_map/ppermute | solution.py:40
  61.7 4.3 %place.5._ = bf16[127,16,2048]{2,1,0:T(8,128)(2,1)} custom-call(bf16[256,352]{1,0:T(8,128)(2,1)S(1)} %get-tuple-element.50.refs_3_.spread, bf16[5,16,2048]{2,1,0:T(8,128)(2,1)S(1)} %get-tuple-element.57.gates.refs_2_, bf16[127,16,2048]{2,1,0:T(8,128)(2,1)} %bitcast.7, ...), custom_call_target="tpu_custom_call", output_to_operand_aliasing={{}: (6, {})} | custom-call | flops 1 | bytes 1 | tf_op jit(solution)/shard_map/place/pallas_call | solution.py:612
  66.0 0.0 collective-permute-done.14
  66.0 0.0 collective-permute-done.15
  66.0 0.0 collective-permute-done.16
  66.1 0.0 collective-permute-done.17.refs_0_
  66.1 3.4 %place.4.base = bf16[3,16,16,2048]{3,2,1,0:T(8,128)(2,1)S(1)} custom-call(bf16[256,352]{1,0:T(8,128)(2,1)S(1)} %get-tuple-element.50.refs_3_.spread, bf16[5,16,2048]{2,1,0:T(8,128)(2,1)S(1)} %get-tuple-element.57.gates.refs_2_, bf16[127,16,2048]{2,1,0:T(8,128)(2,1)} %bitcast.8, bf16[256,2048]{1,0:T(8,128)(2,1)S(1)} %collective-permute-done.8.near, ...), custom_call_target="tpu_custom_call" | custom-call | flops 1 | bytes 1 | tf_op jit(solution)/shard_map/place/pallas_call | solution.py:612
  69.5 0.7 multiply_convert_fusion
  70.2 1.2 %collective-permute-done.18.msg = bf16[88,2048]{1,0:T(8,128)(2,1)S(1)} collective-permute-done((bf16[88,2048]{1,0:T(8,128)(2,1)S(1)}, bf16[88,2048]{1,0:T(8,128)(2,1)S(1)}, u32[]{:S(2)}, u32[]{:S(2)}) %collective-permute-start.18) | collective-permute-done | bytes 360480 | tf_op jit(solution)/shard_map/ppermute | solution.py:40
  71.4 2.1 %last.1 = bf16[127,16,2048]{2,1,0:T(8,128)(2,1)} custom-call(bf16[256,352]{1,0:T(8,128)(2,1)S(1)} %get-tuple-element.50.refs_3_.spread, bf16[3,16,16,2048]{3,2,1,0:T(8,128)(2,1)S(1)} %place.4.base, bf16[88,2048]{1,0:T(8,128)(2,1)S(1)} %collective-permute-done.18.msg, bf16[127,16,2048]{2,1,0:T(8,128)(2,1)} %place.5._), custom_call_target="tpu_custom_call", output_to_operand_aliasing={{}: (3, {})} | custom-call | flops 1 | bytes 1 | tf_op jit(solution)/shard_map/last/pallas_call | solution.py:688
  (8 shorter events, 0.1 us)
Async XLA Ops:
  0.6 5.2 %copy-start.7 = (s32[64]{0:T(128)S(1)}, s32[64]{0:T(128)}, u32[]{:S(2)}) copy-start(s32[64]{0:T(128)} %source.5) | copy-start | bytes 772
  0.6 5.2 %copy-start.3 = (f32[16,2048]{1,0:T(8,128)S(1)}, f32[16,2048]{1,0:T(8,128)}, u32[]{:S(2)}) copy-start(f32[16,2048]{1,0:T(8,128)} %decay.5) | copy-start | bytes 393220
  0.7 5.2 %copy-start.4 = (f32[16,2048]{1,0:T(8,128)S(1)}, f32[16,2048]{1,0:T(8,128)}, u32[]{:S(2)}) copy-start(f32[16,2048]{1,0:T(8,128)} %resid.3) | copy-start | bytes 393220
  0.7 5.2 %copy-start.2 = (bf16[128,2048]{1,0:T(8,128)(2,1)S(1)}, bf16[128,2048]{1,0:T(8,128)(2,1)}, u32[]{:S(2)}) copy-start(bf16[128,2048]{1,0:T(8,128)(2,1)} %filt.3) | copy-start | bytes 1572868
  0.7 5.2 %copy-start = (f32[16,16,2048]{2,1,0:T(8,128)S(1)}, f32[16,16,2048]{2,1,0:T(8,128)}, u32[]{:S(2)}) copy-start(f32[16,16,2048]{2,1,0:T(8,128)} %states.3) | copy-start | bytes 6291460
  2.7 21.8 %collective-permute-start.4 = (bf16[64,2048]{1,0:T(8,128)(2,1)S(1)}, bf16[64,2048]{1,0:T(8,128)(2,1)S(1)}, u32[]{:S(2)}, u32[]{:S(2)}) collective-permute-start(bf16[64,2048]{1,0:T(8,128)(2,1)S(1)} %get-tuple-element.51), channel_id=1, source_target_pairs={{0,12},{4,8},{8,4},{12,0},{1,13},{5,9},{9,5},{13,1},{2,14},{6,10},... | collective-permute-start | bytes 786440 | tf_op jit(solution)/shard_map/ppermute | solution.py:40
  5.2 19.3 %collective-permute-start.3 = (bf16[64,2048]{1,0:T(8,128)(2,1)S(1)}, bf16[64,2048]{1,0:T(8,128)(2,1)S(1)}, u32[]{:S(2)}, u32[]{:S(2)}) collective-permute-start(bf16[64,2048]{1,0:T(8,128)(2,1)S(1)} %get-tuple-element.41._), channel_id=1, source_target_pairs={{0,8},{4,12},{8,0},{12,4},{1,9},{5,13},{9,1},{13,5},{2,10},{6,14},... | collective-permute-start | bytes 786440 | tf_op jit(solution)/shard_map/ppermute | solution.py:40
  12.7 6.6 %collective-permute-start = (bf16[40,2048]{1,0:T(8,128)(2,1)S(1)}, bf16[40,2048]{1,0:T(8,128)(2,1)S(1)}, u32[]{:S(2)}, u32[]{:S(2)}) collective-permute-start(bf16[40,2048]{1,0:T(8,128)(2,1)S(1)} %get-tuple-element.47), channel_id=1, source_target_pairs={{0,4},{4,0},{8,12},{12,8},{1,5},{5,1},{9,13},{13,9},{2,6},{6,2},{1... | collective-permute-start | bytes 491528 | tf_op jit(solution)/shard_map/ppermute | solution.py:40
  12.8 9.2 %collective-permute-start.1 = (bf16[40,2048]{1,0:T(8,128)(2,1)S(1)}, bf16[40,2048]{1,0:T(8,128)(2,1)S(1)}, u32[]{:S(2)}, u32[]{:S(2)}) collective-permute-start(bf16[40,2048]{1,0:T(8,128)(2,1)S(1)} %get-tuple-element.48), channel_id=1, source_target_pairs={{0,8},{4,12},{8,0},{12,4},{1,9},{5,13},{9,1},{13,5},{2,10},{6,14},... | collective-permute-start | bytes 491528 | tf_op jit(solution)/shard_map/ppermute | solution.py:40
  14.5 10.0 %collective-permute-start.2 = (bf16[40,2048]{1,0:T(8,128)(2,1)S(1)}, bf16[40,2048]{1,0:T(8,128)(2,1)S(1)}, u32[]{:S(2)}, u32[]{:S(2)}) collective-permute-start(bf16[40,2048]{1,0:T(8,128)(2,1)S(1)} %get-tuple-element.49), channel_id=1, source_target_pairs={{0,12},{4,8},{8,4},{12,0},{1,13},{5,9},{9,5},{13,1},{2,14},{6,10},... | collective-permute-start | bytes 491528 | tf_op jit(solution)/shard_map/ppermute | solution.py:40
  14.6 9.9 %copy-start.5 = (bf16[2,3,16,2048]{3,2,1,0:T(8,128)(2,1)S(1)}, bf16[2,3,16,2048]{3,2,1,0:T(8,128)(2,1)}, u32[]{:S(2)}) copy-start(bf16[2,3,16,2048]{3,2,1,0:T(8,128)(2,1)} %mr.1) | copy-start | bytes 1179652
  14.6 9.9 %copy-start.6 = (bf16[2,3,16,2048]{3,2,1,0:T(8,128)(2,1)S(1)}, bf16[2,3,16,2048]{3,2,1,0:T(8,128)(2,1)}, u32[]{:S(2)}) copy-start(bf16[2,3,16,2048]{3,2,1,0:T(8,128)(2,1)} %li.1) | copy-start | bytes 1179652
  25.8 10.1 %collective-permute-start.8 = (bf16[256,2048]{1,0:T(8,128)(2,1)S(1)}, bf16[256,2048]{1,0:T(8,128)(2,1)S(1)}, u32[]{:S(2)}, u32[]{:S(2)}) collective-permute-start(bf16[256,2048]{1,0:T(8,128)(2,1)S(1)} %get-tuple-element.58), channel_id=1, source_target_pairs={{0,4},{4,0},{8,12},{12,8},{1,5},{5,1},{9,13},{13,9},{2,6},{6,2},{1... | collective-permute-start | bytes 3145736 | tf_op jit(solution)/shard_map/ppermute | solution.py:40
  26.0 2.9 %collective-permute-start.5 = (bf16[64,2048]{1,0:T(8,128)(2,1)S(1)}, bf16[64,2048]{1,0:T(8,128)(2,1)S(1)}, u32[]{:S(2)}, u32[]{:S(2)}) collective-permute-start(bf16[64,2048]{1,0:T(8,128)(2,1)S(1)} %get-tuple-element.53.refs_0_), channel_id=1, source_target_pairs={{0,4},{4,0},{8,12},{12,8},{1,5},{5,1},{9,13},{13,9},{2,6},{6,2},{1... | collective-permute-start | bytes 786440 | tf_op jit(solution)/shard_map/ppermute | solution.py:40
  26.4 9.5 %collective-permute-start.6 = (bf16[64,2048]{1,0:T(8,128)(2,1)S(1)}, bf16[64,2048]{1,0:T(8,128)(2,1)S(1)}, u32[]{:S(2)}, u32[]{:S(2)}) collective-permute-start(bf16[64,2048]{1,0:T(8,128)(2,1)S(1)} %get-tuple-element.53.refs_0_), channel_id=1, source_target_pairs={{0,8},{4,12},{8,0},{12,4},{1,9},{5,13},{9,1},{13,5},{2,10},{6,14},... | collective-permute-start | bytes 786440 | tf_op jit(solution)/shard_map/ppermute | solution.py:40
  28.9 22.1 %collective-permute-start.12 = (bf16[96,2048]{1,0:T(8,128)(2,1)S(1)}, bf16[96,2048]{1,0:T(8,128)(2,1)S(1)}, u32[]{:S(2)}, u32[]{:S(2)}) collective-permute-start(bf16[96,2048]{1,0:T(8,128)(2,1)S(1)} %get-tuple-element.66), channel_id=1, source_target_pairs={{0,8},{4,12},{8,0},{12,4},{1,9},{5,13},{9,1},{13,5},{2,10},{6,14},... | collective-permute-start | bytes 1179656 | tf_op jit(solution)/shard_map/ppermute | solution.py:40
  31.4 21.0 %collective-permute-start.13 = (bf16[96,2048]{1,0:T(8,128)(2,1)S(1)}, bf16[96,2048]{1,0:T(8,128)(2,1)S(1)}, u32[]{:S(2)}, u32[]{:S(2)}) collective-permute-start(bf16[96,2048]{1,0:T(8,128)(2,1)S(1)} %get-tuple-element.67), channel_id=1, source_target_pairs={{0,12},{4,8},{8,4},{12,0},{1,13},{5,9},{9,5},{13,1},{2,14},{6,10},... | collective-permute-start | bytes 1179656 | tf_op jit(solution)/shard_map/ppermute | solution.py:40
  35.9 3.8 %collective-permute-start.7 = (bf16[64,2048]{1,0:T(8,128)(2,1)S(1)}, bf16[64,2048]{1,0:T(8,128)(2,1)S(1)}, u32[]{:S(2)}, u32[]{:S(2)}) collective-permute-start(bf16[64,2048]{1,0:T(8,128)(2,1)S(1)} %collective-permute-done.6.refs_2_), channel_id=1, source_target_pairs={{0,4},{4,0},{8,12},{12,8},{1,5},{5,1},{9,13},{13,9},{2,6},{6,2},{1... | collective-permute-start | bytes 786440 | tf_op jit(solution)/shard_map/ppermute | solution.py:40
  36.0 3.8 %copy-start.1 = (bf16[2,2048,512]{2,1,0:T(8,128)(2,1)S(1)}, bf16[2,2048,512]{2,1,0:T(8,128)(2,1)}, u32[]{:S(2)}) copy-start(bf16[2,2048,512]{2,1,0:T(8,128)(2,1)} %refs_4_.1) | copy-start | bytes 12582916
  44.0 10.5 %copy-start.8 = (s32[8]{0:T(128)S(1)}, s32[8]{0:T(128)}, u32[]{:S(2)}) copy-start(s32[8]{0:T(128)} %slot_of.1) | copy-start | bytes 100
  44.1 16.8 %copy-start.9 = (s32[16]{0:T(128)S(1)}, s32[16]{0:T(128)}, u32[]{:S(2)}) copy-start(s32[16]{0:T(128)} %param.17) | copy-start | bytes 196
  44.1 9.1 %collective-permute-start.9 = (bf16[32,1024]{1,0:T(8,128)(2,1)S(1)}, bf16[32,1024]{1,0:T(8,128)(2,1)S(1)}, u32[]{:S(2)}, u32[]{:S(2)}) collective-permute-start(bf16[32,1024]{1,0:T(8,128)(2,1)S(1)} %get-tuple-element.60), channel_id=1, source_target_pairs={{0,4},{4,0},{8,12},{12,8},{1,5},{5,1},{9,13},{13,9},{2,6},{6,2},{1... | collective-permute-start | bytes 196616 | tf_op jit(solution)/shard_map/ppermute | solution.py:40
  44.6 9.6 %collective-permute-start.10 = (bf16[32,1024]{1,0:T(8,128)(2,1)S(1)}, bf16[32,1024]{1,0:T(8,128)(2,1)S(1)}, u32[]{:S(2)}, u32[]{:S(2)}) collective-permute-start(bf16[32,1024]{1,0:T(8,128)(2,1)S(1)} %get-tuple-element.62), channel_id=1, source_target_pairs={{0,8},{4,12},{8,0},{12,4},{1,9},{5,13},{9,1},{13,5},{2,10},{6,14},... | collective-permute-start | bytes 196616 | tf_op jit(solution)/shard_map/ppermute | solution.py:40
  46.7 7.9 %collective-permute-start.11 = (bf16[32,1024]{1,0:T(8,128)(2,1)S(1)}, bf16[32,1024]{1,0:T(8,128)(2,1)S(1)}, u32[]{:S(2)}, u32[]{:S(2)}) collective-permute-start(bf16[32,1024]{1,0:T(8,128)(2,1)S(1)} %get-tuple-element.63), channel_id=1, source_target_pairs={{0,12},{4,8},{8,4},{12,0},{1,13},{5,9},{9,5},{13,1},{2,14},{6,10},... | collective-permute-start | bytes 196616 | tf_op jit(solution)/shard_map/ppermute | solution.py:40
  52.4 13.7 %collective-permute-start.17 = (bf16[88,2048]{1,0:T(8,128)(2,1)S(1)}, bf16[88,2048]{1,0:T(8,128)(2,1)S(1)}, u32[]{:S(2)}, u32[]{:S(2)}) collective-permute-start(bf16[88,2048]{1,0:T(8,128)(2,1)S(1)} %get-tuple-element.74), channel_id=1, source_target_pairs={{0,8},{4,12},{8,0},{12,4},{1,9},{5,13},{9,1},{13,5},{2,10},{6,14},... | collective-permute-start | bytes 1081352 | tf_op jit(solution)/shard_map/ppermute | solution.py:40
  55.3 10.8 %collective-permute-start.14 = (bf16[32,1024]{1,0:T(8,128)(2,1)S(1)}, bf16[32,1024]{1,0:T(8,128)(2,1)S(1)}, u32[]{:S(2)}, u32[]{:S(2)}) collective-permute-start(bf16[32,1024]{1,0:T(8,128)(2,1)S(1)} %get-tuple-element.71), channel_id=1, source_target_pairs={{0,1},{1,2},{2,3},{3,0},{4,5},{5,6},{6,7},{7,4},{8,9},{9,10},{10,1... | collective-permute-start | bytes 196616 | tf_op jit(solution)/shard_map/ppermute | solution.py:679
  56.9 9.2 %collective-permute-start.15 = (bf16[32,1024]{1,0:T(8,128)(2,1)S(1)}, bf16[32,1024]{1,0:T(8,128)(2,1)S(1)}, u32[]{:S(2)}, u32[]{:S(2)}) collective-permute-start(bf16[32,1024]{1,0:T(8,128)(2,1)S(1)} %get-tuple-element.72), channel_id=1, source_target_pairs={{0,2},{1,3},{2,0},{3,1},{4,6},{5,7},{6,4},{7,5},{8,10},{9,11},{10,... | collective-permute-start | bytes 196616 | tf_op jit(solution)/shard_map/ppermute | solution.py:679
  59.5 6.6 %collective-permute-start.16 = (bf16[32,1024]{1,0:T(8,128)(2,1)S(1)}, bf16[32,1024]{1,0:T(8,128)(2,1)S(1)}, u32[]{:S(2)}, u32[]{:S(2)}) collective-permute-start(bf16[32,1024]{1,0:T(8,128)(2,1)S(1)} %get-tuple-element.73), channel_id=1, source_target_pairs={{0,3},{1,0},{2,1},{3,2},{4,7},{5,4},{6,5},{7,6},{8,11},{9,8},{10,9... | collective-permute-start | bytes 196616 | tf_op jit(solution)/shard_map/ppermute | solution.py:679
  60.8 10.6 %collective-permute-start.18 = (bf16[88,2048]{1,0:T(8,128)(2,1)S(1)}, bf16[88,2048]{1,0:T(8,128)(2,1)S(1)}, u32[]{:S(2)}, u32[]{:S(2)}) collective-permute-start(bf16[88,2048]{1,0:T(8,128)(2,1)S(1)} %get-tuple-element.77), channel_id=1, source_target_pairs={{0,12},{4,8},{8,4},{12,0},{1,13},{5,9},{9,5},{13,1},{2,14},{6,10},... | collective-permute-start | bytes 1081352 | tf_op jit(solution)/shard_map/ppermute | solution.py:40
